TPU v7x, 128 devices: a whole 4x4x4 slice. The times are simulated.
128 devices in a mesh: shard: 64 (over z, x, y), rep: 2 (over core).
Axes of the slice: x: 4, y: 4, z: 4, core: 2. Of those that a mesh axis runs over, the one named last changes fastest.
Arguments:
- touched_ids: int32 [16384, 32], P(('shard', 'rep')), may hold values from 0 to 131071, as said below
- bag_lengths: int32 [16384, 4], P(('shard', 'rep')), may hold values from 1 to 24, 32 in all within a row
- train_map: int32 [131072], replicated, may hold values from 0 to 131071, as said below
- serve_map: int32 [131072], P('shard'), may hold values from 0 to 131071, as said below
- slot_grads: bfloat16 [16384, 32, 128], P(('shard', 'rep')), may hold values from -6 to 6
- table: float32 [131072, 128], P('shard'), may hold values from -6 to 6
- moment: float32 [131072, 128], P('shard'), may hold values from -4 to 4
- row_var: float32 [131072], P('shard'), may hold values from 0.01 to 1
- serving_old: bfloat16 [131072, 128], P('shard'), may hold values from -6 to 6
- w_first: bfloat16 [512, 1024], replicated, may hold values from -0.25 to 0.25
- w_second: bfloat16 [1024, 1024], replicated, may hold values from -0.1875 to 0.1875
- w_score: bfloat16 [1024], replicated, may hold values from -0.1875 to 0.1875
Outputs:
- new_table: float32 [131072, 128], P('shard')
- new_moment: float32 [131072, 128], P('shard')
- new_var: float32 [131072], P('shard')
- serving_table: bfloat16 [131072, 128], P('shard')
- scores: float32 [16384], P(('shard', 'rep'))
Inputs may be any that keep to these rules, and one draw needn't show every extreme that they name: `touched_ids`: of the 4096 ids of one device's samples at most 256 have their training position in one owner's range of 2048 positions; 4 owners receive exactly 256 from every device. `train_map`: A permutation of the row ids; the owner of a row is its position // 2048. `serve_map`: A permutation; the row at training position j * 2048 + s has its serving position in the range of serving owner s % 64.
All inputs are finite; a program needn't handle non-finite values.
Results may differ from a plain program's by a relative error of at most 0.008.
Values may be sent and summed in bfloat16 or wider, within the bound.
No kernel may reach another device: no remote copies, remote signals or barrier semaphores. Data moves between devices by JAX's collectives and lax.ppermute only.
A program may use at most 256 MiB of HBM per device.

v0:
```python
import jax
import jax.numpy as jnp
from jax import lax
from jax.sharding import PartitionSpec as P

beta_one = 0.9
beta_two = 0.999
learn_rate = 0.1
epsilon = 1e-06


def from_everyone(value, axis):
    size = lax.axis_size(axis)
    return lax.all_to_all(
        jnp.broadcast_to(value[None], (size, *value.shape)), axis, 0, 0, tiled=True
    )


def over_copies(value, axis):
    return from_everyone(value, axis).sum(axis=0)


def in_one(arrays, axis):
    line, at, gathered = (jnp.concatenate([a.reshape(-1) for a in arrays]), 0, [])
    total = over_copies(line, axis)
    for a in arrays:
        gathered.append(total[at : at + a.size].reshape(a.shape))
        at += a.size
    return tuple(gathered)


def rank_in_owner(owner_of, owners):
    count = owner_of.shape[0]
    block = 512
    hot = (owner_of[:, None] == jnp.arange(owners, dtype=jnp.int32)[None, :]).astype(jnp.bfloat16)
    hot_blocks = hot.reshape(count // block, block, owners)
    lower = (jnp.arange(block)[:, None] >= jnp.arange(block)[None, :]).astype(jnp.bfloat16)
    within = jnp.einsum("ij,njo->nio", lower, hot_blocks, preferred_element_type=jnp.float32)
    totals = within[:, -1, :]
    offsets = jnp.cumsum(totals, axis=0) - totals
    counts = (within + offsets[:, None, :]).reshape(count, owners)
    return (jnp.sum(counts * hot.astype(jnp.float32), axis=1) - 1.0).astype(jnp.int32)


def accumulate(grads, row_ids, tab_rows):
    count = row_ids.shape[0]
    block = 2048
    id_blocks = row_ids.reshape(count // block, block)
    grad_blocks = grads.reshape(count // block, block, grads.shape[1])
    spots = jnp.arange(tab_rows, dtype=jnp.int32)

    def add_block(carry, pieces):
        total, touch = carry
        ids, grad_piece = pieces
        hit = (ids[:, None] == spots[None, :]).astype(jnp.bfloat16)
        total = total + lax.dot_general(
            hit, grad_piece, (((0,), (0,)), ((), ())), preferred_element_type=jnp.float32
        )
        touch = touch + jnp.sum(hit.astype(jnp.float32), axis=0)
        return ((total, touch), None)

    start = (
        jnp.zeros((tab_rows, grads.shape[1]), jnp.float32),
        jnp.zeros((tab_rows,), jnp.float32),
    )
    (grad_sum, touches), _ = lax.scan(add_block, start, (id_blocks, grad_blocks))
    return (grad_sum, touches)


def place_rows(serving_old, slot_index, rows_in):
    tab_rows, row_width = serving_old.shape
    block = 512
    old_blocks = serving_old.reshape(tab_rows // block, block, row_width)
    firsts = jnp.arange(tab_rows // block, dtype=jnp.int32) * block

    def place_block(pieces):
        old_piece, first = pieces
        wanted = first + jnp.arange(block, dtype=jnp.int32)
        hit = (wanted[:, None] == slot_index[None, :]).astype(jnp.bfloat16)
        fresh = jnp.dot(hit, rows_in, preferred_element_type=jnp.float32)
        found = jnp.sum(hit.astype(jnp.float32), axis=1) > 0.5
        return jnp.where(found[:, None], fresh.astype(jnp.bfloat16), old_piece)

    return lax.map(place_block, (old_blocks, firsts)).reshape(tab_rows, row_width)


def per_device(
    touched_ids,
    bag_lengths,
    train_map,
    serve_map,
    slot_grads,
    table,
    moment,
    row_var,
    serving_old,
    w_first,
    w_second,
    w_score,
):
    owners = lax.axis_size("shard")
    tab_rows, row_width = table.shape
    samples, bag_size = touched_ids.shape
    fields = bag_lengths.shape[1]
    slot_count = samples * bag_size
    capacity = 4 * slot_count // owners
    position = train_map[touched_ids.reshape(slot_count)]
    owner_of = position // tab_rows
    local_row = position % tab_rows
    slot_rank = rank_in_owner(owner_of, owners)
    ends = jnp.cumsum(bag_lengths, axis=1)
    slot_field = jnp.sum(
        (jnp.arange(bag_size, dtype=jnp.int32)[None, None, :] >= ends[:, :, None]).astype(
            jnp.int32
        ),
        axis=1,
    ).reshape(slot_count)
    source = jnp.arange(slot_count, dtype=jnp.int32)
    owner_hot = (owner_of[:, None] == jnp.arange(owners, dtype=jnp.int32)[None, :]).astype(
        jnp.bfloat16
    )
    rank_hot = (slot_rank[:, None] == jnp.arange(capacity, dtype=jnp.int32)[None, :]).astype(
        jnp.bfloat16
    )
    columns = jnp.concatenate(
        [
            rank_hot * (source // 64).astype(jnp.bfloat16)[:, None],
            rank_hot * (source % 64).astype(jnp.bfloat16)[:, None],
            rank_hot,
            rank_hot * slot_field.astype(jnp.bfloat16)[:, None],
        ],
        axis=1,
    )
    layout = lax.dot_general(
        owner_hot, columns, (((0,), (0,)), ((), ())), preferred_element_type=jnp.float32
    ).reshape(owners, 4, capacity)
    bucket_source = (layout[:, 0, :] * 64.0 + layout[:, 1, :]).astype(jnp.int32)
    filled = layout[:, 2, :] > 0.5
    bucket_field = layout[:, 3, :].astype(jnp.int32)
    flat_grads = slot_grads.reshape(slot_count, row_width)
    send_grads = jnp.where(
        filled[:, :, None], flat_grads[bucket_source], jnp.zeros((), jnp.bfloat16)
    )
    send_rows = jnp.where(filled, local_row[bucket_source], -1)
    recv_grads, recv_rows = (
        lax.all_to_all(send_grads, "shard", split_axis=0, concat_axis=0, tiled=True),
        lax.all_to_all(send_rows, "shard", split_axis=0, concat_axis=0, tiled=True),
    )
    grad_sum, touches = accumulate(
        recv_grads.reshape(-1, row_width), recv_rows.reshape(-1), tab_rows
    )
    grad_sum, touches = in_one((grad_sum, touches), "rep")
    touched = touches > 0.0
    new_moment = jnp.where(
        touched[:, None], beta_one * moment + (1.0 - beta_one) * grad_sum, moment
    )
    new_var = jnp.where(
        touched,
        beta_two * row_var + (1.0 - beta_two) * jnp.mean(grad_sum * grad_sum, axis=1),
        row_var,
    )
    new_table = jnp.where(
        touched[:, None],
        table - learn_rate * new_moment / (jnp.sqrt(new_var)[:, None] + epsilon),
        table,
    )
    rounded = new_table.astype(jnp.bfloat16)
    blocks = tab_rows // owners
    serve_local = jnp.where(touched, serve_map % tab_rows, tab_rows)
    serve_rows, serve_slots = (
        lax.all_to_all(
            rounded.reshape(blocks, owners, row_width),
            "shard",
            split_axis=1,
            concat_axis=1,
            tiled=True,
        ),
        lax.all_to_all(
            serve_local.reshape(blocks, owners), "shard", split_axis=1, concat_axis=1, tiled=True
        ),
    )
    serving_table = place_rows(
        serving_old, serve_slots.reshape(-1), serve_rows.reshape(-1, row_width)
    )
    valid = recv_rows >= 0
    reply = jnp.where(
        valid[:, :, None], rounded[jnp.where(valid, recv_rows, 0)], jnp.zeros((), jnp.bfloat16)
    )
    returned = lax.all_to_all(reply, "shard", split_axis=0, concat_axis=0, tiled=True)
    bag_key = jnp.where(filled, bucket_source // bag_size * fields + bucket_field, -1).reshape(-1)
    member = (jnp.arange(samples * fields, dtype=jnp.int32)[:, None] == bag_key[None, :]).astype(
        jnp.bfloat16
    )
    pooled = jnp.dot(
        member, returned.reshape(owners * capacity, row_width), preferred_element_type=jnp.float32
    )
    features = pooled.reshape(samples, fields * row_width).astype(jnp.bfloat16)
    hidden_one = jax.nn.relu(jnp.dot(features, w_first, preferred_element_type=jnp.float32)).astype(
        jnp.bfloat16
    )
    hidden_two = jax.nn.relu(
        jnp.dot(hidden_one, w_second, preferred_element_type=jnp.float32)
    ).astype(jnp.bfloat16)
    scores = jnp.dot(hidden_two, w_score, preferred_element_type=jnp.float32)
    return (new_table, new_moment, new_var, serving_table, scores)


def solution(mesh):
    in_specs = (
        P(("shard", "rep"), None),
        P(("shard", "rep"), None),
        P(),
        P("shard"),
        P(("shard", "rep"), None, None),
        P("shard", None),
        P("shard", None),
        P("shard"),
        P("shard", None),
        P(),
        P(),
        P(),
    )
    out_specs = (
        P("shard", None),
        P("shard", None),
        P("shard"),
        P("shard", None),
        P(("shard", "rep")),
    )
    return jax.shard_map(
        per_device, mesh=mesh, in_specs=in_specs, out_specs=out_specs, check_vma=False
    )
```

profile of v0, /device:TPU:1, one launch (start us, length us, event | category | flops | bytes accessed | tf_op | source)
XLA Modules:
  0.0 630.0 jit_solution(13959067976011344931)
XLA Ops:
  0.7 1.0 copy.36
  1.8 52.1 %gather_fusion = s32[4096]{0:T(1024)S(1)} fusion(s32[131072]{0:T(1024)} %param.18, s32[4096]{0:T(1024)S(1)} %broadcast_clamp_fusion.2), kind=kCustom, calls=%fused_computation | custom fusion | bytes 49152 | tf_op jit(solution)/shard_map/gather | solution.py:107
  55.4 1.9 fusion.36
  57.2 3.6 fusion.38
  60.9 1.8 fusion.27
  62.9 0.9 fusion.73
  63.7 0.8 compare_select_fusion.2
  64.5 160.6 %gather_fusion.1 = s32[16384]{0:T(1024)} fusion(s32[4096]{0:T(1024)S(1)} %get-tuple-element.150, s32[16384]{0:T(1024)S(1)} %broadcast_clamp_fusion.1), kind=kCustom, calls=%fused_computation.1 | custom fusion | bytes 196608 | tf_op jit(solution)/shard_map/gather | solution.py:144
  225.1 1.6 broadcast_select_fusion.2
  226.7 12.0 %all-to-all-start = ((s32[64,1,256]{2,1,0:T(1,128)}), s32[64,1,256]{2,1,0:T(1,128)S(1)}, u32[]{:S(2)}, u32[]{:S(2)}) async-start(s32[64,1,256]{2,1,0:T(1,128)} %broadcast_select_fusion.2), calls=%async_computation | async-start | bytes 131072 | tf_op jit(solution)/shard_map/all_to_all | solution.py:147
  238.7 62.6 %gather_fusion.2 = bf16[16384,128]{1,0:T(8,128)(2,1)} fusion(bf16[4096,128]{1,0:T(8,128)(2,1)S(1)} %bitcast.79, s32[16384]{0:T(1024)} %copy-done.4), kind=kCustom, calls=%fused_computation.2 | custom fusion | bytes 8454144 | tf_op jit(solution)/shard_map/gather | solution.py:142
  301.3 7.6 %broadcast_select_fusion.1 = bf16[64,256,128]{2,1,0:T(8,128)(2,1)} fusion(bf16[64,256,128]{2,1,0:T(8,128)(2,1)} %bitcast.81, pred[64,256]{1,0:T(8,128)(4,1)S(1)} %bitcast.94), kind=kLoop, calls=%fused_computation.45 | loop fusion | flops 2097152 | bytes 8404992 | tf_op jit(solution)/shard_map/jit(_where)/select_n | solution.py:141
  309.0 10.2 %all-to-all-start.1 = ((bf16[64,256,128]{2,1,0:T(8,128)(2,1)}), bf16[64,256,128]{2,1,0:T(8,128)(2,1)}, u32[]{:S(2)}, u32[]{:S(2)}) async-start(bf16[64,256,128]{2,1,0:T(8,128)(2,1)} %broadcast_select_fusion.1), calls=%async_computation.1 | async-start | bytes 8388608 | tf_op jit(solution)/shard_map/all_to_all | solution.py:146
  319.4 0.6 reshape_reshape.6
  320.2 51.1 %all-to-all-done.1 = bf16[64,256,128]{2,1,0:T(8,128)(2,1)} async-done(((bf16[64,256,128]{2,1,0:T(8,128)(2,1)}), bf16[64,256,128]{2,1,0:T(8,128)(2,1)}, u32[]{:S(2)}, u32[]{:S(2)}) %all-to-all-start.1) | async-done | bytes 4194336 | tf_op jit(solution)/shard_map/all_to_all | solution.py:146
  371.3 73.7 %while.24 = (s32[]{:T(128)}, f32[2048,128]{1,0:T(8,128)S(1)}, f32[2048]{0:T(1024)S(1)}, s32[8,2048]{1,0:T(8,128)}, bf16[8,2048,128]{2,1,0:T(8,128)(2,1)}, /*index=5*/s32[]{:T(128)}, s32[]{:T(128)}) while((s32[]{:T(128)}, f32[2048,128]{1,0:T(8,128)S(1)}, f32[2048]{0:T(1024)S(1)}, s32[8,2048]{1,0:T(8,128)}, ...), condition=%wide.region_6.7_spmd.clone, body=%wide.region_4.6_spmd.clone.sunk | while | flops 1095239680 | bytes 2687080 | solution.py:66
  371.3 0.8 constant_dynamic-slice_fusion.2
  372.1 2.1 convert_reduce_fusion.6
  374.2 6.3 fusion.94
  380.5 0.9 constant_dynamic-slice_fusion.2
  381.4 2.1 convert_reduce_fusion.6
  383.4 6.3 fusion.94
  389.7 0.9 constant_dynamic-slice_fusion.2
  390.6 2.1 convert_reduce_fusion.6
  392.7 6.3 fusion.94
  398.9 0.9 constant_dynamic-slice_fusion.2
  399.8 2.1 convert_reduce_fusion.6
  401.9 6.3 fusion.94
  408.2 0.9 constant_dynamic-slice_fusion.2
  409.0 2.1 convert_reduce_fusion.6
  411.1 6.3 fusion.94
  417.4 0.9 constant_dynamic-slice_fusion.2
  418.2 2.1 convert_reduce_fusion.6
  420.3 6.3 fusion.94
  426.6 0.9 constant_dynamic-slice_fusion.2
  427.5 2.1 convert_reduce_fusion.6
  429.5 6.3 fusion.94
  435.8 0.9 constant_dynamic-slice_fusion.2
  436.7 2.1 convert_reduce_fusion.6
  438.8 6.3 fusion.94
  445.1 5.0 broadcast_in_dim.63
  450.1 8.9 %all_to_all.42 = f32[2,1,264192]{2,1,0:T(1,128)} all-to-all(f32[2,1,264192]{2,1,0:T(1,128)S(1)} %broadcast_in_dim.63), channel_id=1, replica_groups=mesh['shard'=64,'rep'=2] {'rep'}, dimensions={0} | all-to-all | bytes 4227072 | tf_op jit(solution)/shard_map/all_to_all | solution.py:14
  459.0 10.9 %reduce_sum.56 = f32[264192]{0:T(1024)S(1)} reduce(f32[2,1,264192]{2,1,0:T(1,128)} %all_to_all.42, f32[]{:T(128)} %constant.124.clone.1), dimensions={0,1}, to_apply=%region_7.8 | reduce | flops 264192 | bytes 3170308 | tf_op jit(solution)/shard_map/reduce_sum | solution.py:20
  470.2 1.3 fusion.70
  471.6 1.4 all_to_all.30
  472.9 1.4 copy.39
  474.3 6.6 %all-to-all-start.3 = ((s32[32,64,1]{0,2,1:T(1,128)}), s32[32,64,1]{0,2,1:T(1,128)}, u32[]{:S(2)}, u32[]{:S(2)}) async-start(s32[32,64,1]{0,2,1:T(1,128)} %copy.39), calls=%async_computation.3 | async-start | bytes 65536 | tf_op jit(solution)/shard_map/all_to_all | solution.py:178
  480.9 1.3 sqrt_add_fusion
  482.2 3.2 fusion.74
  485.4 1.1 copy.40
  486.5 2.6 all-to-all-done.3
  489.2 7.1 %all-to-all-start.4 = ((bf16[32,64,128]{2,0,1:T(8,128)(2,1)}), bf16[32,64,128]{2,0,1:T(8,128)(2,1)S(1)}, u32[]{:S(2)}, u32[]{:S(2)}) async-start(bf16[32,64,128]{2,0,1:T(8,128)(2,1)} %copy.40), calls=%async_computation.4 | async-start | bytes 1048576 | tf_op jit(solution)/shard_map/all_to_all | solution.py:171
  496.4 57.4 %gather_fusion.3 = bf16[16384,128]{1,0:T(8,128)(2,1)} fusion(bf16[2048,128]{1,0:T(8,128)(2,1)S(1)} %get-tuple-element.141, s32[16384]{0:T(1024)S(1)} %broadcast_clamp_fusion), kind=kCustom, calls=%fused_computation.3 | custom fusion | bytes 8454144 | tf_op jit(solution)/shard_map/gather | solution.py:187
  553.7 7.6 %broadcast_select_fusion = bf16[64,256,128]{2,1,0:T(8,128)(2,1)} fusion(bf16[64,256,128]{2,1,0:T(8,128)(2,1)} %bitcast.80, pred[64,256]{1,0:T(8,128)(4,1)S(1)} %bitcast.93), kind=kLoop, calls=%fused_computation.44 | loop fusion | flops 2097152 | bytes 8404992 | tf_op jit(solution)/shard_map/jit(_where)/select_n | solution.py:186
  561.4 10.2 %all-to-all-start.5 = ((bf16[64,256,128]{2,1,0:T(8,128)(2,1)}), bf16[64,256,128]{2,1,0:T(8,128)(2,1)}, u32[]{:S(2)}, u32[]{:S(2)}) async-start(bf16[64,256,128]{2,1,0:T(8,128)(2,1)} %broadcast_select_fusion), calls=%async_computation.5 | async-start | bytes 8388608 | tf_op jit(solution)/shard_map/all_to_all | solution.py:189
  571.8 0.8 copy.42
  573.2 16.5 %while.25 = (s32[]{:T(128)}, bf16[4,512,128]{2,1,0:T(8,128)(2,1)}, s32[4]{0:T(128)S(1)}, s32[32,64]{1,0:T(8,128)}, bf16[2048,128]{1,0:T(8,128)(2,1)S(1)}, /*inde...) while((s32[]{:T(128)}, bf16[4,512,128]{2,1,0:T(8,128)(2,1)}, s32[4]{0:T(128)S(1)}, ...), condition=%wide.wide.region_11.12_spmd, body=%wide.wide.region_9.11_spmd.sunk | while | flops 273809920 | bytes 814193 | solution.py:84
  575.0 2.3 fusion.97
  579.1 2.3 fusion.97
  583.3 2.3 fusion.97
  587.4 2.3 fusion.97
  589.7 31.5 %all-to-all-done.5 = bf16[64,256,128]{2,1,0:T(8,128)(2,1)} async-done(((bf16[64,256,128]{2,1,0:T(8,128)(2,1)}), bf16[64,256,128]{2,1,0:T(8,128)(2,1)}, u32[]{:S(2)}, u32[]{:S(2)}) %all-to-all-start.5) | async-done | bytes 4194336 | tf_op jit(solution)/shard_map/all_to_all | solution.py:189
  621.2 7.4 %fusion.41 = bf16[512,128]{1,0:T(8,128)(2,1)S(1)} fusion(bf16[16384,128]{1,0:T(8,128)(2,1)} %bitcast.25, s32[16384]{0:T(1024)S(1)} %fusion.53), kind=kOutput, calls=%fused_computation.54 | convolution fusion | flops 2155937792 | bytes 4390912 | tf_op jit(solution)/shard_map/dot_general | solution.py:194
  629.3 0.7 convolution_bitcast_fusion.1
  (85 shorter events, 11.1 us)
Async XLA Ops:
  0.6 628.1 %copy-start = (bf16[1024,1024]{1,0:T(8,128)(2,1)S(1)}, bf16[1024,1024]{1,0:T(8,128)(2,1)}, u32[]{:S(2)}) copy-start(bf16[1024,1024]{1,0:T(8,128)(2,1)} %param.26) | copy-start | bytes 6291460
  1.8 52.1 %copy-start.9 = (s32[128,4]{0,1:T(4,128)S(1)}, s32[128,4]{0,1:T(4,128)}, u32[]{:S(2)}) copy-start(s32[128,4]{0,1:T(4,128)} %param.17) | copy-start | bytes 6148
  64.5 160.6 %copy-start.4 = (s32[16384]{0:T(1024)}, s32[16384]{0:T(1024)S(1)}, u32[]{:S(2)}) copy-start(s32[16384]{0:T(1024)S(1)} %broadcast_clamp_fusion.1) | copy-start | bytes 196612
  64.5 174.2 %copy-start.1 = (bf16[128,32,128]{2,1,0:T(8,128)(2,1)S(1)}, bf16[128,32,128]{2,1,0:T(8,128)(2,1)}, u32[]{:S(2)}) copy-start(bf16[128,32,128]{2,1,0:T(8,128)(2,1)} %param.20) | copy-start | bytes 3145732
  226.7 82.3 %all-to-all-start = ((s32[64,1,256]{2,1,0:T(1,128)}), s32[64,1,256]{2,1,0:T(1,128)S(1)}, u32[]{:S(2)}, u32[]{:S(2)}) async-start(s32[64,1,256]{2,1,0:T(1,128)} %broadcast_select_fusion.2), calls=%async_computation | async-start | bytes 131072 | tf_op jit(solution)/shard_map/all_to_all | solution.py:147
  309.0 62.3 %all-to-all-start.1 = ((bf16[64,256,128]{2,1,0:T(8,128)(2,1)}), bf16[64,256,128]{2,1,0:T(8,128)(2,1)}, u32[]{:S(2)}, u32[]{:S(2)}) async-start(bf16[64,256,128]{2,1,0:T(8,128)(2,1)} %broadcast_select_fusion.1), calls=%async_computation.1 | async-start | bytes 8388608 | tf_op jit(solution)/shard_map/all_to_all | solution.py:146
  469.9 12.4 %copy-start.2 = (f32[264192]{0:T(1024)}, f32[264192]{0:T(1024)S(1)}, u32[]{:S(2)}) copy-start(f32[264192]{0:T(1024)S(1)} %reduce_sum.56) | copy-start | bytes 3170308
  474.3 14.8 %all-to-all-start.3 = ((s32[32,64,1]{0,2,1:T(1,128)}), s32[32,64,1]{0,2,1:T(1,128)}, u32[]{:S(2)}, u32[]{:S(2)}) async-start(s32[32,64,1]{0,2,1:T(1,128)} %copy.39), calls=%async_computation.3 | async-start | bytes 65536 | tf_op jit(solution)/shard_map/all_to_all | solution.py:178
  489.2 72.2 %all-to-all-start.4 = ((bf16[32,64,128]{2,0,1:T(8,128)(2,1)}), bf16[32,64,128]{2,0,1:T(8,128)(2,1)S(1)}, u32[]{:S(2)}, u32[]{:S(2)}) async-start(bf16[32,64,128]{2,0,1:T(8,128)(2,1)} %copy.40), calls=%async_computation.4 | async-start | bytes 1048576 | tf_op jit(solution)/shard_map/all_to_all | solution.py:171
  561.4 10.2 %copy-start.8 = (bf16[1024]{0:T(1024)(128)(2,1)S(1)}, bf16[1024]{0:T(1024)(128)(2,1)}, u32[]{:S(2)}) copy-start(bf16[1024]{0:T(1024)(128)(2,1)} %param.27) | copy-start | bytes 6148
  561.4 10.2 %copy-start.6 = (pred[64,256]{1,0:T(8,128)(4,1)S(1)}, pred[64,256]{1,0:T(8,128)(4,1)}, u32[]{:S(2)}) copy-start(pred[64,256]{1,0:T(8,128)(4,1)} %get-tuple-element.139) | copy-start | bytes 49156
  561.4 10.4 %copy-start.5 = (s32[64,1,256]{2,1,0:T(1,128)S(1)}, s32[64,1,256]{2,1,0:T(1,128)}, u32[]{:S(2)}) copy-start(s32[64,1,256]{2,1,0:T(1,128)} %get-tuple-element.149) | copy-start | bytes 196612
  561.4 59.8 %all-to-all-start.5 = ((bf16[64,256,128]{2,1,0:T(8,128)(2,1)}), bf16[64,256,128]{2,1,0:T(8,128)(2,1)}, u32[]{:S(2)}, u32[]{:S(2)}) async-start(bf16[64,256,128]{2,1,0:T(8,128)(2,1)} %broadcast_select_fusion), calls=%async_computation.5 | async-start | bytes 8388608 | tf_op jit(solution)/shard_map/all_to_all | solution.py:189
  572.6 0.6 copy-start.7
  621.2 7.5 %copy-start.3 = (bf16[512,1024]{1,0:T(8,128)(2,1)S(1)}, bf16[512,1024]{1,0:T(8,128)(2,1)}, u32[]{:S(2)}) copy-start(bf16[512,1024]{1,0:T(8,128)(2,1)} %param.25) | copy-start | bytes 3145732
where the time goes:
time: 639 us; the launch traced here: 630 us
  local copies, waits for them, and re-layouts  354 us (55%)
  waiting for transfers between devices  85.3 us (13%)
  matrix products  70.5 us (11%)
  other arithmetic  63.6 us (10%)
  starting transfers between devices  46 us (7%)
  blocking collectives  8.91 us (1%)
    gather x1, local copies, waits for them, and re-layouts, per_device(): send_rows = jnp.where(filled, local_row[bucket_source], -1)  161 us
    gather x1, local copies, waits for them, and re-layouts, per_device(): flat_grads[bucket_source]  62.6 us
    gather x1, local copies, waits for them, and re-layouts, per_device(): rounded[jnp.where(valid, recv_rows, 0)]  57.4 us
    gather x2, local copies, waits for them, and re-layouts, per_device(): position = train_map[touched_ids.reshape(slot_count)]  52.1 us
    all_to_all x1, waiting for transfers between devices, per_device(): lax.all_to_all(send_grads, 'shard', split_axis=0, concat_axis=0, tiled=True)  51.1 us
    dot_general x8, matrix products, add_block(): lax.dot_general(hit, grad_piece, (((0,), (0,)), ((), ())), preferred_elem...  50.1 us
    all_to_all x1, waiting for transfers between devices, per_device(): lax.all_to_all(reply, 'shard', split_axis=0, concat_axis=0, tiled=True)  31.5 us
    reduce_sum x8, other arithmetic, add_block(): touch = touch + jnp.sum(hit.astype(jnp.float32), axis=0)  16.5 us
  transfers between devices with their start and end apart: 5, of which 3 were waited for; matrix products, arithmetic and copies ran while one was open for 25% of the time, Pallas kernels for 0%

commit v1 on v0

v1 whole, which is shorter than its diff:
```python
import functools

import jax
import jax.numpy as jnp
from jax import lax
from jax.experimental import pallas as pl
from jax.experimental.pallas import tpu as pltpu
from jax.sharding import PartitionSpec as P

beta_one = 0.9
beta_two = 0.999
learn_rate = 0.1
epsilon = 1e-06

ROUND = 64
DEVS = 128
LANES = 128
UNTOUCHED = 1e30
F32 = jnp.float32
BF16 = jnp.bfloat16
I32 = jnp.int32
ALL = ("shard", "rep")


def iota(shape, dim):
    return lax.broadcasted_iota(I32, shape, dim)


def one_hot(mask):
    return jnp.where(mask, 1.0, 0.0).astype(BF16)


def route_kernel(round_ref, ids_ref, map_ref, extra_ref, slots_ref, keys_ref, row_ref):
    bag, samples = ids_ref.shape[0] - 4, ids_ref.shape[1]
    step = 4
    wide = step * samples
    first = round_ref[0] * ROUND
    table = map_ref[...]
    high = (table >> 9).astype(F32).T
    low = ((table & 511) - 256).astype(F32).T
    parts = jnp.concatenate([high, low], axis=0).astype(BF16)
    upto = one_hot(iota((wide, wide), 0) <= iota((wide, wide), 1))
    ends = []
    total = jnp.zeros((1, samples), I32)
    for f in range(3):
        total = total + ids_ref[bag + f : bag + f + 1, :]
        ends.append(total)
    sample = iota((1, samples), 1)
    seen = jnp.zeros((DEVS, 1), F32)
    layout = jnp.zeros((DEVS, 4 * ROUND), F32)
    for t in range(0, bag, step):
        ids = jnp.concatenate([ids_ref[t + u : t + u + 1, :] for u in range(step)], axis=1)
        keys = []
        for u in range(step):
            field = sum((jnp.where(e <= t + u, 1, 0) for e in ends), jnp.zeros((1, samples), I32))
            keys.append(field * samples + sample)
        key = jnp.concatenate(keys, axis=1) + 1
        hit = one_hot(iota((table.shape[0], wide), 0) == (ids >> 7))
        both = jnp.dot(parts, hit, preferred_element_type=F32)
        value = both[:LANES] * 512.0 + both[LANES:] + 256.0
        value = jnp.where(iota((LANES, wide), 0) == (ids & 127), value, 0.0)
        position = jnp.sum(value, axis=0, keepdims=True).astype(I32)
        owner = position >> 11
        stride = (position >> 6) & 31
        dest = (position & 63) * 2 + ((stride + owner) & 1)
        local = owner * 16 + (stride >> 1) + 1
        mine = iota((DEVS, wide), 0) == dest
        hot = one_hot(mine)
        running = jnp.dot(hot, upto, preferred_element_type=F32)
        rank = jnp.sum(jnp.where(mine, running + seen, 0.0), axis=0, keepdims=True)
        seen = seen + running[:, wide - 1 : wide]
        rank = rank.astype(I32) - 1 - first
        here = iota((ROUND, wide), 0) == rank
        columns = jnp.concatenate(
            [
                jnp.where(here, v.astype(F32), 0.0)
                for v in (local >> 5, key >> 5, local & 31, key & 31)
            ],
            axis=0,
        ).astype(BF16)
        layout = layout + lax.dot_general(
            hot, columns, (((1,), (1,)), ((), ())), preferred_element_type=F32
        )
        fits = (rank >= 0) & (rank < ROUND)
        slot = jnp.where(fits, dest * ROUND + rank, DEVS * ROUND)
        for u in range(step):
            slots_ref[t + u : t + u + 1, :] = slot[:, u * samples : (u + 1) * samples]
    layout = layout[:, :LANES] * 32.0 + layout[:, LANES:] - 1.0
    keys_ref[...] = layout
    most = jnp.max(seen, axis=0, keepdims=True)
    line = jnp.where(iota((DEVS, LANES), 1) < ROUND, layout, extra_ref[...])
    row_ref[:, 0:1, :] = line.reshape(DEVS, 1, LANES)
    row_ref[:, 1:8, :] = jnp.broadcast_to(most.reshape(1, 1, 1), (DEVS, 7, LANES))


def route(round_index, ids, train_map, extra):
    bag = ids.shape[0] - 4
    return pl.pallas_call(
        route_kernel,
        in_specs=[pl.BlockSpec(memory_space=pltpu.SMEM)]
        + [pl.BlockSpec(memory_space=pltpu.VMEM)] * 3,
        out_specs=[pl.BlockSpec(memory_space=pltpu.VMEM)] * 3,
        out_shape=(
            jax.ShapeDtypeStruct((bag, ids.shape[1]), I32),
            jax.ShapeDtypeStruct((DEVS, LANES), F32),
            jax.ShapeDtypeStruct((DEVS, 8, LANES), F32),
        ),
        name="route",
    )(round_index, ids, train_map, extra)


def pack_kernel(slots_ref, grads_ref, out_ref, from_ref, to_ref):
    bag, samples = slots_ref.shape
    block = 512

    def widen(i, carry):
        at = pl.multiple_of(i * block, block)
        from_ref[pl.ds(at, block), :] = grads_ref[pl.ds(at, block), :].astype(F32)
        return carry

    def clear(i, carry):
        at = pl.multiple_of(i * block, block)
        to_ref[pl.ds(at, block), :] = jnp.zeros((block, LANES), F32)
        return carry

    def move(b, carry):
        for t in range(bag):
            to_ref[pl.ds(slots_ref[t, b], 1), :] = from_ref[pl.ds(b * bag + t, 1), :]
        return carry

    def narrow(i, carry):
        at = pl.multiple_of(i * block, block)
        out_ref[pl.ds(at, block), :] = to_ref[pl.ds(at, block), :].astype(BF16)
        return carry

    lax.fori_loop(0, bag * samples // block, widen, 0)
    lax.fori_loop(0, DEVS * ROUND // block, clear, 0)
    lax.fori_loop(0, samples, move, 0)
    lax.fori_loop(0, DEVS * ROUND // block, narrow, 0)


def pack(slots, grads):
    return pl.pallas_call(
        pack_kernel,
        in_specs=[
            pl.BlockSpec(memory_space=pltpu.SMEM),
            pl.BlockSpec(memory_space=pltpu.VMEM),
        ],
        out_specs=pl.BlockSpec(memory_space=pltpu.VMEM),
        out_shape=jax.ShapeDtypeStruct((DEVS * ROUND, LANES), BF16),
        scratch_shapes=[
            pltpu.VMEM(grads.shape, F32),
            pltpu.VMEM((DEVS * ROUND + 8, LANES), F32),
        ],
        name="pack",
    )(slots, grads)


def pair_up(line, low):
    other = pltpu.roll(line, ROUND, 1)
    half = DEVS // 2
    left = (line if low else other)[:half]
    right = (other if low else line)[half:]
    return jnp.where(iota((half, LANES), 1) < ROUND, left, right)


def pair_rows(ref, i):
    half = DEVS // 2
    left = ref[pl.ds(i * 8, 8)]
    right = ref[pl.ds(half + i * 8, 8)]
    pieces = []
    for u in range(8):
        pieces += [left[u], right[u]]
    return jnp.concatenate(pieces, axis=0)


def lanes_of(index_ref, i):
    rows = index_ref[pl.ds(pl.multiple_of(i * 8, 8), 8), :]
    return jnp.concatenate([rows[u : u + 1] for u in range(8)], axis=1)


def add_rows(index_ref, rows_ref, acc_ref, with_count):
    width = 8 * LANES

    def add(i, carry):
        hit = one_hot(iota((acc_ref.shape[0], width), 0) == lanes_of(index_ref, i))
        rows = pair_rows(rows_ref, i)
        if with_count:
            rows = jnp.concatenate([rows, jnp.ones_like(rows)], axis=1)
        acc_ref[...] = acc_ref[...] + jnp.dot(hit, rows, preferred_element_type=F32)
        return carry

    lax.fori_loop(0, DEVS * ROUND // width, add, 0)


def sum_kernel(line_ref, rows_ref, start_ref, out_ref, index_ref, *, low, with_count):
    index_ref[...] = pair_up(line_ref[...], low).astype(I32)
    out_ref[...] = start_ref[...]
    add_rows(index_ref, rows_ref, out_ref, with_count)


def sum_rows(line, rows, start, low, with_count):
    return pl.pallas_call(
        functools.partial(sum_kernel, low=low, with_count=with_count),
        in_specs=[pl.BlockSpec(memory_space=pltpu.VMEM)] * 3,
        out_specs=pl.BlockSpec(memory_space=pltpu.VMEM),
        out_shape=jax.ShapeDtypeStruct(start.shape, F32),
        scratch_shapes=[pltpu.VMEM((DEVS // 2, LANES), I32)],
        name="sum_rows",
    )(line, rows, start)


def update_kernel(
    core_ref, state_ref, rows_ref, start_ref, new_ref, sums_ref, spots_ref, index_ref, acc_ref
):
    index_ref[...] = pair_up(state_ref[:, 16:17, :].reshape(DEVS, LANES), True).astype(I32)
    acc_ref[...] = start_ref[...]
    add_rows(index_ref, rows_ref, acc_ref, True)
    core = core_ref[0]

    def step(i, carry):
        at = pl.multiple_of(i * LANES, LANES)
        part = pl.ds(i * 16, 16)
        total = acc_ref[pl.ds(at, LANES), :]
        grad = total[:, :LANES].reshape(16, 8, LANES)
        touched = (total[:, LANES:] > 0.5).reshape(16, 8, LANES)
        shape = (16, 8, LANES)
        source = iota(shape, 0)
        within = iota(shape, 1)
        lane = iota(shape, 2)
        parity = (core + i * 8 + (source >> 1)) & 1
        own = (source & 1) * 16 + within * 2 + parity
        extra = jnp.broadcast_to(state_ref[part, 16:17, :], shape)
        var = jnp.sum(jnp.where(lane == ROUND + own, extra, 0.0), axis=2, keepdims=True)
        spot = jnp.sum(jnp.where(lane == ROUND + 32 + own, extra, 0.0), axis=2, keepdims=True)
        table = state_ref[part, 0:8, :]
        moment = state_ref[part, 8:16, :]
        mean = jnp.sum(grad * grad, axis=2, keepdims=True) * (1.0 / LANES)
        new_var = beta_two * var + (1.0 - beta_two) * mean
        new_moment = beta_one * moment + (1.0 - beta_one) * grad
        new_table = table - learn_rate * new_moment / (jnp.sqrt(new_var) + epsilon)
        new_table = jnp.where(touched, new_table, table)
        new_ref[pl.ds(at, LANES), :] = new_table.reshape(LANES, LANES).astype(BF16)
        sums_ref[part] = jnp.where(touched, grad, UNTOUCHED)
        spot = jnp.where(touched & (lane == within), spot, 0.0)
        away = jnp.where(touched | (lane != within), 0.0, 4096.0)
        spots_ref[pl.ds(pl.multiple_of(i * 16, 16), 16), :] = jnp.sum(spot + away, axis=1)
        return carry

    lax.fori_loop(0, 8, step, 0)


def update(core, state, rows, start):
    return pl.pallas_call(
        update_kernel,
        in_specs=[pl.BlockSpec(memory_space=pltpu.SMEM)]
        + [pl.BlockSpec(memory_space=pltpu.VMEM)] * 3,
        out_specs=[pl.BlockSpec(memory_space=pltpu.VMEM)] * 3,
        out_shape=(
            jax.ShapeDtypeStruct((start.shape[0], LANES), BF16),
            jax.ShapeDtypeStruct((DEVS, 8, LANES), F32),
            jax.ShapeDtypeStruct((DEVS, LANES), F32),
        ),
        scratch_shapes=[
            pltpu.VMEM((DEVS // 2, LANES), I32),
            pltpu.VMEM(start.shape, F32),
        ],
        name="update",
    )(core, state, rows, start)


def reply_kernel(line_ref, new_ref, out_ref, turned_ref):
    turned_ref[...] = line_ref[...].T
    rows = new_ref.shape[0]

    def look(i, carry):
        turned = pltpu.roll(turned_ref[0:ROUND, :], LANES - i * 8, 1).astype(I32)
        hit = jnp.concatenate(
            [one_hot(iota((ROUND, rows), 1) == turned[:, u : u + 1]) for u in range(8)], axis=0
        )
        found = jnp.dot(hit, new_ref[...], preferred_element_type=F32)
        at = pl.multiple_of(i * 8 * ROUND, 8 * ROUND)
        out_ref[pl.ds(at, 8 * ROUND), :] = found.astype(BF16)
        return carry

    lax.fori_loop(0, DEVS // 8, look, 0)


def reply(line, new_rows):
    return pl.pallas_call(
        reply_kernel,
        in_specs=[pl.BlockSpec(memory_space=pltpu.VMEM)] * 2,
        out_specs=pl.BlockSpec(memory_space=pltpu.VMEM),
        out_shape=jax.ShapeDtypeStruct((DEVS * ROUND, LANES), BF16),
        scratch_shapes=[pltpu.VMEM((DEVS, LANES), F32)],
        name="reply",
    )(line, new_rows)


def score_kernel(
    keys_ref, rows_ref, start_ref, first_ref, second_ref, score_ref, out_ref, index_ref, acc_ref
):
    index_ref[...] = pair_up(keys_ref[...], False).astype(I32)
    acc_ref[...] = start_ref[...]
    add_rows(index_ref, rows_ref, acc_ref, False)
    samples = out_ref.shape[1]
    pooled = jnp.concatenate(
        [acc_ref[f * samples : (f + 1) * samples, :] for f in range(4)], axis=1
    ).astype(BF16)
    hidden = jnp.dot(pooled, first_ref[...], preferred_element_type=F32)
    hidden = jnp.maximum(hidden, 0.0).astype(BF16)
    hidden = jnp.dot(hidden, second_ref[...], preferred_element_type=F32)
    hidden = jnp.maximum(hidden, 0.0).astype(BF16)
    weights = jnp.broadcast_to(score_ref[...], (16, score_ref.shape[1]))
    scores = lax.dot_general(
        weights, hidden, (((1,), (1,)), ((), ())), preferred_element_type=F32
    )
    out_ref[...] = scores[0:1, :]


def score(keys, rows, start, w_first, w_second, w_score):
    return pl.pallas_call(
        score_kernel,
        in_specs=[pl.BlockSpec(memory_space=pltpu.VMEM)] * 6,
        out_specs=pl.BlockSpec(memory_space=pltpu.VMEM),
        out_shape=jax.ShapeDtypeStruct((1, start.shape[0] // 4), F32),
        scratch_shapes=[
            pltpu.VMEM((DEVS // 2, LANES), I32),
            pltpu.VMEM(start.shape, F32),
        ],
        name="score",
    )(keys, rows, start, w_first, w_second, w_score)


def exchange(value, width):
    out = lax.all_to_all(value.reshape(DEVS, -1, width), ALL, 0, 0, tiled=True)
    return out


def place_rows(serving_old, slot_index, rows_in):
    tab_rows, row_width = serving_old.shape
    block = 512
    old_blocks = serving_old.reshape(tab_rows // block, block, row_width)
    firsts = jnp.arange(tab_rows // block, dtype=jnp.int32) * block

    def place_block(pieces):
        old_piece, first = pieces
        wanted = first + jnp.arange(block, dtype=jnp.int32)
        hit = (wanted[:, None] == slot_index[None, :]).astype(jnp.bfloat16)
        fresh = jnp.dot(hit, rows_in, preferred_element_type=jnp.float32)
        found = jnp.sum(hit.astype(jnp.float32), axis=1) > 0.5
        return jnp.where(found[:, None], fresh.astype(jnp.bfloat16), old_piece)

    return lax.map(place_block, (old_blocks, firsts)).reshape(tab_rows, row_width)


def per_device(
    touched_ids,
    bag_lengths,
    train_map,
    serve_map,
    slot_grads,
    table,
    moment,
    row_var,
    serving_old,
    w_first,
    w_second,
    w_score,
):
    owners = lax.axis_size("shard")
    owner = lax.axis_index("shard")
    rep = lax.axis_index("rep")
    tab_rows, row_width = table.shape
    samples, bag = touched_ids.shape
    swap = [(0, 1), (1, 0)]
    odd = owner % 2 == 1
    rows_here = tab_rows // 2

    ids = jnp.concatenate([touched_ids, bag_lengths], axis=1).T
    map_rows = train_map.reshape(-1, LANES)
    grads = slot_grads.reshape(samples * bag, row_width)

    def outgoing(value):
        half = lax.dynamic_slice_in_dim(value, rep * rows_here, rows_here, 0)
        half = half.reshape(8, 2, owners, row_width)
        half = jnp.where(odd, half[:, ::-1], half)
        return half.transpose(2, 1, 0, 3).reshape(DEVS, 8, row_width)

    spots = (serve_map % tab_rows).astype(F32).reshape(tab_rows // owners, owners).T
    spread = jnp.concatenate([row_var.reshape(tab_rows // owners, owners).T, spots], axis=1)
    spread = jnp.broadcast_to(spread[:, None, :], (owners, 2, 2 * tab_rows // owners))
    extra = jnp.concatenate([jnp.zeros((DEVS, ROUND), F32), spread.reshape(DEVS, -1)], axis=1)

    slots, keys, head = route(jnp.zeros((1,), I32), ids, map_rows, extra)
    state = jnp.concatenate([outgoing(table), outgoing(moment), head], axis=1)
    state = exchange(state, row_width)
    received = exchange(pack(slots, grads), row_width)
    state, received = lax.optimization_barrier((state, received))
    rounds = (jnp.max(state[:, 17, 0]).astype(I32) + ROUND - 1) // ROUND

    def more_sums(carry):
        k, acc = carry
        slots, _, head = route(k.reshape(1), ids, map_rows, extra)
        line = exchange(head, row_width)[:, 0, :]
        got = exchange(pack(slots, grads), row_width)
        return (k + 1, sum_rows(line, got, acc, True, True))

    one = jnp.ones((), I32)
    _, start = lax.while_loop(
        lambda c: c[0] < rounds,
        more_sums,
        (one, jnp.zeros((rows_here, 2 * row_width), F32)),
    )
    new_rows, sums, places = update(rep.reshape(1).astype(I32), state, received, start)

    back = exchange(sums, row_width)
    answer = exchange(reply(state[:, 16, :], new_rows), row_width)

    other_rows = lax.ppermute(new_rows, "rep", swap)
    places = places[:, :8].reshape(-1).astype(I32)
    other_places = lax.ppermute(places, "rep", swap)
    serving_table = place_rows(
        serving_old,
        jnp.concatenate([places, other_places]),
        jnp.concatenate([new_rows, other_rows]),
    )

    back = back.reshape(owners, 2, 8, row_width)
    back = jnp.where(odd, back[:, ::-1], back)
    half = back.transpose(2, 1, 0, 3).reshape(rows_here, row_width)
    other = lax.ppermute(half, "rep", swap)
    grad_sum = jnp.where(
        rep == 0, jnp.concatenate([half, other]), jnp.concatenate([other, half])
    )
    touched = grad_sum[:, :1] < 0.5 * UNTOUCHED
    new_moment = jnp.where(touched, beta_one * moment + (1.0 - beta_one) * grad_sum, moment)
    mean = jnp.mean(jnp.where(touched, grad_sum * grad_sum, 0.0), axis=1)
    new_var = jnp.where(touched[:, 0], beta_two * row_var + (1.0 - beta_two) * mean, row_var)
    new_table = jnp.where(
        touched, table - learn_rate * new_moment / (jnp.sqrt(new_var)[:, None] + epsilon), table
    )

    def more_pooled(carry):
        k, acc = carry
        _, keys, head = route(k.reshape(1), ids, map_rows, extra)
        line = exchange(head, row_width)[:, 0, :]
        got = exchange(reply(line, new_rows), row_width)
        return (k + 1, sum_rows(keys, got, acc, False, False))

    answer, rounds = lax.optimization_barrier((answer, rounds))
    _, pooled = lax.while_loop(
        lambda c: c[0] < rounds,
        more_pooled,
        (one, jnp.zeros((4 * samples, row_width), F32)),
    )
    scores = score(keys, answer, pooled, w_first, w_second, w_score.reshape(1, -1))
    return (new_table, new_moment, new_var, serving_table, scores.reshape(samples))


def solution(mesh):
    in_specs = (
        P(("shard", "rep"), None),
        P(("shard", "rep"), None),
        P(),
        P("shard"),
        P(("shard", "rep"), None, None),
        P("shard", None),
        P("shard", None),
        P("shard"),
        P("shard", None),
        P(),
        P(),
        P(),
    )
    out_specs = (
        P("shard", None),
        P("shard", None),
        P("shard"),
        P("shard", None),
        P(("shard", "rep")),
    )
    return jax.shard_map(
        per_device, mesh=mesh, in_specs=in_specs, out_specs=out_specs, check_vma=False
    )
```

time: 639 us -> 170 us (0.27); the launches traced: 630 us -> 169 us
  local copies, waits for them, and re-layouts: 354 us -> 11.5 us
  matrix products: 70.5 us -> 9.98 us
  other arithmetic: 63.6 us -> 14.7 us
  Pallas kernels: 0 us -> 45.6 us
  waiting for transfers between devices: 85.3 us -> 53.2 us
  starting transfers between devices: 46 us -> 32.9 us
  blocking collectives: 8.91 us -> 0 us
    gather x5 -> x0, local copies, waits for them, and re-layouts: 333 us -> none  [the longest x1 161 us: per_device(): send_rows = jnp.where(filled, local_row[bucket_source], -1)]
    dot_general x13 -> x0, matrix products: 61.1 us -> none  [the longest x8 50.1 us: add_block(): lax.dot_general(hit, grad_piece, (((0,), (0,)), ((), ())), preferred_elem...]
    pallas_call x0 -> x5, Pallas kernels: none -> 45.6 us  [the longest x1 12.6 us: reply(): pl.pallas_call(reply_kernel, in_specs=[pl.BlockSpec(memory_space=pltpu.VM...]
    all_to_all x5 -> x4, waiting for transfers between devices: 85.3 us -> 53.2 us  [exchange(): out = lax.all_to_all(value.reshape(DEVS, -1, width), ALL, 0, 0, tiled=True)]
    reduce_sum x12 -> x1, other arithmetic: 28 us -> 0.64 us  [per_device(): mean = jnp.mean(jnp.where(touched, grad_sum * grad_sum, 0.0), axis=1)]
    all_to_all x5 -> x4, starting transfers between devices: 46 us -> 30.3 us  [exchange(): out = lax.all_to_all(value.reshape(DEVS, -1, width), ALL, 0, 0, tiled=True)]
    select_n x10 -> x2, other arithmetic: 19.2 us -> 3.43 us  [the longest x1 1.78 us: per_device(): jnp.where(rep == 0, jnp.concatenate([half, other]), jnp.concatenate([othe...]
    all_to_all x1 -> x0, blocking collectives: 8.91 us -> none  [from_everyone(): lax.all_to_all(jnp.broadcast_to(value[None], (size, *value.shape)), axis,...]
  transfers between devices with their start and end apart: 5 -> 7, of which waited for: 3 -> 3; matrix products, arithmetic and copies ran while one was open for 25% -> 15% of each run, Pallas kernels for 0% -> 12%
where the time goes in v1:
time: 170 us; the launch traced here: 169 us
  waiting for transfers between devices  53.2 us (31%)
  Pallas kernels  45.6 us (27%)
  starting transfers between devices  32.9 us (19%)
  other arithmetic  14.7 us (9%)
  local copies, waits for them, and re-layouts  11.5 us (7%)
  matrix products  9.98 us (6%)
    all_to_all x4, waiting for transfers between devices, exchange(): out = lax.all_to_all(value.reshape(DEVS, -1, width), ALL, 0, 0, tiled=True)  53.2 us
    all_to_all x4, starting transfers between devices, exchange(): out = lax.all_to_all(value.reshape(DEVS, -1, width), ALL, 0, 0, tiled=True)  30.3 us
    pallas_call x1, Pallas kernels, reply(): pl.pallas_call(reply_kernel, in_specs=[pl.BlockSpec(memory_space=pltpu.VM...  12.6 us
    pallas_call x1, Pallas kernels, update(): pl.pallas_call(update_kernel, in_specs=[pl.BlockSpec(memory_space=pltpu.S...  10.1 us
    dot_general x4, matrix products, place_block(): fresh = jnp.dot(hit, rows_in, preferred_element_type=jnp.float32)  9.98 us
    pallas_call x1, Pallas kernels, pack(): pl.pallas_call(pack_kernel, in_specs=[pl.BlockSpec(memory_space=pltpu.SME...  8.32 us
    pallas_call x1, Pallas kernels, score(): pl.pallas_call(score_kernel, in_specs=[pl.BlockSpec(memory_space=pltpu.VM...  7.4 us
    pallas_call x1, Pallas kernels, route(): pl.pallas_call(route_kernel, in_specs=[pl.BlockSpec(memory_space=pltpu.SM...  7.12 us
  transfers between devices with their start and end apart: 7, of which 3 were waited for; matrix products, arithmetic and copies ran while one was open for 15% of the time, Pallas kernels for 12%

profile of v1, /device:TPU:1, one launch (start us, length us, event | category | flops | bytes accessed | tf_op | source)
XLA Modules:
  0.0 169.4 jit_solution(12260183957525917834)
XLA Ops:
  0.6 1.3 constant_dynamic-slice_fusion
  1.9 0.0 copy-start.9
  1.9 0.0 copy-start.7
  1.9 0.0 copy-start.8
  2.0 0.0 copy-start.10
  2.0 0.0 copy-start.2
  2.0 0.3 copy.39
  2.4 0.3 copy.40
  2.7 0.1 reshape.96
  2.8 0.1 reshape.95
  2.9 0.1 copy.41
  3.0 0.1 concatenate.26.extra_ref
  3.1 7.1 %route.3 = (s32[32,128]{1,0:T(8,128)}, f32[128,128]{1,0:T(8,128)}, f32[128,8,128]{2,1,0:T(8,128)}) custom-call(s32[1]{0:T(128)} %constant.85.clone.1.round_ref, s32[36,128]{1,0:T(8,128)S(1)} %add_bitcast_fusion.ids_ref, s32[1024,128]{1,0:T(8,128)S(1)} %bitcast.67, f32[128,128]{1,0:T(8,128)S(1)} %concatenate.26.extra_ref), custom_call_target="tpu_custom_call" | custom-call | tf_op jit(solution)/shard_map/route/pallas_call | solution.py:98
  10.3 2.3 %pad_maximum_fusion = f32[128,24,128]{2,1,0:T(8,128)} fusion(f32[128,8,128]{2,1,0:T(8,128)} %get-tuple-element.127, f32[128,8,128]{2,1,0:T(8,128)S(1)} %bitcast.77, f32[128,8,128]{2,1,0:T(8,128)S(1)} %bitcast.76), kind=kLoop, calls=%fused_computation.12 | loop fusion | flops 786432 | bytes 3145728 | tf_op jit(solution)/shard_map/concatenate | solution.py:396
  12.6 11.5 %all-to-all-start.4 = ((f32[128,24,128]{2,1,0:T(8,128)}), f32[128,24,128]{2,1,0:T(8,128)S(1)}, u32[]{:S(2)}, u32[]{:S(2)}) async-start(f32[128,24,128]{2,1,0:T(8,128)} %pad_maximum_fusion), calls=%async_computation.4 | async-start | bytes 3145728 | tf_op jit(solution)/shard_map/all_to_all | solution.py:336
  24.1 8.3 %pack.2 = bf16[8192,128]{1,0:T(8,128)(2,1)} custom-call(s32[32,128]{1,0:T(8,128)} %get-tuple-element.128.slots_ref, bf16[4096,128]{1,0:T(8,128)(2,1)} %bitcast.21.grads_ref), custom_call_target="tpu_custom_call" | custom-call | tf_op jit(solution)/shard_map/pack/pallas_call | solution.py:143
  32.4 16.1 %all-to-all-done.4.state_ref = f32[128,24,128]{2,1,0:T(8,128)S(1)} async-done(((f32[128,24,128]{2,1,0:T(8,128)}), f32[128,24,128]{2,1,0:T(8,128)S(1)}, u32[]{:S(2)}, u32[]{:S(2)}) %all-to-all-start.4) | async-done | bytes 1572896 | tf_op jit(solution)/shard_map/all_to_all | solution.py:336
  48.4 6.0 %all-to-all-start.5 = ((bf16[128,64,128]{2,1,0:T(8,128)(2,1)}), bf16[128,64,128]{2,1,0:T(8,128)(2,1)}, u32[]{:S(2)}, u32[]{:S(2)}) async-start(bf16[128,64,128]{2,1,0:T(8,128)(2,1)} %bitcast.70), calls=%async_computation.5 | async-start | bytes 4194304 | tf_op jit(solution)/shard_map/all_to_all | solution.py:336
  54.5 0.6 reshape.105.score_ref
  55.1 29.3 %all-to-all-done.5.rows_ref = bf16[128,64,128]{2,1,0:T(8,128)(2,1)} async-done(((bf16[128,64,128]{2,1,0:T(8,128)(2,1)}), bf16[128,64,128]{2,1,0:T(8,128)(2,1)}, u32[]{:S(2)}, u32[]{:S(2)}) %all-to-all-start.5) | async-done | bytes 2097184 | tf_op jit(solution)/shard_map/all_to_all | solution.py:336
  84.4 0.7 slice_reduce_fusion
  85.8 1.4 copy.43
  87.2 1.0 broadcast_in_dim.56
  88.3 10.1 %update.1 = (bf16[1024,128]{1,0:T(8,128)(2,1)S(1)}, f32[128,8,128]{2,1,0:T(8,128)}, f32[128,128]{1,0:T(8,128)}) custom-call(s32[1]{0:T(128)} %bitcast.9.core_ref, f32[128,24,128]{2,1,0:T(8,128)} %copy-done.3, bf16[128,64,128]{2,1,0:T(8,128)(2,1)} %all-to-all-done.5.rows_ref, f32[1024,256]{1,0:T(8,128)} %get-tuple-element.131.start_ref), custom_call_target="tpu_custom_call" | custom-call | tf_op jit(solution)/shard_map/update/pallas_call | solution.py:254
  98.4 1.3 collective-permute-start.2
  99.7 0.8 slice_convert_fusion
  100.6 0.1 convert_element_type.24
  100.6 0.1 collective-permute-start.1
  100.7 3.9 %all-to-all-start.6 = ((f32[128,8,128]{2,1,0:T(8,128)}), f32[128,8,128]{2,1,0:T(8,128)S(1)}, u32[]{:S(2)}, u32[]{:S(2)}) async-start(f32[128,8,128]{2,1,0:T(8,128)} %get-tuple-element.132), calls=%async_computation.6 | async-start | bytes 1048576 | tf_op jit(solution)/shard_map/all_to_all | solution.py:336
  104.7 1.5 slice_bitcast_fusion.line_ref
  106.1 12.6 %reply.2 = bf16[8192,128]{1,0:T(8,128)(2,1)} custom-call(f32[128,128]{1,0:T(8,128)} %slice_bitcast_fusion.line_ref, bf16[1024,128]{1,0:T(8,128)(2,1)S(1)} %get-tuple-element.370.new_ref), custom_call_target="tpu_custom_call" | custom-call | tf_op jit(solution)/shard_map/reply/pallas_call | solution.py:290
  118.7 0.0 collective-permute-done.1
  118.7 0.0 collective-permute-done.2
  118.7 0.8 pad_maximum_fusion.1
  119.5 0.0 all-to-all-done.6
  119.6 1.0 copy.42
  120.5 1.2 collective-permute-start
  121.8 8.8 %all-to-all-start.7 = ((bf16[128,64,128]{2,1,0:T(8,128)(2,1)}), bf16[128,64,128]{2,1,0:T(8,128)(2,1)S(1)}, u32[]{:S(2)}, u32[]{:S(2)}) async-start(bf16[128,64,128]{2,1,0:T(8,128)(2,1)} %bitcast.69), calls=%async_computation.7 | async-start | bytes 4194304 | tf_op jit(solution)/shard_map/all_to_all | solution.py:336
  130.6 17.2 %while.31 = (s32[]{:T(128)}, bf16[4,512,128]{2,1,0:T(8,128)(2,1)}, s32[4]{0:T(128)S(1)}, s32[2048]{0:T(1024)S(1)}, bf16[2048,128]{1,0:T(8,128)(2,1)}, /*index=5*/bf16[4,512,128]{2,1,0:T(8,128)(2,1)}, s32[]{:T(128)}) while((s32[]{:T(128)}, bf16[4,512,128]{2,1,0:T(8,128)(2,1)}, s32[4]{0:T(128)S(1)}, s32[2048]{0:T(1024)S(1)}, ...), condition=%wide.region_6.7_spmd, body=%wide.region_4.6_spmd.sunk | while | flops 273809920 | bytes 814685 | solution.py:354
  130.6 0.6 dynamic_slice.22
  131.2 0.6 iota_add_fusion.2
  131.8 0.5 convert_reduce_fusion.2
  132.4 2.5 %fusion.28 = bf16[4,512,128]{2,1,0:T(8,128)(2,1)} fusion(bf16[4,512,128]{2,1,0:T(8,128)(2,1)} %get-tuple-element.351, s32[]{:T(128)} %get-tuple-element.350, bf16[2048,128]{1,0:T(8,128)(2,1)} %get-tuple-element.361, s32[2048]{0:T(1024)S(1)} %get-tuple-element.360, s32[512]{0:T(512)S(1)} %iota_add_fusion.2, ...), kind=kOutput, calls=%fused_computation.9.clone.1 | convolution fusion | flops 269615104 | bytes 797696 | tf_op jit(solution)/shard_map/while/body/eval_jaxpr/dot_general | solution.py:350
  134.9 0.6 dynamic_slice.22
  135.5 0.6 iota_add_fusion.2
  136.1 0.5 convert_reduce_fusion.2
  136.7 2.5 %fusion.28 = bf16[4,512,128]{2,1,0:T(8,128)(2,1)} fusion(bf16[4,512,128]{2,1,0:T(8,128)(2,1)} %get-tuple-element.351, s32[]{:T(128)} %get-tuple-element.350, bf16[2048,128]{1,0:T(8,128)(2,1)} %get-tuple-element.361, s32[2048]{0:T(1024)S(1)} %get-tuple-element.360, s32[512]{0:T(512)S(1)} %iota_add_fusion.2, ...), kind=kOutput, calls=%fused_computation.9.clone.1 | convolution fusion | flops 269615104 | bytes 797696 | tf_op jit(solution)/shard_map/while/body/eval_jaxpr/dot_general | solution.py:350
  139.2 0.6 dynamic_slice.22
  139.8 0.6 iota_add_fusion.2
  140.4 0.5 convert_reduce_fusion.2
  141.0 2.5 %fusion.28 = bf16[4,512,128]{2,1,0:T(8,128)(2,1)} fusion(bf16[4,512,128]{2,1,0:T(8,128)(2,1)} %get-tuple-element.351, s32[]{:T(128)} %get-tuple-element.350, bf16[2048,128]{1,0:T(8,128)(2,1)} %get-tuple-element.361, s32[2048]{0:T(1024)S(1)} %get-tuple-element.360, s32[512]{0:T(512)S(1)} %iota_add_fusion.2, ...), kind=kOutput, calls=%fused_computation.9.clone.1 | convolution fusion | flops 269615104 | bytes 797696 | tf_op jit(solution)/shard_map/while/body/eval_jaxpr/dot_general | solution.py:350
  143.5 0.6 dynamic_slice.22
  144.1 0.6 iota_add_fusion.2
  144.7 0.5 convert_reduce_fusion.2
  145.3 2.5 %fusion.28 = bf16[4,512,128]{2,1,0:T(8,128)(2,1)} fusion(bf16[4,512,128]{2,1,0:T(8,128)(2,1)} %get-tuple-element.351, s32[]{:T(128)} %get-tuple-element.350, bf16[2048,128]{1,0:T(8,128)(2,1)} %get-tuple-element.361, s32[2048]{0:T(1024)S(1)} %get-tuple-element.360, s32[512]{0:T(512)S(1)} %iota_add_fusion.2, ...), kind=kOutput, calls=%fused_computation.9.clone.1 | convolution fusion | flops 269615104 | bytes 797696 | tf_op jit(solution)/shard_map/while/body/eval_jaxpr/dot_general | solution.py:350
  147.8 0.0 collective-permute-done
  147.8 1.8 %maximum_select_fusion = f32[2048,128]{1,0:T(8,128)S(1)} fusion(f32[1024,128]{1,0:T(8,128)} %collective-permute-done, f32[1024,128]{1,0:T(8,128)} %bitcast.25, pred[]{:T(512)S(6)} %eq.23), kind=kLoop, calls=%fused_computation.15 | loop fusion | flops 786432 | bytes 2097153 | tf_op jit(solution)/shard_map/jit(_where)/select_n | solution.py:433
  149.6 0.3 fusion.16
  149.9 0.6 select_reduce_fusion
  150.5 0.6 sqrt_add_fusion
  151.2 1.7 subtract_select_fusion
  152.8 7.9 %all-to-all-done.7.rows_ref = bf16[128,64,128]{2,1,0:T(8,128)(2,1)S(1)} async-done(((bf16[128,64,128]{2,1,0:T(8,128)(2,1)}), bf16[128,64,128]{2,1,0:T(8,128)(2,1)S(1)}, u32[]{:S(2)}, u32[]{:S(2)}) %all-to-all-start.7) | async-done | bytes 2097184 | tf_op jit(solution)/shard_map/all_to_all | solution.py:336
  160.7 1.3 copy-done.4
  162.0 7.4 %score.1 = f32[1,128]{1,0:T(1,128)} custom-call(f32[128,128]{1,0:T(8,128)} %get-tuple-element.136.keys_ref, bf16[128,64,128]{2,1,0:T(8,128)(2,1)} %copy-done.4, f32[512,128]{1,0:T(8,128)S(1)} %get-tuple-element.139.start_ref, bf16[512,1024]{1,0:T(8,128)(2,1)} %first_ref.1, bf16[1024,1024]{1,0:T(8,128)(2,1)} %second_ref.1, bf16[1,1024]{1,0:T(2,128)(2,1)} %reshape.105.score_ref), custom_call_target="tpu_custom_call" | custom-call | tf_op jit(solution)/shard_map/score/pallas_call | solution.py:322
  (31 shorter events, 0.3 us)
Async XLA Ops:
  1.9 0.8 copy-start.9
  1.9 0.9 copy-start.7
  1.9 1.1 copy-start.8
  2.0 1.1 copy-start.10
  2.0 1.1 copy-start.2
  12.6 35.9 %all-to-all-start.4 = ((f32[128,24,128]{2,1,0:T(8,128)}), f32[128,24,128]{2,1,0:T(8,128)S(1)}, u32[]{:S(2)}, u32[]{:S(2)}) async-start(f32[128,24,128]{2,1,0:T(8,128)} %pad_maximum_fusion), calls=%async_computation.4 | async-start | bytes 3145728 | tf_op jit(solution)/shard_map/all_to_all | solution.py:336
  48.4 37.3 %copy-start.3 = (f32[128,24,128]{2,1,0:T(8,128)}, f32[128,24,128]{2,1,0:T(8,128)S(1)}, u32[]{:S(2)}) copy-start(f32[128,24,128]{2,1,0:T(8,128)S(1)} %all-to-all-done.4.state_ref) | copy-start | bytes 4718596
  48.4 6.1 %copy-start.11 = (bf16[1024]{0:T(1024)(128)(2,1)S(1)}, bf16[1024]{0:T(1024)(128)(2,1)}, u32[]{:S(2)}) copy-start(bf16[1024]{0:T(1024)(128)(2,1)} %param.29) | copy-start | bytes 6148
  48.4 35.9 %all-to-all-start.5 = ((bf16[128,64,128]{2,1,0:T(8,128)(2,1)}), bf16[128,64,128]{2,1,0:T(8,128)(2,1)}, u32[]{:S(2)}, u32[]{:S(2)}) async-start(bf16[128,64,128]{2,1,0:T(8,128)(2,1)} %bitcast.70), calls=%async_computation.5 | async-start | bytes 4194304 | tf_op jit(solution)/shard_map/all_to_all | solution.py:336
  98.4 20.3 %collective-permute-start.2 = (bf16[1024,128]{1,0:T(8,128)(2,1)S(1)}, bf16[1024,128]{1,0:T(8,128)(2,1)S(1)}, u32[]{:S(2)}, u32[]{:S(2)}) collective-permute-start(bf16[1024,128]{1,0:T(8,128)(2,1)S(1)} %get-tuple-element.370.new_ref), channel_id=1, source_target_pairs={{0,1},{1,0},{2,3},{3,2},{4,5},{5,4},{6,7},{7,6},{8,9},{9,8},{10,11... | collective-permute-start | bytes 786440 | tf_op jit(solution)/shard_map/ppermute | solution.py:420
  100.6 18.1 %collective-permute-start.1 = (s32[1024]{0:T(1024)S(1)}, s32[1024]{0:T(1024)S(1)}, u32[]{:S(2)}, u32[]{:S(2)}) collective-permute-start(s32[1024]{0:T(1024)S(1)} %convert_element_type.24), channel_id=1, source_target_pairs={{0,1},{1,0},{2,3},{3,2},{4,5},{5,4},{6,7},{7,6},{8,9},{9,8},{10,11... | collective-permute-start | bytes 12296 | tf_op jit(solution)/shard_map/ppermute | solution.py:422
  100.7 18.8 %all-to-all-start.6 = ((f32[128,8,128]{2,1,0:T(8,128)}), f32[128,8,128]{2,1,0:T(8,128)S(1)}, u32[]{:S(2)}, u32[]{:S(2)}) async-start(f32[128,8,128]{2,1,0:T(8,128)} %get-tuple-element.132), calls=%async_computation.6 | async-start | bytes 1048576 | tf_op jit(solution)/shard_map/all_to_all | solution.py:336
  120.5 27.2 %collective-permute-start = (f32[1024,128]{1,0:T(8,128)}, f32[1024,128]{1,0:T(8,128)}, u32[]{:S(2)}, u32[]{:S(2)}) collective-permute-start(f32[1024,128]{1,0:T(8,128)} %bitcast.25), channel_id=1, source_target_pairs={{0,1},{1,0},{2,3},{3,2},{4,5},{5,4},{6,7},{7,6},{8,9},{9,8},{10,11... | collective-permute-start | bytes 1572872 | tf_op jit(solution)/shard_map/ppermute | solution.py:432
  121.8 38.9 %all-to-all-start.7 = ((bf16[128,64,128]{2,1,0:T(8,128)(2,1)}), bf16[128,64,128]{2,1,0:T(8,128)(2,1)S(1)}, u32[]{:S(2)}, u32[]{:S(2)}) async-start(bf16[128,64,128]{2,1,0:T(8,128)(2,1)} %bitcast.69), calls=%async_computation.7 | async-start | bytes 4194304 | tf_op jit(solution)/shard_map/all_to_all | solution.py:336
  147.8 3.4 %copy-start.5 = (f32[2048,128]{1,0:T(8,128)S(1)}, f32[2048,128]{1,0:T(8,128)}, u32[]{:S(2)}) copy-start(f32[2048,128]{1,0:T(8,128)} %param.23) | copy-start | bytes 3145732
  147.8 3.4 %copy-start.6 = (f32[2048,128]{1,0:T(8,128)S(1)}, f32[2048,128]{1,0:T(8,128)}, u32[]{:S(2)}) copy-start(f32[2048,128]{1,0:T(8,128)} %param.24) | copy-start | bytes 3145732
  160.7 1.3 copy-start.4

commit v2 on v1

--- a/solution.py
+++ b/solution.py
@@ -20,6 +20,7 @@
 BF16 = jnp.bfloat16
 I32 = jnp.int32
 ALL = ("shard", "rep")
+SENT = ROUND + 32
 
 
 def iota(shape, dim):
@@ -85,12 +86,17 @@
         slot = jnp.where(fits, dest * ROUND + rank, DEVS * ROUND)
         for u in range(step):
             slots_ref[t + u : t + u + 1, :] = slot[:, u * samples : (u + 1) * samples]
-    layout = layout[:, :LANES] * 32.0 + layout[:, LANES:] - 1.0
-    keys_ref[...] = layout
-    most = jnp.max(seen, axis=0, keepdims=True)
-    line = jnp.where(iota((DEVS, LANES), 1) < ROUND, layout, extra_ref[...])
-    row_ref[:, 0:1, :] = line.reshape(DEVS, 1, LANES)
-    row_ref[:, 1:8, :] = jnp.broadcast_to(most.reshape(1, 1, 1), (DEVS, 7, LANES))
+    keys_ref[...] = layout[:, :LANES] * 32.0 + layout[:, LANES:] - 1.0
+    most = jnp.max(seen, axis=0, keepdims=True).astype(I32)
+    rounds = ((most + ROUND - 1) // ROUND).astype(F32)
+    extra = extra_ref[...]
+    coarse = extra.astype(BF16).astype(F32)
+    index = iota((DEVS, LANES), 1) < ROUND
+    high = jnp.where(index, layout[:, :LANES], coarse)
+    low = jnp.where(index, layout[:, LANES:], extra - coarse)
+    row_ref[:, 0:1, :] = high.reshape(DEVS, 1, LANES)
+    row_ref[:, 1:2, :] = low.reshape(DEVS, 1, LANES)
+    row_ref[:, 2:8, :] = jnp.broadcast_to(rounds.reshape(1, 1, 1), (DEVS, 6, LANES))
 
 
 def route(round_index, ids, train_map, extra):
@@ -109,18 +115,15 @@
     )(round_index, ids, train_map, extra)
 
 
-def pack_kernel(slots_ref, grads_ref, out_ref, from_ref, to_ref):
+def pack_kernel(slots_ref, grads_ref, table_ref, moment_ref, head_ref, out_ref, from_ref, to_ref):
     bag, samples = slots_ref.shape
     block = 512
 
     def widen(i, carry):
         at = pl.multiple_of(i * block, block)
         from_ref[pl.ds(at, block), :] = grads_ref[pl.ds(at, block), :].astype(F32)
-        return carry
-
-    def clear(i, carry):
-        at = pl.multiple_of(i * block, block)
-        to_ref[pl.ds(at, block), :] = jnp.zeros((block, LANES), F32)
+        to_ref[pl.ds(at * 2, block), :] = jnp.zeros((block, LANES), F32)
+        to_ref[pl.ds(at * 2 + block, block), :] = jnp.zeros((block, LANES), F32)
         return carry
 
     def move(b, carry):
@@ -129,31 +132,35 @@
         return carry
 
     def narrow(i, carry):
-        at = pl.multiple_of(i * block, block)
-        out_ref[pl.ds(at, block), :] = to_ref[pl.ds(at, block), :].astype(BF16)
+        at = pl.multiple_of(i * 8, 8)
+        rows = to_ref[pl.ds(pl.multiple_of(i * block, block), block), :].astype(BF16)
+        table = table_ref[pl.ds(at, 8)]
+        coarse = table.astype(BF16).astype(F32)
+        state = jnp.concatenate([coarse, table - coarse], axis=1).astype(BF16)
+        more = jnp.concatenate([moment_ref[pl.ds(at, 8)], head_ref[pl.ds(at, 8)]], axis=1)
+        out_ref[pl.ds(at, 8), 0:ROUND, :] = rows.reshape(8, ROUND, LANES)
+        out_ref[pl.ds(at, 8), ROUND : ROUND + 16, :] = state
+        out_ref[pl.ds(at, 8), ROUND + 16 : ROUND + 32, :] = more.astype(BF16)
         return carry
 
     lax.fori_loop(0, bag * samples // block, widen, 0)
-    lax.fori_loop(0, DEVS * ROUND // block, clear, 0)
     lax.fori_loop(0, samples, move, 0)
-    lax.fori_loop(0, DEVS * ROUND // block, narrow, 0)
-
-
-def pack(slots, grads):
+    lax.fori_loop(0, DEVS // 8, narrow, 0)
+
+
+def pack(slots, grads, table, moment, head):
     return pl.pallas_call(
         pack_kernel,
-        in_specs=[
-            pl.BlockSpec(memory_space=pltpu.SMEM),
-            pl.BlockSpec(memory_space=pltpu.VMEM),
-        ],
+        in_specs=[pl.BlockSpec(memory_space=pltpu.SMEM)]
+        + [pl.BlockSpec(memory_space=pltpu.VMEM)] * 4,
         out_specs=pl.BlockSpec(memory_space=pltpu.VMEM),
-        out_shape=jax.ShapeDtypeStruct((DEVS * ROUND, LANES), BF16),
+        out_shape=jax.ShapeDtypeStruct((DEVS, SENT, LANES), BF16),
         scratch_shapes=[
             pltpu.VMEM(grads.shape, F32),
             pltpu.VMEM((DEVS * ROUND + 8, LANES), F32),
         ],
         name="pack",
-    )(slots, grads)
+    )(slots, grads, table, moment, head)
 
 
 def pair_up(line, low):
@@ -161,80 +168,72 @@
     half = DEVS // 2
     left = (line if low else other)[:half]
     right = (other if low else line)[half:]
-    return jnp.where(iota((half, LANES), 1) < ROUND, left, right)
-
-
-def pair_rows(ref, i):
-    half = DEVS // 2
-    left = ref[pl.ds(i * 8, 8)]
-    right = ref[pl.ds(half + i * 8, 8)]
-    pieces = []
-    for u in range(8):
-        pieces += [left[u], right[u]]
-    return jnp.concatenate(pieces, axis=0)
-
-
-def lanes_of(index_ref, i):
-    rows = index_ref[pl.ds(pl.multiple_of(i * 8, 8), 8), :]
-    return jnp.concatenate([rows[u : u + 1] for u in range(8)], axis=1)
-
-
-def add_rows(index_ref, rows_ref, acc_ref, with_count):
+    return jnp.where(iota((half, LANES), 1) < ROUND, left, right).astype(I32)
+
+
+def add_rows(index_ref, left_ref, right_ref, acc_ref, with_count):
     width = 8 * LANES
+    step = pl.program_id(0)
+    turns = left_ref.shape[0] // 8
 
     def add(i, carry):
-        hit = one_hot(iota((acc_ref.shape[0], width), 0) == lanes_of(index_ref, i))
-        rows = pair_rows(rows_ref, i)
+        at = pl.ds(pl.multiple_of(i * 8, 8), 8)
+        pieces = pl.ds(pl.multiple_of((step * turns + i) * 8, 8), 8)
+        index = index_ref[pieces, :]
+        index = jnp.concatenate([index[u : u + 1] for u in range(8)], axis=1)
+        left, right = left_ref[at], right_ref[at]
+        rows = jnp.concatenate([p[u] for u in range(8) for p in (left, right)], axis=0)
         if with_count:
             rows = jnp.concatenate([rows, jnp.ones_like(rows)], axis=1)
+        hit = one_hot(iota((acc_ref.shape[0], width), 0) == index)
         acc_ref[...] = acc_ref[...] + jnp.dot(hit, rows, preferred_element_type=F32)
         return carry
 
-    lax.fori_loop(0, DEVS * ROUND // width, add, 0)
-
-
-def sum_kernel(line_ref, rows_ref, start_ref, out_ref, index_ref, *, low, with_count):
-    index_ref[...] = pair_up(line_ref[...], low).astype(I32)
-    out_ref[...] = start_ref[...]
-    add_rows(index_ref, rows_ref, out_ref, with_count)
-
-
-def sum_rows(line, rows, start, low, with_count):
-    return pl.pallas_call(
-        functools.partial(sum_kernel, low=low, with_count=with_count),
-        in_specs=[pl.BlockSpec(memory_space=pltpu.VMEM)] * 3,
-        out_specs=pl.BlockSpec(memory_space=pltpu.VMEM),
-        out_shape=jax.ShapeDtypeStruct(start.shape, F32),
-        scratch_shapes=[pltpu.VMEM((DEVS // 2, LANES), I32)],
-        name="sum_rows",
-    )(line, rows, start)
-
-
-def update_kernel(
-    core_ref, state_ref, rows_ref, start_ref, new_ref, sums_ref, spots_ref, index_ref, acc_ref
-):
-    index_ref[...] = pair_up(state_ref[:, 16:17, :].reshape(DEVS, LANES), True).astype(I32)
-    acc_ref[...] = start_ref[...]
-    add_rows(index_ref, rows_ref, acc_ref, True)
-    core = core_ref[0]
-
+    lax.fori_loop(0, turns, add, 0)
+
+
+STEPS = 4
+
+
+def half_spec(second):
+    count = DEVS // 2 // STEPS
+    return pl.BlockSpec((count, ROUND, LANES), lambda i: (i + second * STEPS, 0, 0))
+
+
+def whole(shape, at=None):
+    place = at if at is not None else (0,) * len(shape)
+    return pl.BlockSpec(shape, lambda i: place)
+
+
+STATE_SPEC = whole((DEVS, 32, LANES), (0, ROUND // 32, 0))
+
+
+def line_of(state_ref):
+    high = state_ref[:, 24:25, :].astype(F32).reshape(DEVS, LANES)
+    low = state_ref[:, 25:26, :].astype(F32).reshape(DEVS, LANES)
+    return high * 32.0 + low - 1.0
+
+
+def adam(core, state_ref, acc_ref, new_ref, sums_ref, spots_ref):
     def step(i, carry):
         at = pl.multiple_of(i * LANES, LANES)
         part = pl.ds(i * 16, 16)
         total = acc_ref[pl.ds(at, LANES), :]
-        grad = total[:, :LANES].reshape(16, 8, LANES)
-        touched = (total[:, LANES:] > 0.5).reshape(16, 8, LANES)
         shape = (16, 8, LANES)
+        grad = total[:, :LANES].reshape(shape)
+        touched = (total[:, LANES:] > 0.5).reshape(shape)
+        state = state_ref[part].astype(F32)
+        table = state[:, 0:8, :] + state[:, 8:16, :]
+        moment = state[:, 16:24, :]
         source = iota(shape, 0)
         within = iota(shape, 1)
         lane = iota(shape, 2)
         parity = (core + i * 8 + (source >> 1)) & 1
         own = (source & 1) * 16 + within * 2 + parity
-        extra = jnp.broadcast_to(state_ref[part, 16:17, :], shape)
+        high = jnp.broadcast_to(state[:, 24:25, :], shape)
+        extra = high + jnp.broadcast_to(state[:, 25:26, :], shape)
         var = jnp.sum(jnp.where(lane == ROUND + own, extra, 0.0), axis=2, keepdims=True)
         spot = jnp.sum(jnp.where(lane == ROUND + 32 + own, extra, 0.0), axis=2, keepdims=True)
-        table = state_ref[part, 0:8, :]
-        moment = state_ref[part, 8:16, :]
         mean = jnp.sum(grad * grad, axis=2, keepdims=True) * (1.0 / LANES)
         new_var = beta_two * var + (1.0 - beta_two) * mean
         new_moment = beta_one * moment + (1.0 - beta_one) * grad
@@ -250,37 +249,127 @@
     lax.fori_loop(0, 8, step, 0)
 
 
-def update(core, state, rows, start):
+def update_kernel(
+    core_ref,
+    state_ref,
+    left_ref,
+    right_ref,
+    new_ref,
+    sums_ref,
+    spots_ref,
+    acc_ref,
+    line_ref,
+    rounds_ref,
+    index_ref,
+):
+    @pl.when(pl.program_id(0) == 0)
+    def _():
+        line = line_of(state_ref)
+        line_ref[...] = line
+        index_ref[...] = pair_up(line, True)
+        rounds = state_ref[:, 26:27, :].astype(F32).reshape(DEVS, LANES)
+        rounds_ref[0] = jnp.max(rounds).astype(I32)
+        acc_ref[...] = jnp.zeros(acc_ref.shape, F32)
+
+    add_rows(index_ref, left_ref, right_ref, acc_ref, True)
+
+    @pl.when(pl.program_id(0) == STEPS - 1)
+    def _():
+        adam(core_ref[0], state_ref, acc_ref, new_ref, sums_ref, spots_ref)
+
+
+def updated_shapes(rows):
+    return (
+        jax.ShapeDtypeStruct((rows, LANES), BF16),
+        jax.ShapeDtypeStruct((DEVS, 8, LANES), F32),
+        jax.ShapeDtypeStruct((DEVS, LANES), F32),
+    )
+
+
+def updated_specs(rows):
+    return [whole((rows, LANES)), whole((DEVS, 8, LANES)), whole((DEVS, LANES))]
+
+
+def update(core, received, rows):
     return pl.pallas_call(
         update_kernel,
-        in_specs=[pl.BlockSpec(memory_space=pltpu.SMEM)]
-        + [pl.BlockSpec(memory_space=pltpu.VMEM)] * 3,
-        out_specs=[pl.BlockSpec(memory_space=pltpu.VMEM)] * 3,
-        out_shape=(
-            jax.ShapeDtypeStruct((start.shape[0], LANES), BF16),
-            jax.ShapeDtypeStruct((DEVS, 8, LANES), F32),
+        grid=(STEPS,),
+        in_specs=[
+            pl.BlockSpec(memory_space=pltpu.SMEM),
+            STATE_SPEC,
+            half_spec(0),
+            half_spec(1),
+        ],
+        out_specs=updated_specs(rows)
+        + [
+            whole((rows, 2 * LANES)),
+            whole((DEVS, LANES)),
+            pl.BlockSpec(memory_space=pltpu.SMEM),
+        ],
+        out_shape=updated_shapes(rows)
+        + (
+            jax.ShapeDtypeStruct((rows, 2 * LANES), F32),
             jax.ShapeDtypeStruct((DEVS, LANES), F32),
+            jax.ShapeDtypeStruct((1,), I32),
         ),
-        scratch_shapes=[
-            pltpu.VMEM((DEVS // 2, LANES), I32),
-            pltpu.VMEM(start.shape, F32),
-        ],
+        scratch_shapes=[pltpu.VMEM((DEVS // 2, LANES), I32)],
         name="update",
-    )(core, state, rows, start)
-
-
-def reply_kernel(line_ref, new_ref, out_ref, turned_ref):
+    )(core, received, received, received)
+
+
+def adam_kernel(core_ref, state_ref, acc_ref, new_ref, sums_ref, spots_ref):
+    adam(core_ref[0], state_ref, acc_ref, new_ref, sums_ref, spots_ref)
+
+
+def adam_again(core, received, acc):
+    rows = acc.shape[0]
+    return pl.pallas_call(
+        adam_kernel,
+        grid=(1,),
+        in_specs=[pl.BlockSpec(memory_space=pltpu.SMEM), STATE_SPEC, whole(acc.shape)],
+        out_specs=updated_specs(rows),
+        out_shape=updated_shapes(rows),
+        name="adam",
+    )(core, received, acc)
+
+
+def more_kernel(line_ref, left_ref, right_ref, start_ref, out_ref, index_ref, *, low, with_count):
+    @pl.when(pl.program_id(0) == 0)
+    def _():
+        index_ref[...] = pair_up(line_ref[...], low)
+        out_ref[...] = start_ref[...]
+
+    add_rows(index_ref, left_ref, right_ref, out_ref, with_count)
+
+
+def more_rows(line, rows, start, low, with_count):
+    return pl.pallas_call(
+        functools.partial(more_kernel, low=low, with_count=with_count),
+        grid=(STEPS,),
+        in_specs=[whole(line.shape), half_spec(0), half_spec(1), whole(start.shape)],
+        out_specs=whole(start.shape),
+        out_shape=jax.ShapeDtypeStruct(start.shape, F32),
+        scratch_shapes=[pltpu.VMEM((DEVS // 2, LANES), I32)],
+        name="more_rows",
+    )(line, rows, rows, start)
+
+
+def reply_kernel(line_ref, new_ref, out_ref, turned_ref, table_ref):
     turned_ref[...] = line_ref[...].T
-    rows = new_ref.shape[0]
+    half = new_ref.shape[0] // 2
+    table_ref[...] = jnp.concatenate([new_ref[0:half, :], new_ref[half:, :]], axis=1)
 
     def look(i, carry):
         turned = pltpu.roll(turned_ref[0:ROUND, :], LANES - i * 8, 1).astype(I32)
+        within = turned & (half - 1)
         hit = jnp.concatenate(
-            [one_hot(iota((ROUND, rows), 1) == turned[:, u : u + 1]) for u in range(8)], axis=0
+            [one_hot(iota((ROUND, half), 1) == within[:, u : u + 1]) for u in range(8)], axis=0
         )
-        found = jnp.dot(hit, new_ref[...], preferred_element_type=F32)
-        at = pl.multiple_of(i * 8 * ROUND, 8 * ROUND)
-        out_ref[pl.ds(at, 8 * ROUND), :] = found.astype(BF16)
+        found = jnp.dot(hit, table_ref[...], preferred_element_type=F32)
+        for u in range(8):
+            piece = found[u * ROUND : (u + 1) * ROUND]
+            piece = jnp.where(turned[:, u : u + 1] < half, piece[:, :LANES], piece[:, LANES:])
+            out_ref[i * 8 + u] = piece.astype(BF16)
         return carry
 
     lax.fori_loop(0, DEVS // 8, look, 0)
@@ -291,50 +380,70 @@
         reply_kernel,
         in_specs=[pl.BlockSpec(memory_space=pltpu.VMEM)] * 2,
         out_specs=pl.BlockSpec(memory_space=pltpu.VMEM),
-        out_shape=jax.ShapeDtypeStruct((DEVS * ROUND, LANES), BF16),
-        scratch_shapes=[pltpu.VMEM((DEVS, LANES), F32)],
+        out_shape=jax.ShapeDtypeStruct((DEVS, ROUND, LANES), BF16),
+        scratch_shapes=[
+            pltpu.VMEM((DEVS, LANES), F32),
+            pltpu.VMEM((new_rows.shape[0] // 2, 2 * LANES), BF16),
+        ],
         name="reply",
     )(line, new_rows)
 
 
 def score_kernel(
-    keys_ref, rows_ref, start_ref, first_ref, second_ref, score_ref, out_ref, index_ref, acc_ref
+    keys_ref,
+    left_ref,
+    right_ref,
+    start_ref,
+    first_ref,
+    second_ref,
+    score_ref,
+    out_ref,
+    index_ref,
+    acc_ref,
 ):
-    index_ref[...] = pair_up(keys_ref[...], False).astype(I32)
-    acc_ref[...] = start_ref[...]
-    add_rows(index_ref, rows_ref, acc_ref, False)
-    samples = out_ref.shape[1]
-    pooled = jnp.concatenate(
-        [acc_ref[f * samples : (f + 1) * samples, :] for f in range(4)], axis=1
-    ).astype(BF16)
-    hidden = jnp.dot(pooled, first_ref[...], preferred_element_type=F32)
-    hidden = jnp.maximum(hidden, 0.0).astype(BF16)
-    hidden = jnp.dot(hidden, second_ref[...], preferred_element_type=F32)
-    hidden = jnp.maximum(hidden, 0.0).astype(BF16)
-    weights = jnp.broadcast_to(score_ref[...], (16, score_ref.shape[1]))
-    scores = lax.dot_general(
-        weights, hidden, (((1,), (1,)), ((), ())), preferred_element_type=F32
-    )
-    out_ref[...] = scores[0:1, :]
+    @pl.when(pl.program_id(0) == 0)
+    def _():
+        index_ref[...] = pair_up(keys_ref[...], False)
+        acc_ref[...] = start_ref[...]
+
+    add_rows(index_ref, left_ref, right_ref, acc_ref, False)
+
+    @pl.when(pl.program_id(0) == STEPS - 1)
+    def _():
+        samples = out_ref.shape[1]
+        pooled = jnp.concatenate(
+            [acc_ref[f * samples : (f + 1) * samples, :] for f in range(4)], axis=1
+        ).astype(BF16)
+        hidden = jnp.dot(pooled, first_ref[...], preferred_element_type=F32)
+        hidden = jnp.maximum(hidden, 0.0).astype(BF16)
+        hidden = jnp.dot(hidden, second_ref[...], preferred_element_type=F32)
+        hidden = jnp.maximum(hidden, 0.0).astype(BF16)
+        weights = jnp.broadcast_to(score_ref[...], (16, score_ref.shape[1]))
+        scores = lax.dot_general(
+            weights, hidden, (((1,), (1,)), ((), ())), preferred_element_type=F32
+        )
+        out_ref[...] = scores[0:1, :]
 
 
 def score(keys, rows, start, w_first, w_second, w_score):
+    samples = start.shape[0] // 4
     return pl.pallas_call(
         score_kernel,
-        in_specs=[pl.BlockSpec(memory_space=pltpu.VMEM)] * 6,
-        out_specs=pl.BlockSpec(memory_space=pltpu.VMEM),
-        out_shape=jax.ShapeDtypeStruct((1, start.shape[0] // 4), F32),
+        grid=(STEPS,),
+        in_specs=[whole(keys.shape), half_spec(0), half_spec(1), whole(start.shape)]
+        + [whole(w.shape) for w in (w_first, w_second, w_score)],
+        out_specs=whole((1, samples)),
+        out_shape=jax.ShapeDtypeStruct((1, samples), F32),
         scratch_shapes=[
             pltpu.VMEM((DEVS // 2, LANES), I32),
             pltpu.VMEM(start.shape, F32),
         ],
         name="score",
-    )(keys, rows, start, w_first, w_second, w_score)
-
-
-def exchange(value, width):
-    out = lax.all_to_all(value.reshape(DEVS, -1, width), ALL, 0, 0, tiled=True)
-    return out
+    )(keys, rows, rows, start, w_first, w_second, w_score)
+
+
+def exchange(value):
+    return lax.all_to_all(value, ALL, 0, 0, tiled=True)
 
 
 def place_rows(serving_old, slot_index, rows_in):
@@ -392,30 +501,28 @@
     spread = jnp.broadcast_to(spread[:, None, :], (owners, 2, 2 * tab_rows // owners))
     extra = jnp.concatenate([jnp.zeros((DEVS, ROUND), F32), spread.reshape(DEVS, -1)], axis=1)
 
+    table_out, moment_out = outgoing(table), outgoing(moment)
     slots, keys, head = route(jnp.zeros((1,), I32), ids, map_rows, extra)
-    state = jnp.concatenate([outgoing(table), outgoing(moment), head], axis=1)
-    state = exchange(state, row_width)
-    received = exchange(pack(slots, grads), row_width)
-    state, received = lax.optimization_barrier((state, received))
-    rounds = (jnp.max(state[:, 17, 0]).astype(I32) + ROUND - 1) // ROUND
+    received = exchange(pack(slots, grads, table_out, moment_out, head))
+    core = rep.reshape(1).astype(I32)
+    new_rows, sums, places, acc, line, rounds = update(core, received, rows_here)
+    rounds = rounds[0]
+    one = jnp.ones((), I32)
 
     def more_sums(carry):
-        k, acc = carry
+        k, acc = carry[0], carry[1]
         slots, _, head = route(k.reshape(1), ids, map_rows, extra)
-        line = exchange(head, row_width)[:, 0, :]
-        got = exchange(pack(slots, grads), row_width)
-        return (k + 1, sum_rows(line, got, acc, True, True))
-
-    one = jnp.ones((), I32)
-    _, start = lax.while_loop(
-        lambda c: c[0] < rounds,
-        more_sums,
-        (one, jnp.zeros((rows_here, 2 * row_width), F32)),
-    )
-    new_rows, sums, places = update(rep.reshape(1).astype(I32), state, received, start)
-
-    back = exchange(sums, row_width)
-    answer = exchange(reply(state[:, 16, :], new_rows), row_width)
+        got = exchange(pack(slots, grads, table_out, moment_out, head))
+        line = got[:, ROUND + 24].astype(F32) * 32.0 + got[:, ROUND + 25].astype(F32) - 1.0
+        acc = more_rows(line, got, acc, True, True)
+        return (k + 1, acc) + tuple(adam_again(core, received, acc))
+
+    _, _, new_rows, sums, places = lax.while_loop(
+        lambda c: c[0] < rounds, more_sums, (one, acc, new_rows, sums, places)
+    )
+
+    back = exchange(sums)
+    answer = exchange(reply(line, new_rows))
 
     other_rows = lax.ppermute(new_rows, "rep", swap)
     places = places[:, :8].reshape(-1).astype(I32)
@@ -444,9 +551,9 @@
     def more_pooled(carry):
         k, acc = carry
         _, keys, head = route(k.reshape(1), ids, map_rows, extra)
-        line = exchange(head, row_width)[:, 0, :]
-        got = exchange(reply(line, new_rows), row_width)
-        return (k + 1, sum_rows(keys, got, acc, False, False))
+        got = exchange(head)
+        line = got[:, 0] * 32.0 + got[:, 1] - 1.0
+        return (k + 1, more_rows(keys, exchange(reply(line, new_rows)), acc, False, False))
 
     answer, rounds = lax.optimization_barrier((answer, rounds))
     _, pooled = lax.while_loop(

time: 170 us -> 149 us (0.88)
  starting transfers between devices: 32.9 us -> 25.8 us
  local copies, waits for them, and re-layouts: 11.5 us -> 6.87 us
  Pallas kernels: 45.6 us -> 41.1 us
  other arithmetic: 14.7 us -> 11.4 us
  waiting for transfers between devices: 53.2 us -> 50.7 us
    all_to_all x4 -> x3, starting transfers between devices: 30.3 us -> 22.4 us  [exchange(): return lax.all_to_all(value, ALL, 0, 0, tiled=True)]
    pallas_call x1, Pallas kernels: 12.6 us -> 9.16 us  [reply(): pl.pallas_call(reply_kernel, in_specs=[pl.BlockSpec(memory_space=pltpu.VM...]
    all_to_all x4 -> x3, waiting for transfers between devices: 53.2 us -> 50.7 us  [exchange(): return lax.all_to_all(value, ALL, 0, 0, tiled=True)]
    concatenate x1 -> x0, other arithmetic: 2.32 us -> none  [per_device(): state = jnp.concatenate([outgoing(table), outgoing(moment), head], axis=1)]
  transfers between devices with their start and end apart: 7 -> 6, of which waited for: 3 -> 3; matrix products, arithmetic and copies ran while one was open for 15% -> 16% of each run, Pallas kernels for 12% -> 6%
where the time goes in v2:
time: 149 us; the launch traced here: 148 us
  waiting for transfers between devices  50.7 us (34%)
  Pallas kernels  41.1 us (28%)
  starting transfers between devices  25.8 us (17%)
  other arithmetic  11.4 us (8%)
  matrix products  9.98 us (7%)
  local copies, waits for them, and re-layouts  6.87 us (5%)
  loops' own time  1.59 us (1%)
    all_to_all x3, waiting for transfers between devices, exchange(): return lax.all_to_all(value, ALL, 0, 0, tiled=True)  50.7 us
    all_to_all x3, starting transfers between devices, exchange(): return lax.all_to_all(value, ALL, 0, 0, tiled=True)  22.4 us
    dot_general x4, matrix products, place_block(): fresh = jnp.dot(hit, rows_in, preferred_element_type=jnp.float32)  9.98 us
    pallas_call x1, Pallas kernels, reply(): pl.pallas_call(reply_kernel, in_specs=[pl.BlockSpec(memory_space=pltpu.VM...  9.16 us
    pallas_call x1, Pallas kernels, update(): pl.pallas_call(update_kernel, grid=(STEPS,), in_specs=[pl.BlockSpec(memor...  8.96 us
    pallas_call x1, Pallas kernels, pack(): pl.pallas_call(pack_kernel, in_specs=[pl.BlockSpec(memory_space=pltpu.SME...  8.54 us
    pallas_call x1, Pallas kernels, score(): pl.pallas_call(score_kernel, grid=(STEPS,), in_specs=[whole(keys.shape),...  7.26 us
    pallas_call x1, Pallas kernels, route(): pl.pallas_call(route_kernel, in_specs=[pl.BlockSpec(memory_space=pltpu.SM...  7.16 us
  transfers between devices with their start and end apart: 6, of which 3 were waited for; matrix products, arithmetic and copies ran while one was open for 16% of the time, Pallas kernels for 6%

profile of v2, /device:TPU:1, one launch (start us, length us, event | category | flops | bytes accessed | tf_op | source)
XLA Modules:
  0.0 148.3 jit_solution(14920978205586803770)
XLA Ops:
  0.6 0.0 copy-start.15
  0.7 0.0 copy-start.13
  0.7 0.0 copy-start.4
  0.7 1.3 constant_dynamic-slice_fusion
  2.0 0.0 copy-start.6
  2.1 0.3 copy.36
  2.4 0.0 copy-start.7
  2.5 0.3 copy.37
  2.8 0.1 reshape.92
  2.9 0.0 copy-done.13
  2.9 0.1 reshape.91
  3.0 0.1 copy.35
  3.1 0.1 concatenate.23.extra_ref
  3.2 7.2 %route.9 = (s32[32,128]{1,0:T(8,128)}, f32[128,128]{1,0:T(8,128)}, f32[128,8,128]{2,1,0:T(8,128)}) custom-call(s32[1]{0:T(128)} %constant.96.clone.1.round_ref, s32[36,128]{1,0:T(8,128)S(1)} %add_bitcast_fusion.1.ids_ref, s32[1024,128]{1,0:T(8,128)S(1)} %bitcast.60, f32[128,128]{1,0:T(8,128)S(1)} %concatenate.23.extra_ref), custom_call_target="tpu_custom_call" | custom-call | tf_op jit(solution)/shard_map/route/pallas_call | solution.py:104
  10.4 8.5 %pack.5 = bf16[128,96,128]{2,1,0:T(8,128)(2,1)} custom-call(s32[32,128]{1,0:T(8,128)} %get-tuple-element.303.slots_ref, bf16[4096,128]{1,0:T(8,128)(2,1)S(1)} %bitcast.62, f32[128,8,128]{2,1,0:T(8,128)S(1)} %bitcast.63, f32[128,8,128]{2,1,0:T(8,128)S(1)} %bitcast.65, f32[128,8,128]{2,1,0:T(8,128)} %get-tuple-element.304.head_ref), custom_call_target="tpu_custom_call" | custom-call | tf_op jit(solution)/shard_map/pack/pallas_call | solution.py:152
  18.9 11.5 %all-to-all-start.3 = ((bf16[128,96,128]{2,1,0:T(8,128)(2,1)}), bf16[128,96,128]{2,1,0:T(8,128)(2,1)S(1)}, u32[]{:S(2)}, u32[]{:S(2)}) async-start(bf16[128,96,128]{2,1,0:T(8,128)(2,1)} %pack.5), calls=%async_computation.3 | async-start | bytes 6291456 | tf_op jit(solution)/shard_map/all_to_all | solution.py:446
  30.4 41.7 %all-to-all-done.3.state_ref.left_ref.right_ref = bf16[128,96,128]{2,1,0:T(8,128)(2,1)S(1)} async-done(((bf16[128,96,128]{2,1,0:T(8,128)(2,1)}), bf16[128,96,128]{2,1,0:T(8,128)(2,1)S(1)}, u32[]{:S(2)}, u32[]{:S(2)}) %all-to-all-start.3) | async-done | bytes 3145760 | tf_op jit(solution)/shard_map/all_to_all | solution.py:446
  72.1 9.0 %update.1 = (bf16[1024,128]{1,0:T(8,128)(2,1)}, f32[128,8,128]{2,1,0:T(8,128)}, f32[128,128]{1,0:T(8,128)}, f32[1024,256]{1,0:T(8,128)}, f32[128,128]{1,0:T(8,128)}, /*index=5*/s32[1]{0:T(128)}) custom-call(s32[1]{0:T(128)} %bitcast.7.core_ref, bf16[128,96,128]{2,1,0:T(8,128)(2,1)S(1)} %all-to-all-done.3.state_ref.left_ref.right_ref, ...), custom_call_target="tpu_custom_call" | custom-call | tf_op jit(solution)/shard_map/update/pallas_call | solution.py:294
  81.1 0.0 copy-start.17
  81.1 0.9 while.40
  81.9 1.1 collective-permute-start.2
  83.0 3.6 %all-to-all-start.4 = ((f32[128,8,128]{2,1,0:T(8,128)}), f32[128,8,128]{2,1,0:T(8,128)S(1)}, u32[]{:S(2)}, u32[]{:S(2)}) async-start(f32[128,8,128]{2,1,0:T(8,128)} %get-tuple-element.310), calls=%async_computation.4 | async-start | bytes 1048576 | tf_op jit(solution)/shard_map/all_to_all | solution.py:446
  86.6 0.8 slice_convert_fusion.2
  87.5 0.1 convert_element_type.34
  87.5 1.2 collective-permute-start.1
  88.7 0.0 copy-done.17
  88.7 0.6 reshape.103.score_ref
  89.3 9.2 %reply.5 = bf16[128,64,128]{2,1,0:T(8,128)(2,1)} custom-call(f32[128,128]{1,0:T(8,128)} %get-tuple-element.315.line_ref, bf16[1024,128]{1,0:T(8,128)(2,1)} %get-tuple-element.632.new_ref), custom_call_target="tpu_custom_call" | custom-call | tf_op jit(solution)/shard_map/reply/pallas_call | solution.py:379
  98.5 0.0 collective-permute-done.1
  98.5 0.0 collective-permute-done.2
  98.5 0.8 pad_maximum_fusion
  99.3 0.9 all-to-all-done.4
  100.2 0.2 copy.38
  100.4 1.1 collective-permute-start
  101.5 7.4 %all-to-all-start.5 = ((bf16[128,64,128]{2,1,0:T(8,128)(2,1)}), bf16[128,64,128]{2,1,0:T(8,128)(2,1)S(1)}, u32[]{:S(2)}, u32[]{:S(2)}) async-start(bf16[128,64,128]{2,1,0:T(8,128)(2,1)} %reply.5), calls=%async_computation.5 | async-start | bytes 4194304 | tf_op jit(solution)/shard_map/all_to_all | solution.py:446
  108.9 17.2 %while.41 = (s32[]{:T(128)}, bf16[4,512,128]{2,1,0:T(8,128)(2,1)}, s32[4]{0:T(128)S(1)}, s32[2048]{0:T(1024)S(1)}, bf16[2048,128]{1,0:T(8,128)(2,1)}, /*index=5*/bf16[4,512,128]{2,1,0:T(8,128)(2,1)}, s32[]{:T(128)}) while((s32[]{:T(128)}, bf16[4,512,128]{2,1,0:T(8,128)(2,1)}, s32[4]{0:T(128)S(1)}, s32[2048]{0:T(1024)S(1)}, ...), condition=%wide.region_5.6_spmd, body=%wide.region_3.5_spmd.sunk | while | flops 273809920 | bytes 814685 | solution.py:463
  108.9 0.6 dynamic_slice.22
  109.5 0.6 iota_add_fusion.2
  110.1 0.5 convert_reduce_fusion.2
  110.7 2.5 %fusion.34 = bf16[4,512,128]{2,1,0:T(8,128)(2,1)} fusion(bf16[4,512,128]{2,1,0:T(8,128)(2,1)} %get-tuple-element.613, s32[]{:T(128)} %get-tuple-element.612, bf16[2048,128]{1,0:T(8,128)(2,1)} %get-tuple-element.623, s32[2048]{0:T(1024)S(1)} %get-tuple-element.622, s32[512]{0:T(512)S(1)} %iota_add_fusion.2, ...), kind=kOutput, calls=%fused_computation.14.clone.1 | convolution fusion | flops 269615104 | bytes 797696 | tf_op jit(solution)/shard_map/while/body/eval_jaxpr/dot_general | solution.py:459
  113.2 0.6 dynamic_slice.22
  113.8 0.6 iota_add_fusion.2
  114.4 0.5 convert_reduce_fusion.2
  115.0 2.5 %fusion.34 = bf16[4,512,128]{2,1,0:T(8,128)(2,1)} fusion(bf16[4,512,128]{2,1,0:T(8,128)(2,1)} %get-tuple-element.613, s32[]{:T(128)} %get-tuple-element.612, bf16[2048,128]{1,0:T(8,128)(2,1)} %get-tuple-element.623, s32[2048]{0:T(1024)S(1)} %get-tuple-element.622, s32[512]{0:T(512)S(1)} %iota_add_fusion.2, ...), kind=kOutput, calls=%fused_computation.14.clone.1 | convolution fusion | flops 269615104 | bytes 797696 | tf_op jit(solution)/shard_map/while/body/eval_jaxpr/dot_general | solution.py:459
  117.5 0.6 dynamic_slice.22
  118.0 0.6 iota_add_fusion.2
  118.7 0.5 convert_reduce_fusion.2
  119.3 2.5 %fusion.34 = bf16[4,512,128]{2,1,0:T(8,128)(2,1)} fusion(bf16[4,512,128]{2,1,0:T(8,128)(2,1)} %get-tuple-element.613, s32[]{:T(128)} %get-tuple-element.612, bf16[2048,128]{1,0:T(8,128)(2,1)} %get-tuple-element.623, s32[2048]{0:T(1024)S(1)} %get-tuple-element.622, s32[512]{0:T(512)S(1)} %iota_add_fusion.2, ...), kind=kOutput, calls=%fused_computation.14.clone.1 | convolution fusion | flops 269615104 | bytes 797696 | tf_op jit(solution)/shard_map/while/body/eval_jaxpr/dot_general | solution.py:459
  121.8 0.6 dynamic_slice.22
  122.3 0.6 iota_add_fusion.2
  123.0 0.5 convert_reduce_fusion.2
  123.6 2.5 %fusion.34 = bf16[4,512,128]{2,1,0:T(8,128)(2,1)} fusion(bf16[4,512,128]{2,1,0:T(8,128)(2,1)} %get-tuple-element.613, s32[]{:T(128)} %get-tuple-element.612, bf16[2048,128]{1,0:T(8,128)(2,1)} %get-tuple-element.623, s32[2048]{0:T(1024)S(1)} %get-tuple-element.622, s32[512]{0:T(512)S(1)} %iota_add_fusion.2, ...), kind=kOutput, calls=%fused_computation.14.clone.1 | convolution fusion | flops 269615104 | bytes 797696 | tf_op jit(solution)/shard_map/while/body/eval_jaxpr/dot_general | solution.py:459
  126.1 0.0 collective-permute-done
  126.1 1.5 maximum_select_fusion
  127.5 0.3 fusion.19
  127.9 0.0 copy-start.5
  127.9 0.6 select_reduce_fusion
  128.5 0.6 sqrt_add_fusion
  129.1 0.0 copy-done.12
  129.1 1.7 %subtract_select_fusion = (f32[2048,128]{1,0:T(8,128)}, f32[2048,128]{1,0:T(8,128)}) fusion(f32[2048,128]{1,0:T(8,128)S(1)} %copy-done.11, f32[2048]{0:T(1024)S(1)} %get-tuple-element.375, pred[2048]{0:T(1024)(128)(4,1)S(1)} %fusion.19, f32[2048,128]{1,0:T(8,128)S(1)} %copy-done.12, f32[2048,128]{1,0:T(8,128)S(1)} %maximum_select_fusion), kind=kLoop, calls=%fused_computation.18 | loop fusion | flops 2097152 | bytes 5253120 | tf_op jit(solution)/shard_map/jit(_where)/select_n | solution.py:547
  130.8 8.2 %all-to-all-done.5.left_ref.right_ref = bf16[128,64,128]{2,1,0:T(8,128)(2,1)S(1)} async-done(((bf16[128,64,128]{2,1,0:T(8,128)(2,1)}), bf16[128,64,128]{2,1,0:T(8,128)(2,1)S(1)}, u32[]{:S(2)}, u32[]{:S(2)}) %all-to-all-start.5) | async-done | bytes 2097184 | tf_op jit(solution)/shard_map/all_to_all | solution.py:446
  139.0 1.3 copy-done.9
  140.3 0.7 while.42
  141.0 7.3 %score.1 = f32[1,128]{1,0:T(1,128)} custom-call(f32[128,128]{1,0:T(8,128)} %get-tuple-element.314.keys_ref, bf16[128,64,128]{2,1,0:T(8,128)(2,1)} %copy-done.9, bf16[128,64,128]{2,1,0:T(8,128)(2,1)} %copy-done.9, f32[512,128]{1,0:T(8,128)S(1)} %get-tuple-element.318.start_ref, bf16[512,1024]{1,0:T(8,128)(2,1)} %first_ref.1, bf16[1024,1024]{1,0:T(8,128)(2,1)} %second_ref.1, ...), custom_call_target="tpu_custom_call" | custom-call | tf_op jit(solution)/shard_map/score/pallas_call | solution.py:430
  (32 shorter events, 0.3 us)
Async XLA Ops:
  0.6 2.1 %copy-start.15 = (s32[2048]{0:T(1024)S(1)}, s32[2048]{0:T(1024)}, u32[]{:S(2)}) copy-start(s32[2048]{0:T(1024)} %param.21) | copy-start | bytes 24580
  0.7 2.2 %copy-start.13 = (f32[2048]{0:T(1024)S(1)}, f32[2048]{0:T(1024)}, u32[]{:S(2)}) copy-start(f32[2048]{0:T(1024)} %param.25) | copy-start | bytes 24580
  0.7 2.5 %copy-start.14 = (s32[128,32]{0,1:T(8,128)S(1)}, s32[128,32]{0,1:T(8,128)}, u32[]{:S(2)}) copy-start(s32[128,32]{0,1:T(8,128)} %param.18) | copy-start | bytes 49156
  0.7 2.5 %copy-start.16 = (s32[128,4]{0,1:T(4,128)S(1)}, s32[128,4]{0,1:T(4,128)}, u32[]{:S(2)}) copy-start(s32[128,4]{0,1:T(4,128)} %param.19) | copy-start | bytes 6148
  0.7 2.5 %copy-start.4 = (s32[131072]{0:T(1024)S(1)}, s32[131072]{0:T(1024)}, u32[]{:S(2)}) copy-start(s32[131072]{0:T(1024)} %param.20) | copy-start | bytes 1572868
  2.0 8.3 %copy-start.6 = (bf16[128,32,128]{2,1,0:T(8,128)(2,1)S(1)}, bf16[128,32,128]{2,1,0:T(8,128)(2,1)}, u32[]{:S(2)}) copy-start(bf16[128,32,128]{2,1,0:T(8,128)(2,1)} %param.22) | copy-start | bytes 3145732
  2.4 16.5 %copy-start.7 = (f32[64,2,8,128]{3,2,1,0:T(8,128)}, f32[64,2,8,128]{3,2,1,0:T(8,128)S(1)}, u32[]{:S(2)}) copy-start(f32[64,2,8,128]{3,2,1,0:T(8,128)S(1)} %copy.36) | copy-start | bytes 1572868
  2.8 16.1 %copy-start.8 = (f32[64,2,8,128]{3,2,1,0:T(8,128)}, f32[64,2,8,128]{3,2,1,0:T(8,128)S(1)}, u32[]{:S(2)}) copy-start(f32[64,2,8,128]{3,2,1,0:T(8,128)S(1)} %copy.37) | copy-start | bytes 1572868
  18.9 53.2 %all-to-all-start.3 = ((bf16[128,96,128]{2,1,0:T(8,128)(2,1)}), bf16[128,96,128]{2,1,0:T(8,128)(2,1)S(1)}, u32[]{:S(2)}, u32[]{:S(2)}) async-start(bf16[128,96,128]{2,1,0:T(8,128)(2,1)} %pack.5), calls=%async_computation.3 | async-start | bytes 6291456 | tf_op jit(solution)/shard_map/all_to_all | solution.py:446
  81.1 7.7 %copy-start.17 = (bf16[1024]{0:T(1024)(128)(2,1)S(1)}, bf16[1024]{0:T(1024)(128)(2,1)}, u32[]{:S(2)}) copy-start(bf16[1024]{0:T(1024)(128)(2,1)} %param.29) | copy-start | bytes 6148
  81.9 16.6 %copy-start.10 = (bf16[1024,128]{1,0:T(8,128)(2,1)S(1)}, bf16[1024,128]{1,0:T(8,128)(2,1)}, u32[]{:S(2)}) copy-start(bf16[1024,128]{1,0:T(8,128)(2,1)} %get-tuple-element.632.new_ref) | copy-start | bytes 786436
  81.9 16.6 %collective-permute-start.2 = (bf16[1024,128]{1,0:T(8,128)(2,1)}, bf16[1024,128]{1,0:T(8,128)(2,1)S(1)}, u32[]{:S(2)}, u32[]{:S(2)}) collective-permute-start(bf16[1024,128]{1,0:T(8,128)(2,1)} %get-tuple-element.632.new_ref), channel_id=1, source_target_pairs={{0,1},{1,0},{2,3},{3,2},{4,5},{5,4},{6,7},{7,6},{8,9},{9,8},{10,11... | collective-permute-start | bytes 786440 | tf_op jit(solution)/shard_map/ppermute | solution.py:527
  83.0 17.1 %all-to-all-start.4 = ((f32[128,8,128]{2,1,0:T(8,128)}), f32[128,8,128]{2,1,0:T(8,128)S(1)}, u32[]{:S(2)}, u32[]{:S(2)}) async-start(f32[128,8,128]{2,1,0:T(8,128)} %get-tuple-element.310), calls=%async_computation.4 | async-start | bytes 1048576 | tf_op jit(solution)/shard_map/all_to_all | solution.py:446
  87.5 10.9 %collective-permute-start.1 = (s32[1024]{0:T(1024)S(1)}, s32[1024]{0:T(1024)S(1)}, u32[]{:S(2)}, u32[]{:S(2)}) collective-permute-start(s32[1024]{0:T(1024)S(1)} %convert_element_type.34), channel_id=1, source_target_pairs={{0,1},{1,0},{2,3},{3,2},{4,5},{5,4},{6,7},{7,6},{8,9},{9,8},{10,11... | collective-permute-start | bytes 12296 | tf_op jit(solution)/shard_map/ppermute | solution.py:529
  100.4 25.6 %collective-permute-start = (f32[1024,128]{1,0:T(8,128)S(1)}, f32[1024,128]{1,0:T(8,128)}, u32[]{:S(2)}, u32[]{:S(2)}) collective-permute-start(f32[1024,128]{1,0:T(8,128)S(1)} %bitcast.70), channel_id=1, source_target_pairs={{0,1},{1,0},{2,3},{3,2},{4,5},{5,4},{6,7},{7,6},{8,9},{9,8},{10,11... | collective-permute-start | bytes 1572872 | tf_op jit(solution)/shard_map/ppermute | solution.py:539
  101.5 37.5 %all-to-all-start.5 = ((bf16[128,64,128]{2,1,0:T(8,128)(2,1)}), bf16[128,64,128]{2,1,0:T(8,128)(2,1)S(1)}, u32[]{:S(2)}, u32[]{:S(2)}) async-start(bf16[128,64,128]{2,1,0:T(8,128)(2,1)} %reply.5), calls=%async_computation.5 | async-start | bytes 4194304 | tf_op jit(solution)/shard_map/all_to_all | solution.py:446
  126.0 3.1 %copy-start.11 = (f32[2048,128]{1,0:T(8,128)S(1)}, f32[2048,128]{1,0:T(8,128)}, u32[]{:S(2)}) copy-start(f32[2048,128]{1,0:T(8,128)} %param.23) | copy-start | bytes 3145732
  126.0 3.1 %copy-start.12 = (f32[2048,128]{1,0:T(8,128)S(1)}, f32[2048,128]{1,0:T(8,128)}, u32[]{:S(2)}) copy-start(f32[2048,128]{1,0:T(8,128)} %param.24) | copy-start | bytes 3145732
  127.9 11.1 %copy-start.5 = (s32[1024,128]{1,0:T(8,128)S(1)}, s32[1024,128]{1,0:T(8,128)}, u32[]{:S(2)}) copy-start(s32[1024,128]{1,0:T(8,128)} %get-tuple-element.657) | copy-start | bytes 1572868
  139.0 1.4 copy-start.9

commit v3 on v2

--- a/solution.py
+++ b/solution.py
@@ -29,6 +29,12 @@
 
 def one_hot(mask):
     return jnp.where(mask, 1.0, 0.0).astype(BF16)
+
+
+def hot_rows(count, index):
+    index = index.astype(jnp.int16)
+    place = iota((count, index.shape[1]), 0).astype(jnp.int16)
+    return jnp.where(place == index, jnp.bfloat16(1), jnp.bfloat16(0))
 
 
 def route_kernel(round_ref, ids_ref, map_ref, extra_ref, slots_ref, keys_ref, row_ref):
@@ -56,7 +62,7 @@
             field = sum((jnp.where(e <= t + u, 1, 0) for e in ends), jnp.zeros((1, samples), I32))
             keys.append(field * samples + sample)
         key = jnp.concatenate(keys, axis=1) + 1
-        hit = one_hot(iota((table.shape[0], wide), 0) == (ids >> 7))
+        hit = hot_rows(table.shape[0], ids >> 7)
         both = jnp.dot(parts, hit, preferred_element_type=F32)
         value = both[:LANES] * 512.0 + both[LANES:] + 256.0
         value = jnp.where(iota((LANES, wide), 0) == (ids & 127), value, 0.0)
@@ -116,7 +122,9 @@
 
 
 def pack_kernel(slots_ref, grads_ref, table_ref, moment_ref, head_ref, out_ref, from_ref, to_ref):
-    bag, samples = slots_ref.shape
+    count = slots_ref.shape[0]
+    bag = 32
+    samples = count // bag
     block = 512
 
     def widen(i, carry):
@@ -126,9 +134,11 @@
         to_ref[pl.ds(at * 2 + block, block), :] = jnp.zeros((block, LANES), F32)
         return carry
 
-    def move(b, carry):
-        for t in range(bag):
-            to_ref[pl.ds(slots_ref[t, b], 1), :] = from_ref[pl.ds(b * bag + t, 1), :]
+    def move(i, carry):
+        first = (i & 3) * (bag * bag) + (i >> 2)
+        for u in range(bag):
+            slot = slots_ref[i * bag + u]
+            to_ref[pl.ds(slot, 1), :] = from_ref[pl.ds(first + u * bag, 1), :]
         return carry
 
     def narrow(i, carry):
@@ -144,7 +154,7 @@
         return carry
 
     lax.fori_loop(0, bag * samples // block, widen, 0)
-    lax.fori_loop(0, samples, move, 0)
+    lax.fori_loop(0, count // bag, move, 0)
     lax.fori_loop(0, DEVS // 8, narrow, 0)
 
 
@@ -160,7 +170,7 @@
             pltpu.VMEM((DEVS * ROUND + 8, LANES), F32),
         ],
         name="pack",
-    )(slots, grads, table, moment, head)
+    )(slots.reshape(-1), grads, table, moment, head)
 
 
 def pair_up(line, low):
@@ -185,7 +195,7 @@
         rows = jnp.concatenate([p[u] for u in range(8) for p in (left, right)], axis=0)
         if with_count:
             rows = jnp.concatenate([rows, jnp.ones_like(rows)], axis=1)
-        hit = one_hot(iota((acc_ref.shape[0], width), 0) == index)
+        hit = hot_rows(acc_ref.shape[0], index)
         acc_ref[...] = acc_ref[...] + jnp.dot(hit, rows, preferred_element_type=F32)
         return carry
 
@@ -223,7 +233,7 @@
         grad = total[:, :LANES].reshape(shape)
         touched = (total[:, LANES:] > 0.5).reshape(shape)
         state = state_ref[part].astype(F32)
-        table = state[:, 0:8, :] + state[:, 8:16, :]
+        still = state[:, 0:8, :] + state[:, 8:16, :]
         moment = state[:, 16:24, :]
         source = iota(shape, 0)
         within = iota(shape, 1)
@@ -236,14 +246,15 @@
         spot = jnp.sum(jnp.where(lane == ROUND + 32 + own, extra, 0.0), axis=2, keepdims=True)
         mean = jnp.sum(grad * grad, axis=2, keepdims=True) * (1.0 / LANES)
         new_var = beta_two * var + (1.0 - beta_two) * mean
-        new_moment = beta_one * moment + (1.0 - beta_one) * grad
-        new_table = table - learn_rate * new_moment / (jnp.sqrt(new_var) + epsilon)
-        new_table = jnp.where(touched, new_table, table)
+        scale = 1.0 / (jnp.sqrt(new_var) + epsilon)
+        change = scale - 1.0 / (jnp.sqrt(beta_two * var) + epsilon)
+        step_of = beta_one * moment * change + (1.0 - beta_one) * grad * scale
+        new_table = still - learn_rate * step_of
         new_ref[pl.ds(at, LANES), :] = new_table.reshape(LANES, LANES).astype(BF16)
         sums_ref[part] = jnp.where(touched, grad, UNTOUCHED)
-        spot = jnp.where(touched & (lane == within), spot, 0.0)
-        away = jnp.where(touched | (lane != within), 0.0, 4096.0)
-        spots_ref[pl.ds(pl.multiple_of(i * 16, 16), 16), :] = jnp.sum(spot + away, axis=1)
+        spot = jnp.where(lane == source * 8 + within, jnp.where(touched, spot, 4096.0), 0.0)
+        spot = jnp.sum(jnp.sum(spot, axis=0), axis=0, keepdims=True)
+        spots_ref[pl.ds(i, 1), :] = spot.astype(I32)
         return carry
 
     lax.fori_loop(0, 8, step, 0)
@@ -282,12 +293,12 @@
     return (
         jax.ShapeDtypeStruct((rows, LANES), BF16),
         jax.ShapeDtypeStruct((DEVS, 8, LANES), F32),
-        jax.ShapeDtypeStruct((DEVS, LANES), F32),
+        jax.ShapeDtypeStruct((8, LANES), I32),
     )
 
 
 def updated_specs(rows):
-    return [whole((rows, LANES)), whole((DEVS, 8, LANES)), whole((DEVS, LANES))]
+    return [whole((rows, LANES)), whole((DEVS, 8, LANES)), whole((8, LANES))]
 
 
 def update(core, received, rows):
@@ -356,23 +367,29 @@
 
 def reply_kernel(line_ref, new_ref, out_ref, turned_ref, table_ref):
     turned_ref[...] = line_ref[...].T
-    half = new_ref.shape[0] // 2
-    table_ref[...] = jnp.concatenate([new_ref[0:half, :], new_ref[half:, :]], axis=1)
+    part = new_ref.shape[0] // 4
+    table_ref[...] = jnp.concatenate(
+        [new_ref[k * part : (k + 1) * part, :] for k in range(4)], axis=1
+    )
 
     def look(i, carry):
-        turned = pltpu.roll(turned_ref[0:ROUND, :], LANES - i * 8, 1).astype(I32)
-        within = turned & (half - 1)
+        turned = pltpu.roll(turned_ref[0:ROUND, :], LANES - i * 16, 1).astype(I32)
+        within = turned & (part - 1)
         hit = jnp.concatenate(
-            [one_hot(iota((ROUND, half), 1) == within[:, u : u + 1]) for u in range(8)], axis=0
+            [one_hot(iota((ROUND, part), 1) == within[:, u : u + 1]) for u in range(16)], axis=0
         )
         found = jnp.dot(hit, table_ref[...], preferred_element_type=F32)
-        for u in range(8):
+        for u in range(16):
             piece = found[u * ROUND : (u + 1) * ROUND]
-            piece = jnp.where(turned[:, u : u + 1] < half, piece[:, :LANES], piece[:, LANES:])
-            out_ref[i * 8 + u] = piece.astype(BF16)
+            row = jnp.broadcast_to(turned[:, u : u + 1], (ROUND, LANES))
+            low = jnp.where(row < part, piece[:, :LANES], piece[:, LANES : 2 * LANES])
+            high = jnp.where(
+                row < 3 * part, piece[:, 2 * LANES : 3 * LANES], piece[:, 3 * LANES :]
+            )
+            out_ref[i * 16 + u] = jnp.where(row < 2 * part, low, high).astype(BF16)
         return carry
 
-    lax.fori_loop(0, DEVS // 8, look, 0)
+    lax.fori_loop(0, DEVS // 16, look, 0)
 
 
 def reply(line, new_rows):
@@ -383,7 +400,7 @@
         out_shape=jax.ShapeDtypeStruct((DEVS, ROUND, LANES), BF16),
         scratch_shapes=[
             pltpu.VMEM((DEVS, LANES), F32),
-            pltpu.VMEM((new_rows.shape[0] // 2, 2 * LANES), BF16),
+            pltpu.VMEM((new_rows.shape[0] // 4, 4 * LANES), BF16),
         ],
         name="reply",
     )(line, new_rows)
@@ -446,21 +463,35 @@
     return lax.all_to_all(value, ALL, 0, 0, tiled=True)
 
 
-def place_rows(serving_old, slot_index, rows_in):
-    tab_rows, row_width = serving_old.shape
+def place_kernel(old_ref, own_ref, other_ref, own_at_ref, other_at_ref, out_ref):
     block = 512
-    old_blocks = serving_old.reshape(tab_rows // block, block, row_width)
-    firsts = jnp.arange(tab_rows // block, dtype=jnp.int32) * block
-
-    def place_block(pieces):
-        old_piece, first = pieces
-        wanted = first + jnp.arange(block, dtype=jnp.int32)
-        hit = (wanted[:, None] == slot_index[None, :]).astype(jnp.bfloat16)
-        fresh = jnp.dot(hit, rows_in, preferred_element_type=jnp.float32)
-        found = jnp.sum(hit.astype(jnp.float32), axis=1) > 0.5
-        return jnp.where(found[:, None], fresh.astype(jnp.bfloat16), old_piece)
-
-    return lax.map(place_block, (old_blocks, firsts)).reshape(tab_rows, row_width)
+
+    def place(i, carry):
+        at = pl.ds(pl.multiple_of(i * block, block), block)
+        total = jnp.zeros((block, 2 * LANES), F32)
+        for at_ref, rows_ref in ((own_at_ref, own_ref), (other_at_ref, other_ref)):
+            spots = at_ref[...] - i * block
+            spots = jnp.where((spots >= 0) & (spots < block), spots, -1)
+            spots = jnp.concatenate([spots[u : u + 1] for u in range(8)], axis=1)
+            rows = rows_ref[...]
+            rows = jnp.concatenate([rows, jnp.ones_like(rows)], axis=1)
+            total = total + jnp.dot(hot_rows(block, spots), rows, preferred_element_type=F32)
+        fresh = total[:, :LANES].astype(BF16).astype(F32)
+        old = old_ref[at, :].astype(F32)
+        out_ref[at, :] = jnp.where(total[:, LANES:] > 0.5, fresh, old).astype(BF16)
+        return carry
+
+    lax.fori_loop(0, old_ref.shape[0] // block, place, 0)
+
+
+def place_rows(old, own, other, own_at, other_at):
+    return pl.pallas_call(
+        place_kernel,
+        in_specs=[pl.BlockSpec(memory_space=pltpu.VMEM)] * 5,
+        out_specs=pl.BlockSpec(memory_space=pltpu.VMEM),
+        out_shape=jax.ShapeDtypeStruct(old.shape, BF16),
+        name="place",
+    )(old, own, other, own_at, other_at)
 
 
 def per_device(
@@ -501,7 +532,8 @@
     spread = jnp.broadcast_to(spread[:, None, :], (owners, 2, 2 * tab_rows // owners))
     extra = jnp.concatenate([jnp.zeros((DEVS, ROUND), F32), spread.reshape(DEVS, -1)], axis=1)
 
-    table_out, moment_out = outgoing(table), outgoing(moment)
+    scale = learn_rate * beta_one / (jnp.sqrt(beta_two * row_var) + epsilon)
+    table_out, moment_out = outgoing(table - moment * scale[:, None]), outgoing(moment)
     slots, keys, head = route(jnp.zeros((1,), I32), ids, map_rows, extra)
     received = exchange(pack(slots, grads, table_out, moment_out, head))
     core = rep.reshape(1).astype(I32)
@@ -525,13 +557,8 @@
     answer = exchange(reply(line, new_rows))
 
     other_rows = lax.ppermute(new_rows, "rep", swap)
-    places = places[:, :8].reshape(-1).astype(I32)
     other_places = lax.ppermute(places, "rep", swap)
-    serving_table = place_rows(
-        serving_old,
-        jnp.concatenate([places, other_places]),
-        jnp.concatenate([new_rows, other_rows]),
-    )
+    serving_table = place_rows(serving_old, new_rows, other_rows, places, other_places)
 
     back = back.reshape(owners, 2, 8, row_width)
     back = jnp.where(odd, back[:, ::-1], back)
@@ -555,7 +582,7 @@
         line = got[:, 0] * 32.0 + got[:, 1] - 1.0
         return (k + 1, more_rows(keys, exchange(reply(line, new_rows)), acc, False, False))
 
-    answer, rounds = lax.optimization_barrier((answer, rounds))
+    rounds, _ = lax.optimization_barrier((rounds, answer[0, 0, 0]))
     _, pooled = lax.while_loop(
         lambda c: c[0] < rounds,
         more_pooled,

time: 149 us -> 146 us (0.980)
  waiting for transfers between devices: 50.7 us -> 64.2 us
  matrix products: 9.98 us -> 0 us
  starting transfers between devices: 25.8 us -> 22.3 us
  other arithmetic: 11.4 us -> 8.29 us
  Pallas kernels: 41.1 us -> 42.7 us
    all_to_all x3, waiting for transfers between devices: 50.7 us -> 63.4 us  [exchange(): return lax.all_to_all(value, ALL, 0, 0, tiled=True)]
    dot_general x4 -> x0, matrix products: 9.98 us -> none  [place_block(): fresh = jnp.dot(hit, rows_in, preferred_element_type=jnp.float32)]
    pallas_call x0 -> x1, Pallas kernels: none -> 4.76 us  [place_rows(): pl.pallas_call(place_kernel, in_specs=[pl.BlockSpec(memory_space=pltpu.VM...]
    add x4 -> x0, other arithmetic: 2.59 us -> none  [place_block(): wanted = first + jnp.arange(block, dtype=jnp.int32)]
    dynamic_slice x4 -> x0, local copies, waits for them, and re-layouts: 2.33 us -> none  [place_rows(): lax.map(place_block, (old_blocks, firsts)).reshape(tab_rows, row_width)]
    pallas_call x1, Pallas kernels: 9.16 us -> 6.94 us  [reply(): pl.pallas_call(reply_kernel, in_specs=[pl.BlockSpec(memory_space=pltpu.VM...]
    reduce_sum x4 -> x0, other arithmetic: 2.19 us -> none  [place_block(): found = jnp.sum(hit.astype(jnp.float32), axis=1) > 0.5]
    all_to_all x3, starting transfers between devices: 22.4 us -> 20.6 us  [exchange(): return lax.all_to_all(value, ALL, 0, 0, tiled=True)]
  transfers between devices with their start and end apart: 6 -> 6, of which waited for: 3 -> 4; matrix products, arithmetic and copies ran while one was open for 16% -> 4% of each run, Pallas kernels for 6% -> 8%
where the time goes in v3:
time: 146 us
  waiting for transfers between devices  64.2 us (44%)
  Pallas kernels  42.7 us (29%)
  starting transfers between devices  22.3 us (15%)
  other arithmetic  8.29 us (6%)
  local copies, waits for them, and re-layouts  5.92 us (4%)
  loops' own time  1.53 us (1%)
    all_to_all x3, waiting for transfers between devices, exchange(): return lax.all_to_all(value, ALL, 0, 0, tiled=True)  63.4 us
    all_to_all x3, starting transfers between devices, exchange(): return lax.all_to_all(value, ALL, 0, 0, tiled=True)  20.6 us
    pallas_call x1, Pallas kernels, update(): pl.pallas_call(update_kernel, grid=(STEPS,), in_specs=[pl.BlockSpec(memor...  9.27 us
    pallas_call x1, Pallas kernels, pack(): pl.pallas_call(pack_kernel, in_specs=[pl.BlockSpec(memory_space=pltpu.SME...  7.46 us
    pallas_call x1, Pallas kernels, score(): pl.pallas_call(score_kernel, grid=(STEPS,), in_specs=[whole(keys.shape),...  7.22 us
    pallas_call x1, Pallas kernels, route(): pl.pallas_call(route_kernel, in_specs=[pl.BlockSpec(memory_space=pltpu.SM...  7.05 us
    pallas_call x1, Pallas kernels, reply(): pl.pallas_call(reply_kernel, in_specs=[pl.BlockSpec(memory_space=pltpu.VM...  6.94 us
    pallas_call x1, Pallas kernels, place_rows(): pl.pallas_call(place_kernel, in_specs=[pl.BlockSpec(memory_space=pltpu.VM...  4.76 us
  transfers between devices with their start and end apart: 6, of which 4 were waited for; matrix products, arithmetic and copies ran while one was open for 4% of the time, Pallas kernels for 8%

profile of v3, /device:TPU:1, one launch (start us, length us, event | category | flops | bytes accessed | tf_op | source)
XLA Modules:
  0.0 145.9 jit_solution(2843548487274231852)
XLA Ops:
  0.6 0.7 add_divide_fusion
  1.4 0.8 reshape.82
  2.1 0.0 copy-start.16
  2.1 0.0 copy-start.4
  2.1 1.5 %constant_dynamic-slice_fusion = (f32[1024,128]{1,0:T(8,128)S(1)}, f32[1024,128]{1,0:T(8,128)S(1)}) fusion(f32[2048,128]{1,0:T(8,128)} %param.22, s32[]{:T(128)S(6)} %select_n.65, f32[1024]{0:T(1024)S(1)} %dynamic-slice, f32[2048,128]{1,0:T(8,128)} %param.21), kind=kLoop, calls=%fused_computation.28 | loop fusion | flops 262144 | bytes 2101252 | tf_op jit(solution)/shard_map/dynamic_slice | solution.py:525
  3.6 0.0 copy-start.6
  3.6 0.1 fusion.4
  3.8 0.3 copy.29
  4.1 0.0 copy-start.7
  4.1 0.3 copy.30
  4.4 0.0 copy-done.16
  4.4 0.0 copy-start.8
  4.4 0.1 reshape.83
  4.5 0.1 copy.28
  4.6 0.1 concatenate.17.extra_ref
  4.7 0.0 copy-done.15
  4.7 0.0 copy-done.19
  4.7 0.0 copy-done.4
  4.8 7.1 %route.9 = (s32[32,128]{1,0:T(8,128)}, f32[128,128]{1,0:T(8,128)}, f32[128,8,128]{2,1,0:T(8,128)}) custom-call(s32[1]{0:T(128)} %constant.83.clone.1.round_ref, s32[36,128]{1,0:T(8,128)S(1)} %add_bitcast_fusion.1.ids_ref, s32[1024,128]{1,0:T(8,128)S(1)} %bitcast.46, f32[128,128]{1,0:T(8,128)S(1)} %concatenate.17.extra_ref), custom_call_target="tpu_custom_call" | custom-call | tf_op jit(solution)/shard_map/route/pallas_call | solution.py:110
  11.8 0.0 copy-done.6
  11.8 7.5 %pack.5 = bf16[128,96,128]{2,1,0:T(8,128)(2,1)} custom-call(s32[4096]{0:T(1024)} %bitcast.65, bf16[4096,128]{1,0:T(8,128)(2,1)S(1)} %bitcast.48, f32[128,8,128]{2,1,0:T(8,128)S(1)} %bitcast.49, f32[128,8,128]{2,1,0:T(8,128)S(1)} %bitcast.51, f32[128,8,128]{2,1,0:T(8,128)} %get-tuple-element.270.head_ref), custom_call_target="tpu_custom_call" | custom-call | tf_op jit(solution)/shard_map/pack/pallas_call | solution.py:162
  19.3 0.0 copy-done.7
  19.3 0.0 copy-done.8
  19.3 11.5 %all-to-all-start.3 = ((bf16[128,96,128]{2,1,0:T(8,128)(2,1)}), bf16[128,96,128]{2,1,0:T(8,128)(2,1)S(1)}, u32[]{:S(2)}, u32[]{:S(2)}) async-start(bf16[128,96,128]{2,1,0:T(8,128)(2,1)} %pack.5), calls=%async_computation.3 | async-start | bytes 6291456 | tf_op jit(solution)/shard_map/all_to_all | solution.py:463
  30.8 41.7 %all-to-all-done.3.state_ref.left_ref.right_ref = bf16[128,96,128]{2,1,0:T(8,128)(2,1)S(1)} async-done(((bf16[128,96,128]{2,1,0:T(8,128)(2,1)}), bf16[128,96,128]{2,1,0:T(8,128)(2,1)S(1)}, u32[]{:S(2)}, u32[]{:S(2)}) %all-to-all-start.3) | async-done | bytes 3145760 | tf_op jit(solution)/shard_map/all_to_all | solution.py:463
  72.4 9.3 %update.1 = (bf16[1024,128]{1,0:T(8,128)(2,1)}, f32[128,8,128]{2,1,0:T(8,128)}, s32[8,128]{1,0:T(8,128)}, f32[1024,256]{1,0:T(8,128)}, f32[128,128]{1,0:T(8,128)}, /*index=5*/s32[1]{0:T(128)}) custom-call(s32[1]{0:T(128)} %bitcast.5.core_ref, bf16[128,96,128]{2,1,0:T(8,128)(2,1)S(1)} %all-to-all-done.3.state_ref.left_ref.right_ref, ...), custom_call_target="tpu_custom_call" | custom-call | tf_op jit(solution)/shard_map/update/pallas_call | solution.py:305
  81.7 0.7 while.30
  82.5 0.0 copy-start.5
  82.5 0.0 copy-start.10
  82.5 4.6 %all-to-all-start.4 = ((f32[128,8,128]{2,1,0:T(8,128)}), f32[128,8,128]{2,1,0:T(8,128)S(1)}, u32[]{:S(2)}, u32[]{:S(2)}) async-start(f32[128,8,128]{2,1,0:T(8,128)} %get-tuple-element.276), calls=%async_computation.4 | async-start | bytes 1048576 | tf_op jit(solution)/shard_map/all_to_all | solution.py:463
  87.1 6.9 %reply.5 = bf16[128,64,128]{2,1,0:T(8,128)(2,1)} custom-call(f32[128,128]{1,0:T(8,128)} %get-tuple-element.280.line_ref, bf16[1024,128]{1,0:T(8,128)(2,1)} %get-tuple-element.527.own_ref.new_ref), custom_call_target="tpu_custom_call" | custom-call | tf_op jit(solution)/shard_map/reply/pallas_call | solution.py:396
  94.0 6.8 %all-to-all-done.4 = f32[128,8,128]{2,1,0:T(8,128)S(1)} async-done(((f32[128,8,128]{2,1,0:T(8,128)}), f32[128,8,128]{2,1,0:T(8,128)S(1)}, u32[]{:S(2)}, u32[]{:S(2)}) %all-to-all-start.4) | async-done | bytes 524320 | tf_op jit(solution)/shard_map/all_to_all | solution.py:463
  100.8 1.0 copy.31
  101.8 0.0 copy-done.5
  101.8 0.0 copy-done.10
  101.8 0.8 while.31
  102.6 0.0 copy-start.17
  102.6 0.0 copy-start.20
  102.6 4.5 %all-to-all-start.5 = ((bf16[128,64,128]{2,1,0:T(8,128)(2,1)}), bf16[128,64,128]{2,1,0:T(8,128)(2,1)S(1)}, u32[]{:S(2)}, u32[]{:S(2)}) async-start(bf16[128,64,128]{2,1,0:T(8,128)(2,1)} %reply.5), calls=%async_computation.5 | async-start | bytes 4194304 | tf_op jit(solution)/shard_map/all_to_all | solution.py:463
  107.1 1.3 reverse_select_fusion
  108.4 0.0 copy-start.14
  108.4 1.2 collective-permute-start
  109.6 0.1 collective-permute-start.1
  109.7 0.0 copy-done.17
  109.7 0.4 collective-permute-start.2
  110.1 0.0 copy-done.20
  110.1 0.6 reshape.93.score_ref
  110.7 0.8 collective-permute-done.2.other_at_ref
  111.5 0.0 collective-permute-done.1.other_ref
  111.5 0.6 copy-done.18
  112.1 0.7 copy-done.13
  112.8 4.8 %place.1 = bf16[2048,128]{1,0:T(8,128)(2,1)} custom-call(bf16[2048,128]{1,0:T(8,128)(2,1)} %old_ref.1, bf16[1024,128]{1,0:T(8,128)(2,1)S(1)} %get-tuple-element.554, bf16[1024,128]{1,0:T(8,128)(2,1)} %copy-done.13, s32[8,128]{1,0:T(8,128)S(1)} %copy-done.17, s32[8,128]{1,0:T(8,128)} %copy-done.18), custom_call_target="tpu_custom_call" | custom-call | tf_op jit(solution)/shard_map/place/pallas_call | solution.py:488
  117.6 0.0 collective-permute-done
  117.6 1.5 %maximum_select_fusion = f32[2048,128]{1,0:T(8,128)S(1)} fusion(f32[1024,128]{1,0:T(8,128)} %collective-permute-done, f32[1024,128]{1,0:T(8,128)S(1)} %bitcast.59, pred[]{:T(512)S(6)} %eq.10), kind=kLoop, calls=%fused_computation.8 | loop fusion | flops 786432 | bytes 2097153 | tf_op jit(solution)/shard_map/jit(_where)/select_n | solution.py:567
  119.1 0.3 fusion.3
  119.4 0.6 select_reduce_fusion
  120.1 0.0 copy-done.14
  120.1 0.6 sqrt_add_fusion
  120.7 0.0 copy-done.11
  120.7 0.0 copy-done.12
  120.7 1.7 %subtract_select_fusion = (f32[2048,128]{1,0:T(8,128)}, f32[2048,128]{1,0:T(8,128)}) fusion(f32[2048,128]{1,0:T(8,128)S(1)} %copy-done.11, f32[2048]{0:T(1024)S(1)} %get-tuple-element.326, pred[2048]{0:T(1024)(128)(4,1)S(1)} %fusion.3, f32[2048,128]{1,0:T(8,128)S(1)} %copy-done.12, f32[2048,128]{1,0:T(8,128)S(1)} %maximum_select_fusion), kind=kLoop, calls=%fused_computation.6 | loop fusion | flops 2097152 | bytes 5253120 | tf_op jit(solution)/shard_map/jit(_where)/select_n | solution.py:574
  122.3 15.0 %all-to-all-done.5.left_ref.right_ref = bf16[128,64,128]{2,1,0:T(8,128)(2,1)S(1)} async-done(((bf16[128,64,128]{2,1,0:T(8,128)(2,1)}), bf16[128,64,128]{2,1,0:T(8,128)(2,1)S(1)}, u32[]{:S(2)}, u32[]{:S(2)}) %all-to-all-start.5) | async-done | bytes 2097184 | tf_op jit(solution)/shard_map/all_to_all | solution.py:463
  137.3 1.4 copy-done.9
  138.7 7.2 %score.1 = f32[1,128]{1,0:T(1,128)} custom-call(f32[128,128]{1,0:T(8,128)} %get-tuple-element.279.keys_ref, bf16[128,64,128]{2,1,0:T(8,128)(2,1)} %copy-done.9, bf16[128,64,128]{2,1,0:T(8,128)(2,1)} %copy-done.9, f32[512,128]{1,0:T(8,128)S(1)} %get-tuple-element.281.start_ref, bf16[512,1024]{1,0:T(8,128)(2,1)} %first_ref.1, bf16[1024,1024]{1,0:T(8,128)(2,1)} %second_ref.1, ...), custom_call_target="tpu_custom_call" | custom-call | tf_op jit(solution)/shard_map/score/pallas_call | solution.py:447
  (13 shorter events, 0.1 us)
Async XLA Ops:
  2.1 2.3 %copy-start.16 = (s32[2048]{0:T(1024)S(1)}, s32[2048]{0:T(1024)}, u32[]{:S(2)}) copy-start(s32[2048]{0:T(1024)} %param.19) | copy-start | bytes 24580
  2.1 2.6 %copy-start.15 = (s32[128,32]{0,1:T(8,128)S(1)}, s32[128,32]{0,1:T(8,128)}, u32[]{:S(2)}) copy-start(s32[128,32]{0,1:T(8,128)} %param.16) | copy-start | bytes 49156
  2.1 2.6 %copy-start.19 = (s32[128,4]{0,1:T(4,128)S(1)}, s32[128,4]{0,1:T(4,128)}, u32[]{:S(2)}) copy-start(s32[128,4]{0,1:T(4,128)} %param.17) | copy-start | bytes 6148
  2.1 2.6 %copy-start.4 = (s32[131072]{0:T(1024)S(1)}, s32[131072]{0:T(1024)}, u32[]{:S(2)}) copy-start(s32[131072]{0:T(1024)} %param.18) | copy-start | bytes 1572868
  3.6 8.2 %copy-start.6 = (bf16[128,32,128]{2,1,0:T(8,128)(2,1)S(1)}, bf16[128,32,128]{2,1,0:T(8,128)(2,1)}, u32[]{:S(2)}) copy-start(bf16[128,32,128]{2,1,0:T(8,128)(2,1)} %param.20) | copy-start | bytes 3145732
  4.1 15.2 %copy-start.7 = (f32[64,2,8,128]{3,2,1,0:T(8,128)}, f32[64,2,8,128]{3,2,1,0:T(8,128)S(1)}, u32[]{:S(2)}) copy-start(f32[64,2,8,128]{3,2,1,0:T(8,128)S(1)} %copy.29) | copy-start | bytes 1572868
  4.4 14.9 %copy-start.8 = (f32[64,2,8,128]{3,2,1,0:T(8,128)}, f32[64,2,8,128]{3,2,1,0:T(8,128)S(1)}, u32[]{:S(2)}) copy-start(f32[64,2,8,128]{3,2,1,0:T(8,128)S(1)} %copy.30) | copy-start | bytes 1572868
  19.3 53.2 %all-to-all-start.3 = ((bf16[128,96,128]{2,1,0:T(8,128)(2,1)}), bf16[128,96,128]{2,1,0:T(8,128)(2,1)S(1)}, u32[]{:S(2)}, u32[]{:S(2)}) async-start(bf16[128,96,128]{2,1,0:T(8,128)(2,1)} %pack.5), calls=%async_computation.3 | async-start | bytes 6291456 | tf_op jit(solution)/shard_map/all_to_all | solution.py:463
  82.5 19.3 %copy-start.5 = (s32[1024,128]{1,0:T(8,128)S(1)}, s32[1024,128]{1,0:T(8,128)}, u32[]{:S(2)}) copy-start(s32[1024,128]{1,0:T(8,128)} %get-tuple-element.552) | copy-start | bytes 1572868
  82.5 19.3 %copy-start.10 = (bf16[1024,128]{1,0:T(8,128)(2,1)S(1)}, bf16[1024,128]{1,0:T(8,128)(2,1)}, u32[]{:S(2)}) copy-start(bf16[1024,128]{1,0:T(8,128)(2,1)} %get-tuple-element.527.own_ref.new_ref) | copy-start | bytes 786436
  82.5 18.3 %all-to-all-start.4 = ((f32[128,8,128]{2,1,0:T(8,128)}), f32[128,8,128]{2,1,0:T(8,128)S(1)}, u32[]{:S(2)}, u32[]{:S(2)}) async-start(f32[128,8,128]{2,1,0:T(8,128)} %get-tuple-element.276), calls=%async_computation.4 | async-start | bytes 1048576 | tf_op jit(solution)/shard_map/all_to_all | solution.py:463
  102.6 7.2 %copy-start.17 = (s32[8,128]{1,0:T(8,128)S(1)}, s32[8,128]{1,0:T(8,128)}, u32[]{:S(2)}) copy-start(s32[8,128]{1,0:T(8,128)} %get-tuple-element.278.own_at_ref) | copy-start | bytes 12292
  102.6 7.6 %copy-start.20 = (bf16[1024]{0:T(1024)(128)(2,1)S(1)}, bf16[1024]{0:T(1024)(128)(2,1)}, u32[]{:S(2)}) copy-start(bf16[1024]{0:T(1024)(128)(2,1)} %param.27) | copy-start | bytes 6148
  102.6 34.7 %all-to-all-start.5 = ((bf16[128,64,128]{2,1,0:T(8,128)(2,1)}), bf16[128,64,128]{2,1,0:T(8,128)(2,1)S(1)}, u32[]{:S(2)}, u32[]{:S(2)}) async-start(bf16[128,64,128]{2,1,0:T(8,128)(2,1)} %reply.5), calls=%async_computation.5 | async-start | bytes 4194304 | tf_op jit(solution)/shard_map/all_to_all | solution.py:463
  108.4 11.7 %copy-start.14 = (f32[2048]{0:T(1024)S(1)}, f32[2048]{0:T(1024)}, u32[]{:S(2)}) copy-start(f32[2048]{0:T(1024)} %param.23) | copy-start | bytes 24580
  108.4 9.2 %collective-permute-start = (f32[1024,128]{1,0:T(8,128)S(1)}, f32[1024,128]{1,0:T(8,128)}, u32[]{:S(2)}, u32[]{:S(2)}) collective-permute-start(f32[1024,128]{1,0:T(8,128)S(1)} %bitcast.58), channel_id=1, source_target_pairs={{0,1},{1,0},{2,3},{3,2},{4,5},{5,4},{6,7},{7,6},{8,9},{9,8},{10,11... | collective-permute-start | bytes 1572872 | tf_op jit(solution)/shard_map/ppermute | solution.py:566
  109.6 1.9 %collective-permute-start.1 = (bf16[1024,128]{1,0:T(8,128)(2,1)S(1)}, bf16[1024,128]{1,0:T(8,128)(2,1)S(1)}, u32[]{:S(2)}, u32[]{:S(2)}) collective-permute-start(bf16[1024,128]{1,0:T(8,128)(2,1)S(1)} %get-tuple-element.554), channel_id=1, source_target_pairs={{0,1},{1,0},{2,3},{3,2},{4,5},{5,4},{6,7},{7,6},{8,9},{9,8},{10,11... | collective-permute-start | bytes 786440 | tf_op jit(solution)/shard_map/ppermute | solution.py:559
  109.7 1.8 %collective-permute-start.2 = (s32[8,128]{1,0:T(8,128)S(1)}, s32[8,128]{1,0:T(8,128)S(1)}, u32[]{:S(2)}, u32[]{:S(2)}) collective-permute-start(s32[8,128]{1,0:T(8,128)S(1)} %copy-done.17), channel_id=1, source_target_pairs={{0,1},{1,0},{2,3},{3,2},{4,5},{5,4},{6,7},{7,6},{8,9},{9,8},{10,11... | collective-permute-start | bytes 12296 | tf_op jit(solution)/shard_map/ppermute | solution.py:560
  111.5 0.6 copy-start.18
  112.1 0.7 copy-start.13
  117.6 3.1 %copy-start.11 = (f32[2048,128]{1,0:T(8,128)S(1)}, f32[2048,128]{1,0:T(8,128)}, u32[]{:S(2)}) copy-start(f32[2048,128]{1,0:T(8,128)} %param.21) | copy-start | bytes 3145732
  117.6 3.1 %copy-start.12 = (f32[2048,128]{1,0:T(8,128)S(1)}, f32[2048,128]{1,0:T(8,128)}, u32[]{:S(2)}) copy-start(f32[2048,128]{1,0:T(8,128)} %param.22) | copy-start | bytes 3145732
  137.3 1.4 copy-start.9

commit v4 on v3

--- a/solution.py
+++ b/solution.py
@@ -121,7 +121,9 @@
     )(round_index, ids, train_map, extra)
 
 
-def pack_kernel(slots_ref, grads_ref, table_ref, moment_ref, head_ref, out_ref, from_ref, to_ref):
+def pack_kernel(
+    slots_ref, place_ref, grads_ref, table_ref, moment_ref, head_ref, out_ref, from_ref, to_ref
+):
     count = slots_ref.shape[0]
     bag = 32
     samples = count // bag
@@ -141,13 +143,21 @@
             to_ref[pl.ds(slot, 1), :] = from_ref[pl.ds(first + u * bag, 1), :]
         return carry
 
+    half, odd = place_ref[0], place_ref[1]
+
+    def rows_of(ref, i):
+        base = half * (ref.shape[0] // 2) + i * 4
+        starts = [base + ((u + odd) & 1) * (LANES // 2) + u // 2 for u in range(8)]
+        rows = [ref[pl.ds(start, 8, stride=LANES), :] for start in starts]
+        return jnp.concatenate([r.reshape(1, 8, LANES) for r in rows], axis=0)
+
     def narrow(i, carry):
         at = pl.multiple_of(i * 8, 8)
         rows = to_ref[pl.ds(pl.multiple_of(i * block, block), block), :].astype(BF16)
-        table = table_ref[pl.ds(at, 8)]
+        table = rows_of(table_ref, i)
         coarse = table.astype(BF16).astype(F32)
         state = jnp.concatenate([coarse, table - coarse], axis=1).astype(BF16)
-        more = jnp.concatenate([moment_ref[pl.ds(at, 8)], head_ref[pl.ds(at, 8)]], axis=1)
+        more = jnp.concatenate([rows_of(moment_ref, i), head_ref[pl.ds(at, 8)]], axis=1)
         out_ref[pl.ds(at, 8), 0:ROUND, :] = rows.reshape(8, ROUND, LANES)
         out_ref[pl.ds(at, 8), ROUND : ROUND + 16, :] = state
         out_ref[pl.ds(at, 8), ROUND + 16 : ROUND + 32, :] = more.astype(BF16)
@@ -158,10 +168,10 @@
     lax.fori_loop(0, DEVS // 8, narrow, 0)
 
 
-def pack(slots, grads, table, moment, head):
+def pack(slots, place, grads, table, moment, head):
     return pl.pallas_call(
         pack_kernel,
-        in_specs=[pl.BlockSpec(memory_space=pltpu.SMEM)]
+        in_specs=[pl.BlockSpec(memory_space=pltpu.SMEM)] * 2
         + [pl.BlockSpec(memory_space=pltpu.VMEM)] * 4,
         out_specs=pl.BlockSpec(memory_space=pltpu.VMEM),
         out_shape=jax.ShapeDtypeStruct((DEVS, SENT, LANES), BF16),
@@ -170,7 +180,7 @@
             pltpu.VMEM((DEVS * ROUND + 8, LANES), F32),
         ],
         name="pack",
-    )(slots.reshape(-1), grads, table, moment, head)
+    )(slots.reshape(-1), place, grads, table, moment, head)
 
 
 def pair_up(line, low):
@@ -182,17 +192,16 @@
 
 
 def add_rows(index_ref, left_ref, right_ref, acc_ref, with_count):
-    width = 8 * LANES
     step = pl.program_id(0)
-    turns = left_ref.shape[0] // 8
+    turns = left_ref.shape[0] // PAIRS
 
     def add(i, carry):
-        at = pl.ds(pl.multiple_of(i * 8, 8), 8)
-        pieces = pl.ds(pl.multiple_of((step * turns + i) * 8, 8), 8)
+        at = pl.ds(pl.multiple_of(i * PAIRS, PAIRS), PAIRS)
+        pieces = pl.ds(pl.multiple_of((step * turns + i) * PAIRS, PAIRS), PAIRS)
         index = index_ref[pieces, :]
-        index = jnp.concatenate([index[u : u + 1] for u in range(8)], axis=1)
+        index = jnp.concatenate([index[u : u + 1] for u in range(PAIRS)], axis=1)
         left, right = left_ref[at], right_ref[at]
-        rows = jnp.concatenate([p[u] for u in range(8) for p in (left, right)], axis=0)
+        rows = jnp.concatenate([p[u] for u in range(PAIRS) for p in (left, right)], axis=0)
         if with_count:
             rows = jnp.concatenate([rows, jnp.ones_like(rows)], axis=1)
         hit = hot_rows(acc_ref.shape[0], index)
@@ -202,6 +211,7 @@
     lax.fori_loop(0, turns, add, 0)
 
 
+PAIRS = 16
 STEPS = 4
 
 
@@ -233,7 +243,7 @@
         grad = total[:, :LANES].reshape(shape)
         touched = (total[:, LANES:] > 0.5).reshape(shape)
         state = state_ref[part].astype(F32)
-        still = state[:, 0:8, :] + state[:, 8:16, :]
+        table = state[:, 0:8, :] + state[:, 8:16, :]
         moment = state[:, 16:24, :]
         source = iota(shape, 0)
         within = iota(shape, 1)
@@ -246,10 +256,8 @@
         spot = jnp.sum(jnp.where(lane == ROUND + 32 + own, extra, 0.0), axis=2, keepdims=True)
         mean = jnp.sum(grad * grad, axis=2, keepdims=True) * (1.0 / LANES)
         new_var = beta_two * var + (1.0 - beta_two) * mean
-        scale = 1.0 / (jnp.sqrt(new_var) + epsilon)
-        change = scale - 1.0 / (jnp.sqrt(beta_two * var) + epsilon)
-        step_of = beta_one * moment * change + (1.0 - beta_one) * grad * scale
-        new_table = still - learn_rate * step_of
+        new_moment = beta_one * moment + (1.0 - beta_one) * grad
+        new_table = table - learn_rate * new_moment / (jnp.sqrt(new_var) + epsilon)
         new_ref[pl.ds(at, LANES), :] = new_table.reshape(LANES, LANES).astype(BF16)
         sums_ref[part] = jnp.where(touched, grad, UNTOUCHED)
         spot = jnp.where(lane == source * 8 + within, jnp.where(touched, spot, 4096.0), 0.0)
@@ -373,23 +381,23 @@
     )
 
     def look(i, carry):
-        turned = pltpu.roll(turned_ref[0:ROUND, :], LANES - i * 16, 1).astype(I32)
+        turned = pltpu.roll(turned_ref[0:ROUND, :], LANES - i * 32, 1).astype(I32)
         within = turned & (part - 1)
         hit = jnp.concatenate(
-            [one_hot(iota((ROUND, part), 1) == within[:, u : u + 1]) for u in range(16)], axis=0
+            [one_hot(iota((ROUND, part), 1) == within[:, u : u + 1]) for u in range(32)], axis=0
         )
         found = jnp.dot(hit, table_ref[...], preferred_element_type=F32)
-        for u in range(16):
+        for u in range(32):
             piece = found[u * ROUND : (u + 1) * ROUND]
             row = jnp.broadcast_to(turned[:, u : u + 1], (ROUND, LANES))
             low = jnp.where(row < part, piece[:, :LANES], piece[:, LANES : 2 * LANES])
             high = jnp.where(
                 row < 3 * part, piece[:, 2 * LANES : 3 * LANES], piece[:, 3 * LANES :]
             )
-            out_ref[i * 16 + u] = jnp.where(row < 2 * part, low, high).astype(BF16)
+            out_ref[i * 32 + u] = jnp.where(row < 2 * part, low, high).astype(BF16)
         return carry
 
-    lax.fori_loop(0, DEVS // 16, look, 0)
+    lax.fori_loop(0, DEVS // 32, look, 0)
 
 
 def reply(line, new_rows):
@@ -521,21 +529,14 @@
     map_rows = train_map.reshape(-1, LANES)
     grads = slot_grads.reshape(samples * bag, row_width)
 
-    def outgoing(value):
-        half = lax.dynamic_slice_in_dim(value, rep * rows_here, rows_here, 0)
-        half = half.reshape(8, 2, owners, row_width)
-        half = jnp.where(odd, half[:, ::-1], half)
-        return half.transpose(2, 1, 0, 3).reshape(DEVS, 8, row_width)
-
     spots = (serve_map % tab_rows).astype(F32).reshape(tab_rows // owners, owners).T
     spread = jnp.concatenate([row_var.reshape(tab_rows // owners, owners).T, spots], axis=1)
     spread = jnp.broadcast_to(spread[:, None, :], (owners, 2, 2 * tab_rows // owners))
     extra = jnp.concatenate([jnp.zeros((DEVS, ROUND), F32), spread.reshape(DEVS, -1)], axis=1)
 
-    scale = learn_rate * beta_one / (jnp.sqrt(beta_two * row_var) + epsilon)
-    table_out, moment_out = outgoing(table - moment * scale[:, None]), outgoing(moment)
+    place = jnp.stack([rep, owner % 2]).astype(I32)
     slots, keys, head = route(jnp.zeros((1,), I32), ids, map_rows, extra)
-    received = exchange(pack(slots, grads, table_out, moment_out, head))
+    received = exchange(pack(slots, place, grads, table, moment, head))
     core = rep.reshape(1).astype(I32)
     new_rows, sums, places, acc, line, rounds = update(core, received, rows_here)
     rounds = rounds[0]
@@ -544,7 +545,7 @@
     def more_sums(carry):
         k, acc = carry[0], carry[1]
         slots, _, head = route(k.reshape(1), ids, map_rows, extra)
-        got = exchange(pack(slots, grads, table_out, moment_out, head))
+        got = exchange(pack(slots, place, grads, table, moment, head))
         line = got[:, ROUND + 24].astype(F32) * 32.0 + got[:, ROUND + 25].astype(F32) - 1.0
         acc = more_rows(line, got, acc, True, True)
         return (k + 1, acc) + tuple(adam_again(core, received, acc))

time: 146 us -> 146 us (level)
  other arithmetic: 8.29 us -> 6.18 us
  local copies, waits for them, and re-layouts: 5.92 us -> 3.92 us
  waiting for transfers between devices: 64.2 us -> 66.2 us
    all_to_all x3, waiting for transfers between devices: 63.4 us -> 65.4 us  [exchange(): return lax.all_to_all(value, ALL, 0, 0, tiled=True)]
    pallas_call x1, Pallas kernels: 7.46 us -> 8.97 us  [pack(): pl.pallas_call(pack_kernel, in_specs=[pl.BlockSpec(memory_space=pltpu.SME...]
    dynamic_slice x1 -> x0, other arithmetic: 1.47 us -> none  [outgoing(): half = lax.dynamic_slice_in_dim(value, rep * rows_here, rows_here, 0)]
  transfers between devices with their start and end apart: 6 -> 6, of which waited for: 4 -> 4; matrix products, arithmetic and copies ran while one was open for 4% -> 4% of each run, Pallas kernels for 8% -> 7%
where the time goes in v4:
time: 146 us; the launch traced here: 145 us
  waiting for transfers between devices  66.2 us (45%)
  Pallas kernels  42.6 us (29%)
  starting transfers between devices  23.6 us (16%)
  other arithmetic  6.18 us (4%)
  local copies, waits for them, and re-layouts  3.92 us (3%)
  loops' own time  1.68 us (1%)
    all_to_all x3, waiting for transfers between devices, exchange(): return lax.all_to_all(value, ALL, 0, 0, tiled=True)  65.4 us
    all_to_all x3, starting transfers between devices, exchange(): return lax.all_to_all(value, ALL, 0, 0, tiled=True)  21.7 us
    pallas_call x1, Pallas kernels, pack(): pl.pallas_call(pack_kernel, in_specs=[pl.BlockSpec(memory_space=pltpu.SME...  8.97 us
    pallas_call x1, Pallas kernels, update(): pl.pallas_call(update_kernel, grid=(STEPS,), in_specs=[pl.BlockSpec(memor...  8.21 us
    pallas_call x1, Pallas kernels, route(): pl.pallas_call(route_kernel, in_specs=[pl.BlockSpec(memory_space=pltpu.SM...  8.1 us
    pallas_call x1, Pallas kernels, score(): pl.pallas_call(score_kernel, grid=(STEPS,), in_specs=[whole(keys.shape),...  6.73 us
    pallas_call x1, Pallas kernels, reply(): pl.pallas_call(reply_kernel, in_specs=[pl.BlockSpec(memory_space=pltpu.VM...  5.8 us
    pallas_call x1, Pallas kernels, place_rows(): pl.pallas_call(place_kernel, in_specs=[pl.BlockSpec(memory_space=pltpu.VM...  4.76 us
  transfers between devices with their start and end apart: 6, of which 4 were waited for; matrix products, arithmetic and copies ran while one was open for 4% of the time, Pallas kernels for 7%

profile of v4, /device:TPU:1, one launch (start us, length us, event | category | flops | bytes accessed | tf_op | source)
XLA Modules:
  0.0 145.0 jit_solution(16145063993434079389)
XLA Ops:
  0.6 0.7 fusion.5
  1.3 0.1 reshape.70
  1.4 0.8 reshape.69
  2.2 0.1 copy.26
  2.3 0.1 pad_add_fusion.place_ref
  2.4 0.1 concatenate.17.extra_ref
  2.5 0.7 add_bitcast_fusion.1.ids_ref
  3.2 8.1 %route.9 = (s32[32,128]{1,0:T(8,128)}, f32[128,128]{1,0:T(8,128)}, f32[128,8,128]{2,1,0:T(8,128)}) custom-call(s32[1]{0:T(128)} %constant.82.clone.1.round_ref, s32[36,128]{1,0:T(8,128)S(1)} %add_bitcast_fusion.1.ids_ref, s32[1024,128]{1,0:T(8,128)} %bitcast.38, f32[128,128]{1,0:T(8,128)S(1)} %concatenate.17.extra_ref), custom_call_target="tpu_custom_call" | custom-call | tf_op jit(solution)/shard_map/route/pallas_call | solution.py:110
  11.3 9.0 %pack.5 = bf16[128,96,128]{2,1,0:T(8,128)(2,1)} custom-call(s32[4096]{0:T(1024)} %bitcast.52, s32[2]{0:T(128)S(1)} %pad_add_fusion.place_ref, bf16[4096,128]{1,0:T(8,128)(2,1)} %bitcast.40, f32[2048,128]{1,0:T(8,128)} %table_ref.1, f32[2048,128]{1,0:T(8,128)} %moment_ref.1, f32[128,8,128]{2,1,0:T(8,128)} %get-tuple-element.281.head_ref), custom_call_target="tpu_custom_call" | custom-call | tf_op jit(solution)/shard_map/pack/pallas_call | solution.py:172
  20.3 11.5 %all-to-all-start.3 = ((bf16[128,96,128]{2,1,0:T(8,128)(2,1)}), bf16[128,96,128]{2,1,0:T(8,128)(2,1)S(1)}, u32[]{:S(2)}, u32[]{:S(2)}) async-start(bf16[128,96,128]{2,1,0:T(8,128)(2,1)} %pack.5), calls=%async_computation.3 | async-start | bytes 6291456 | tf_op jit(solution)/shard_map/all_to_all | solution.py:471
  31.7 41.7 %all-to-all-done.3.state_ref.left_ref.right_ref = bf16[128,96,128]{2,1,0:T(8,128)(2,1)S(1)} async-done(((bf16[128,96,128]{2,1,0:T(8,128)(2,1)}), bf16[128,96,128]{2,1,0:T(8,128)(2,1)S(1)}, u32[]{:S(2)}, u32[]{:S(2)}) %all-to-all-start.3) | async-done | bytes 3145760 | tf_op jit(solution)/shard_map/all_to_all | solution.py:471
  73.4 8.2 %update.1 = (bf16[1024,128]{1,0:T(8,128)(2,1)}, f32[128,8,128]{2,1,0:T(8,128)}, s32[8,128]{1,0:T(8,128)}, f32[1024,256]{1,0:T(8,128)}, f32[128,128]{1,0:T(8,128)}, /*index=5*/s32[1]{0:T(128)}) custom-call(s32[1]{0:T(128)} %bitcast.5.core_ref, bf16[128,96,128]{2,1,0:T(8,128)(2,1)S(1)} %all-to-all-done.3.state_ref.left_ref.right_ref, ...), custom_call_target="tpu_custom_call" | custom-call | tf_op jit(solution)/shard_map/update/pallas_call | solution.py:313
  81.6 0.8 while.30
  82.5 0.0 copy-start.4
  82.5 0.0 copy-start.7
  82.5 4.6 %all-to-all-start.4 = ((f32[128,8,128]{2,1,0:T(8,128)}), f32[128,8,128]{2,1,0:T(8,128)S(1)}, u32[]{:S(2)}, u32[]{:S(2)}) async-start(f32[128,8,128]{2,1,0:T(8,128)} %get-tuple-element.287), calls=%async_computation.4 | async-start | bytes 1048576 | tf_op jit(solution)/shard_map/all_to_all | solution.py:471
  87.1 5.8 %reply.5 = bf16[128,64,128]{2,1,0:T(8,128)(2,1)} custom-call(f32[128,128]{1,0:T(8,128)} %get-tuple-element.291.line_ref, bf16[1024,128]{1,0:T(8,128)(2,1)} %get-tuple-element.545.own_ref.new_ref), custom_call_target="tpu_custom_call" | custom-call | tf_op jit(solution)/shard_map/reply/pallas_call | solution.py:404
  92.9 7.9 %all-to-all-done.4 = f32[128,8,128]{2,1,0:T(8,128)S(1)} async-done(((f32[128,8,128]{2,1,0:T(8,128)}), f32[128,8,128]{2,1,0:T(8,128)S(1)}, u32[]{:S(2)}, u32[]{:S(2)}) %all-to-all-start.4) | async-done | bytes 524320 | tf_op jit(solution)/shard_map/all_to_all | solution.py:471
  100.8 1.0 copy.27
  101.8 0.0 copy-done.4
  101.8 0.0 copy-done.7
  101.8 0.9 while.31
  102.6 0.0 copy-start.8
  102.7 0.0 copy-start.11
  102.7 0.0 copy-start.13
  102.7 5.7 %all-to-all-start.5 = ((bf16[128,64,128]{2,1,0:T(8,128)(2,1)}), bf16[128,64,128]{2,1,0:T(8,128)(2,1)}, u32[]{:S(2)}, u32[]{:S(2)}) async-start(bf16[128,64,128]{2,1,0:T(8,128)(2,1)} %reply.5), calls=%async_computation.5 | async-start | bytes 4194304 | tf_op jit(solution)/shard_map/all_to_all | solution.py:471
  108.3 0.0 copy-done.8
  108.4 0.0 copy-start.10
  108.4 0.0 copy-start.5
  108.4 0.0 copy-start.6
  108.4 1.4 collective-permute-start
  109.8 0.1 collective-permute-start.1
  109.9 0.0 copy-done.11
  109.9 0.4 collective-permute-start.2
  110.3 0.0 copy-done.13
  110.3 0.6 reshape.76.score_ref
  110.9 0.8 collective-permute-done.2.other_at_ref
  111.7 0.0 copy-start.12
  111.7 0.0 collective-permute-done.1.other_ref
  111.7 0.6 copy-done.12
  112.3 0.0 copy-start.9
  112.3 0.7 copy-done.9
  113.0 4.8 %place.1 = bf16[2048,128]{1,0:T(8,128)(2,1)} custom-call(bf16[2048,128]{1,0:T(8,128)(2,1)} %old_ref.1, bf16[1024,128]{1,0:T(8,128)(2,1)S(1)} %get-tuple-element.573, bf16[1024,128]{1,0:T(8,128)(2,1)} %copy-done.9, s32[8,128]{1,0:T(8,128)S(1)} %copy-done.11, s32[8,128]{1,0:T(8,128)} %copy-done.12), custom_call_target="tpu_custom_call" | custom-call | tf_op jit(solution)/shard_map/place/pallas_call | solution.py:496
  117.8 0.0 collective-permute-done
  117.8 1.3 maximum_select_fusion
  119.1 0.3 fusion.3
  119.5 0.6 select_reduce_fusion
  120.1 0.0 copy-done.10
  120.1 0.6 sqrt_add_fusion
  120.7 0.0 copy-done.5
  120.7 0.0 copy-done.6
  120.7 1.7 %subtract_select_fusion = (f32[2048,128]{1,0:T(8,128)}, f32[2048,128]{1,0:T(8,128)}) fusion(f32[2048,128]{1,0:T(8,128)S(1)} %copy-done.5, f32[2048]{0:T(1024)S(1)} %get-tuple-element.339, pred[2048]{0:T(1024)(128)(4,1)S(1)} %fusion.3, f32[2048,128]{1,0:T(8,128)S(1)} %copy-done.6, f32[2048,128]{1,0:T(8,128)S(1)} %maximum_select_fusion), kind=kLoop, calls=%fused_computation.6 | loop fusion | flops 2097152 | bytes 5253120 | tf_op jit(solution)/shard_map/jit(_where)/select_n | solution.py:575
  122.4 15.8 %all-to-all-done.5.left_ref.right_ref = bf16[128,64,128]{2,1,0:T(8,128)(2,1)} async-done(((bf16[128,64,128]{2,1,0:T(8,128)(2,1)}), bf16[128,64,128]{2,1,0:T(8,128)(2,1)}, u32[]{:S(2)}, u32[]{:S(2)}) %all-to-all-start.5) | async-done | bytes 2097184 | tf_op jit(solution)/shard_map/all_to_all | solution.py:471
  138.2 6.7 %score.1 = f32[1,128]{1,0:T(1,128)} custom-call(f32[128,128]{1,0:T(8,128)} %get-tuple-element.290.keys_ref, bf16[128,64,128]{2,1,0:T(8,128)(2,1)} %all-to-all-done.5.left_ref.right_ref, bf16[128,64,128]{2,1,0:T(8,128)(2,1)} %all-to-all-done.5.left_ref.right_ref, f32[512,128]{1,0:T(8,128)S(1)} %get-tuple-element.292.start_ref, bf16[512,1024]{1,0:T(8,128)(2,1)} %first_ref.1, ...), custom_call_target="tpu_custom_call" | custom-call | tf_op jit(solution)/shard_map/score/pallas_call | solution.py:455
  (4 shorter events, 0.1 us)
Async XLA Ops:
  20.3 53.1 %all-to-all-start.3 = ((bf16[128,96,128]{2,1,0:T(8,128)(2,1)}), bf16[128,96,128]{2,1,0:T(8,128)(2,1)S(1)}, u32[]{:S(2)}, u32[]{:S(2)}) async-start(bf16[128,96,128]{2,1,0:T(8,128)(2,1)} %pack.5), calls=%async_computation.3 | async-start | bytes 6291456 | tf_op jit(solution)/shard_map/all_to_all | solution.py:471
  82.5 19.3 %copy-start.4 = (s32[1024,128]{1,0:T(8,128)S(1)}, s32[1024,128]{1,0:T(8,128)}, u32[]{:S(2)}) copy-start(s32[1024,128]{1,0:T(8,128)} %get-tuple-element.570) | copy-start | bytes 1572868
  82.5 19.3 %copy-start.7 = (bf16[1024,128]{1,0:T(8,128)(2,1)S(1)}, bf16[1024,128]{1,0:T(8,128)(2,1)}, u32[]{:S(2)}) copy-start(bf16[1024,128]{1,0:T(8,128)(2,1)} %get-tuple-element.545.own_ref.new_ref) | copy-start | bytes 786436
  82.5 18.3 %all-to-all-start.4 = ((f32[128,8,128]{2,1,0:T(8,128)}), f32[128,8,128]{2,1,0:T(8,128)S(1)}, u32[]{:S(2)}, u32[]{:S(2)}) async-start(f32[128,8,128]{2,1,0:T(8,128)} %get-tuple-element.287), calls=%async_computation.4 | async-start | bytes 1048576 | tf_op jit(solution)/shard_map/all_to_all | solution.py:471
  102.6 5.7 %copy-start.8 = (f32[64,2,8,128]{3,0,1,2:T(8,128)S(1)}, f32[64,2,8,128]{3,0,1,2:T(8,128)}, u32[]{:S(2)}) copy-start(f32[64,2,8,128]{3,0,1,2:T(8,128)} %copy.27) | copy-start | bytes 1572868
  102.7 7.2 %copy-start.11 = (s32[8,128]{1,0:T(8,128)S(1)}, s32[8,128]{1,0:T(8,128)}, u32[]{:S(2)}) copy-start(s32[8,128]{1,0:T(8,128)} %get-tuple-element.289.own_at_ref) | copy-start | bytes 12292
  102.7 7.6 %copy-start.13 = (bf16[1024]{0:T(1024)(128)(2,1)S(1)}, bf16[1024]{0:T(1024)(128)(2,1)}, u32[]{:S(2)}) copy-start(bf16[1024]{0:T(1024)(128)(2,1)} %param.27) | copy-start | bytes 6148
  102.7 35.5 %all-to-all-start.5 = ((bf16[128,64,128]{2,1,0:T(8,128)(2,1)}), bf16[128,64,128]{2,1,0:T(8,128)(2,1)}, u32[]{:S(2)}, u32[]{:S(2)}) async-start(bf16[128,64,128]{2,1,0:T(8,128)(2,1)} %reply.5), calls=%async_computation.5 | async-start | bytes 4194304 | tf_op jit(solution)/shard_map/all_to_all | solution.py:471
  108.4 11.7 %copy-start.10 = (f32[2048]{0:T(1024)S(1)}, f32[2048]{0:T(1024)}, u32[]{:S(2)}) copy-start(f32[2048]{0:T(1024)} %param.23) | copy-start | bytes 24580
  108.4 12.3 %copy-start.5 = (f32[2048,128]{1,0:T(8,128)S(1)}, f32[2048,128]{1,0:T(8,128)}, u32[]{:S(2)}) copy-start(f32[2048,128]{1,0:T(8,128)} %get-tuple-element.571) | copy-start | bytes 3145732
  108.4 12.3 %copy-start.6 = (f32[2048,128]{1,0:T(8,128)S(1)}, f32[2048,128]{1,0:T(8,128)}, u32[]{:S(2)}) copy-start(f32[2048,128]{1,0:T(8,128)} %get-tuple-element.572) | copy-start | bytes 3145732
  108.4 9.3 %collective-permute-start = (f32[1024,128]{1,0:T(8,128)S(1)}, f32[1024,128]{1,0:T(8,128)}, u32[]{:S(2)}, u32[]{:S(2)}) collective-permute-start(f32[1024,128]{1,0:T(8,128)S(1)} %bitcast.45), channel_id=1, source_target_pairs={{0,1},{1,0},{2,3},{3,2},{4,5},{5,4},{6,7},{7,6},{8,9},{9,8},{10,11... | collective-permute-start | bytes 1572872 | tf_op jit(solution)/shard_map/ppermute | solution.py:567
  109.8 1.9 %collective-permute-start.1 = (bf16[1024,128]{1,0:T(8,128)(2,1)S(1)}, bf16[1024,128]{1,0:T(8,128)(2,1)S(1)}, u32[]{:S(2)}, u32[]{:S(2)}) collective-permute-start(bf16[1024,128]{1,0:T(8,128)(2,1)S(1)} %get-tuple-element.573), channel_id=1, source_target_pairs={{0,1},{1,0},{2,3},{3,2},{4,5},{5,4},{6,7},{7,6},{8,9},{9,8},{10,11... | collective-permute-start | bytes 786440 | tf_op jit(solution)/shard_map/ppermute | solution.py:560
  109.9 1.8 %collective-permute-start.2 = (s32[8,128]{1,0:T(8,128)S(1)}, s32[8,128]{1,0:T(8,128)S(1)}, u32[]{:S(2)}, u32[]{:S(2)}) collective-permute-start(s32[8,128]{1,0:T(8,128)S(1)} %copy-done.11), channel_id=1, source_target_pairs={{0,1},{1,0},{2,3},{3,2},{4,5},{5,4},{6,7},{7,6},{8,9},{9,8},{10,11... | collective-permute-start | bytes 12296 | tf_op jit(solution)/shard_map/ppermute | solution.py:561
  111.7 0.6 copy-start.12
  112.3 0.7 copy-start.9

commit v5 on v4

--- a/solution.py
+++ b/solution.py
@@ -502,6 +502,23 @@
     )(old, own, other, own_at, other_at)
 
 
+def send_home(value, owner):
+    value = value.reshape(4, 4, 4, -1, LANES)
+    for axis, unit in enumerate((16, 4, 1)):
+        digit = (owner // unit) % 4
+        out = value
+        for k in range(1, 4):
+            piece = lax.dynamic_index_in_dim(value, (digit + k) % 4, axis, keepdims=True)
+            pairs = []
+            for s in range(64):
+                d = (s // unit) % 4
+                pairs.append((s, s + ((d + k) % 4 - d) * unit))
+            piece = lax.ppermute(piece, "shard", pairs)
+            out = lax.dynamic_update_slice_in_dim(out, piece, (digit - k) % 4, axis)
+        value = out
+    return value.reshape(64, -1, LANES)
+
+
 def per_device(
     touched_ids,
     bag_lengths,
@@ -522,7 +539,6 @@
     tab_rows, row_width = table.shape
     samples, bag = touched_ids.shape
     swap = [(0, 1), (1, 0)]
-    odd = owner % 2 == 1
     rows_here = tab_rows // 2
 
     ids = jnp.concatenate([touched_ids, bag_lengths], axis=1).T
@@ -554,20 +570,18 @@
         lambda c: c[0] < rounds, more_sums, (one, acc, new_rows, sums, places)
     )
 
-    back = exchange(sums)
-    answer = exchange(reply(line, new_rows))
+    found = reply(line, new_rows)
+    answer = exchange(found)
 
     other_rows = lax.ppermute(new_rows, "rep", swap)
     other_places = lax.ppermute(places, "rep", swap)
     serving_table = place_rows(serving_old, new_rows, other_rows, places, other_places)
 
-    back = back.reshape(owners, 2, 8, row_width)
-    back = jnp.where(odd, back[:, ::-1], back)
-    half = back.transpose(2, 1, 0, 3).reshape(rows_here, row_width)
+    half = send_home(sums, owner).transpose(1, 0, 2)
     other = lax.ppermute(half, "rep", swap)
-    grad_sum = jnp.where(
-        rep == 0, jnp.concatenate([half, other]), jnp.concatenate([other, half])
-    )
+    even = (rep + owner) % 2 == 0
+    grad_sum = jnp.stack([jnp.where(even, half, other), jnp.where(even, other, half)], axis=1)
+    grad_sum = grad_sum.reshape(tab_rows, row_width)
     touched = grad_sum[:, :1] < 0.5 * UNTOUCHED
     new_moment = jnp.where(touched, beta_one * moment + (1.0 - beta_one) * grad_sum, moment)
     mean = jnp.mean(jnp.where(touched, grad_sum * grad_sum, 0.0), axis=1)

time: 146 us -> 181 us (1.24)
  local copies, waits for them, and re-layouts: 3.92 us -> 18.7 us
  waiting for transfers between devices: 66.2 us -> 77.5 us
  starting transfers between devices: 23.6 us -> 30.5 us
  other arithmetic: 6.18 us -> 8.5 us
    ppermute x0 -> x9, waiting for transfers between devices: none -> 23.1 us  [send_home(): piece = lax.ppermute(piece, 'shard', pairs)]
    all_to_all x3 -> x2, waiting for transfers between devices: 65.4 us -> 53.9 us  [exchange(): return lax.all_to_all(value, ALL, 0, 0, tiled=True)]
    dynamic_slice x0 -> x6, local copies, waits for them, and re-layouts: none -> 7.75 us  [send_home(): lax.dynamic_index_in_dim(value, (digit + k) % 4, axis, keepdims=True)]
    ppermute x1, starting transfers between devices: 1.36 us -> 8.02 us  [per_device(): other = lax.ppermute(half, 'rep', swap)]
    dynamic_update_slice x0 -> x7, local copies, waits for them, and re-layouts: none -> 6.03 us  [send_home(): out = lax.dynamic_update_slice_in_dim(out, piece, (digit - k) % 4, axis)]
    all_to_all x3 -> x2, starting transfers between devices: 21.7 us -> 17.3 us  [exchange(): return lax.all_to_all(value, ALL, 0, 0, tiled=True)]
    ppermute x0 -> x9, starting transfers between devices: none -> 3.9 us  [send_home(): piece = lax.ppermute(piece, 'shard', pairs)]
  transfers between devices with their start and end apart: 6 -> 14, of which waited for: 4 -> 8; matrix products, arithmetic and copies ran while one was open for 4% -> 5% of each run, Pallas kernels for 7% -> 6%
where the time goes in v5:
time: 181 us; the launch traced here: 180 us
  waiting for transfers between devices  77.5 us (43%)
  Pallas kernels  42.4 us (23%)
  starting transfers between devices  30.5 us (17%)
  local copies, waits for them, and re-layouts  18.7 us (10%)
  other arithmetic  8.5 us (5%)
    all_to_all x2, waiting for transfers between devices, exchange(): return lax.all_to_all(value, ALL, 0, 0, tiled=True)  53.9 us
    ppermute x9, waiting for transfers between devices, send_home(): piece = lax.ppermute(piece, 'shard', pairs)  23.1 us
    all_to_all x2, starting transfers between devices, exchange(): return lax.all_to_all(value, ALL, 0, 0, tiled=True)  17.3 us
    pallas_call x1, Pallas kernels, pack(): pl.pallas_call(pack_kernel, in_specs=[pl.BlockSpec(memory_space=pltpu.SME...  8.97 us
    pallas_call x1, Pallas kernels, update(): pl.pallas_call(update_kernel, grid=(STEPS,), in_specs=[pl.BlockSpec(memor...  8.21 us
    pallas_call x1, Pallas kernels, route(): pl.pallas_call(route_kernel, in_specs=[pl.BlockSpec(memory_space=pltpu.SM...  8.1 us
    ppermute x1, starting transfers between devices, per_device(): other = lax.ppermute(half, 'rep', swap)  8.02 us
    dynamic_slice x6, local copies, waits for them, and re-layouts, send_home(): lax.dynamic_index_in_dim(value, (digit + k) % 4, axis, keepdims=True)  7.75 us
  transfers between devices with their start and end apart: 14, of which 8 were waited for; matrix products, arithmetic and copies ran while one was open for 5% of the time, Pallas kernels for 6%

profile of v5, /device:TPU:1, one launch (start us, length us, event | category | flops | bytes accessed | tf_op | source)
XLA Modules:
  0.0 180.3 jit_solution(12167351918692791629)
XLA Ops:
  0.6 0.7 fusion.5
  1.3 0.1 reshape.81
  1.4 0.8 reshape.80
  2.2 0.1 copy.26
  2.3 0.1 pad_add_fusion.place_ref
  2.4 0.1 concatenate.11.extra_ref
  2.5 0.7 add_bitcast_fusion.1.ids_ref
  3.2 8.1 %route.9 = (s32[32,128]{1,0:T(8,128)}, f32[128,128]{1,0:T(8,128)}, f32[128,8,128]{2,1,0:T(8,128)}) custom-call(s32[1]{0:T(128)} %constant.233.clone.1.round_ref, s32[36,128]{1,0:T(8,128)S(1)} %add_bitcast_fusion.1.ids_ref, s32[1024,128]{1,0:T(8,128)} %bitcast.47, f32[128,128]{1,0:T(8,128)S(1)} %concatenate.11.extra_ref), custom_call_target="tpu_custom_call" | custom-call | tf_op jit(solution)/shard_map/route/pallas_call | solution.py:110
  11.3 9.0 %pack.5 = bf16[128,96,128]{2,1,0:T(8,128)(2,1)} custom-call(s32[4096]{0:T(1024)} %bitcast.61, s32[2]{0:T(128)S(1)} %pad_add_fusion.place_ref, bf16[4096,128]{1,0:T(8,128)(2,1)} %bitcast.49, f32[2048,128]{1,0:T(8,128)} %table_ref.1, f32[2048,128]{1,0:T(8,128)} %moment_ref.1, f32[128,8,128]{2,1,0:T(8,128)} %get-tuple-element.281.head_ref), custom_call_target="tpu_custom_call" | custom-call | tf_op jit(solution)/shard_map/pack/pallas_call | solution.py:172
  20.3 11.5 %all-to-all-start.3 = ((bf16[128,96,128]{2,1,0:T(8,128)(2,1)}), bf16[128,96,128]{2,1,0:T(8,128)(2,1)S(1)}, u32[]{:S(2)}, u32[]{:S(2)}) async-start(bf16[128,96,128]{2,1,0:T(8,128)(2,1)} %pack.5), calls=%async_computation.3 | async-start | bytes 6291456 | tf_op jit(solution)/shard_map/all_to_all | solution.py:471
  31.8 41.6 %all-to-all-done.3.state_ref.left_ref.right_ref = bf16[128,96,128]{2,1,0:T(8,128)(2,1)S(1)} async-done(((bf16[128,96,128]{2,1,0:T(8,128)(2,1)}), bf16[128,96,128]{2,1,0:T(8,128)(2,1)S(1)}, u32[]{:S(2)}, u32[]{:S(2)}) %all-to-all-start.3) | async-done | bytes 3145760 | tf_op jit(solution)/shard_map/all_to_all | solution.py:471
  73.4 8.2 %update.1 = (bf16[1024,128]{1,0:T(8,128)(2,1)}, f32[128,8,128]{2,1,0:T(8,128)}, s32[8,128]{1,0:T(8,128)}, f32[1024,256]{1,0:T(8,128)}, f32[128,128]{1,0:T(8,128)}, /*index=5*/s32[1]{0:T(128)}) custom-call(s32[1]{0:T(128)} %bitcast.5.core_ref, bf16[128,96,128]{2,1,0:T(8,128)(2,1)S(1)} %all-to-all-done.3.state_ref.left_ref.right_ref, ...), custom_call_target="tpu_custom_call" | custom-call | tf_op jit(solution)/shard_map/update/pallas_call | solution.py:313
  81.7 0.8 while.30
  82.5 0.0 copy-start.7
  82.5 1.0 constant_dynamic-slice_fusion.8
  83.4 0.1 collective-permute-start
  83.6 5.0 %collective-permute-done = f32[1,4,4,16,128]{4,3,2,1,0:T(8,128)S(1)} collective-permute-done((f32[1,4,4,16,128]{4,3,2,1,0:T(8,128)S(1)}, f32[1,4,4,16,128]{4,3,2,1,0:T(8,128)S(1)}, u32[]{:S(2)}, u32[]{:S(2)}) %collective-permute-start) | collective-permute-done | bytes 131104 | tf_op jit(solution)/shard_map/ppermute | solution.py:516
  88.5 1.7 constant_dynamic-slice_fusion.6
  90.2 1.2 collective-permute-start.2
  91.4 4.1 %collective-permute-done.1 = f32[1,4,4,16,128]{4,3,2,1,0:T(8,128)S(1)} collective-permute-done((f32[1,4,4,16,128]{4,3,2,1,0:T(8,128)S(1)}, f32[1,4,4,16,128]{4,3,2,1,0:T(8,128)S(1)}, u32[]{:S(2)}, u32[]{:S(2)}) %collective-permute-start.1) | collective-permute-done | bytes 131104 | tf_op jit(solution)/shard_map/ppermute | solution.py:516
  95.5 0.7 constant_dynamic-update-slice_fusion.7
  96.2 0.7 constant_dynamic-update-slice_fusion.6
  96.8 0.9 constant_dynamic-slice_fusion.5
  97.8 0.1 collective-permute-start.3
  97.9 5.0 %collective-permute-done.3 = f32[4,1,4,16,128]{4,3,2,1,0:T(8,128)S(1)} collective-permute-done((f32[4,1,4,16,128]{4,3,2,1,0:T(8,128)S(1)}, f32[4,1,4,16,128]{4,3,2,1,0:T(8,128)S(1)}, u32[]{:S(2)}, u32[]{:S(2)}) %collective-permute-start.3) | collective-permute-done | bytes 131104 | tf_op jit(solution)/shard_map/ppermute | solution.py:516
  102.9 1.7 constant_dynamic-slice_fusion.3
  104.5 0.1 collective-permute-start.4
  104.6 1.1 collective-permute-start.5
  105.8 4.1 %collective-permute-done.4 = f32[4,1,4,16,128]{4,3,2,1,0:T(8,128)S(1)} collective-permute-done((f32[4,1,4,16,128]{4,3,2,1,0:T(8,128)S(1)}, f32[4,1,4,16,128]{4,3,2,1,0:T(8,128)S(1)}, u32[]{:S(2)}, u32[]{:S(2)}) %collective-permute-start.4) | collective-permute-done | bytes 131104 | tf_op jit(solution)/shard_map/ppermute | solution.py:516
  109.8 0.7 constant_dynamic-update-slice_fusion.4
  110.5 0.7 constant_dynamic-update-slice_fusion.3
  111.2 0.9 constant_dynamic-slice_fusion.2
  112.1 0.1 collective-permute-start.6
  112.2 5.0 %collective-permute-done.6 = f32[4,4,1,16,128]{4,3,2,1,0:T(8,128)S(1)} collective-permute-done((f32[4,4,1,16,128]{4,3,2,1,0:T(8,128)S(1)}, f32[4,4,1,16,128]{4,3,2,1,0:T(8,128)S(1)}, u32[]{:S(2)}, u32[]{:S(2)}) %collective-permute-start.6) | collective-permute-done | bytes 131104 | tf_op jit(solution)/shard_map/ppermute | solution.py:516
  117.2 1.7 constant_dynamic-slice_fusion
  118.8 1.2 collective-permute-start.8
  120.0 5.7 %reply.5 = bf16[128,64,128]{2,1,0:T(8,128)(2,1)} custom-call(f32[128,128]{1,0:T(8,128)} %get-tuple-element.291.line_ref, bf16[1024,128]{1,0:T(8,128)(2,1)S(1)} %copy-done.7), custom_call_target="tpu_custom_call" | custom-call | tf_op jit(solution)/shard_map/reply/pallas_call | solution.py:404
  125.7 0.7 constant_dynamic-update-slice_fusion.1
  126.4 0.7 constant_dynamic-update-slice_fusion
  127.0 2.0 %copy.27 = f32[4,4,4,16,128]{4,2,1,0,3:T(4,128)} copy(f32[4,4,4,16,128]{4,3,2,1,0:T(8,128)} %constant_dynamic-update-slice_fusion) | data formatting | bytes 1048576 | tf_op jit(solution)/shard_map/dynamic_update_slice | solution.py:517
  129.1 8.0 %collective-permute-start.9 = (f32[16,64,128]{2,1,0:T(8,128)}, f32[16,64,128]{2,1,0:T(8,128)}, u32[]{:S(2)}, u32[]{:S(2)}) collective-permute-start(f32[16,64,128]{2,1,0:T(8,128)} %bitcast.17), channel_id=1, source_target_pairs={{0,1},{1,0},{2,3},{3,2},{4,5},{5,4},{6,7},{7,6},{8,9},{9,8},{10,11... | collective-permute-start | bytes 1572872 | tf_op jit(solution)/shard_map/ppermute | solution.py:581
  137.1 0.8 while.31
  138.0 0.0 copy-start.13
  138.0 5.8 %all-to-all-start.4 = ((bf16[128,64,128]{2,1,0:T(8,128)(2,1)}), bf16[128,64,128]{2,1,0:T(8,128)(2,1)}, u32[]{:S(2)}, u32[]{:S(2)}) async-start(bf16[128,64,128]{2,1,0:T(8,128)(2,1)} %reply.5), calls=%async_computation.4 | async-start | bytes 4194304 | tf_op jit(solution)/shard_map/all_to_all | solution.py:471
  143.8 1.2 collective-permute-start.10
  145.0 0.1 collective-permute-start.11
  145.1 0.6 reshape.88.score_ref
  145.7 0.5 collective-permute-done.11.other_at_ref
  146.2 0.6 copy-done.12
  146.8 0.7 copy-done.10
  147.5 4.8 %place.1 = bf16[2048,128]{1,0:T(8,128)(2,1)} custom-call(bf16[2048,128]{1,0:T(8,128)(2,1)} %old_ref.1, bf16[1024,128]{1,0:T(8,128)(2,1)S(1)} %get-tuple-element.584, bf16[1024,128]{1,0:T(8,128)(2,1)} %copy-done.10, s32[8,128]{1,0:T(8,128)S(1)} %copy-done.13, s32[8,128]{1,0:T(8,128)} %copy-done.12), custom_call_target="tpu_custom_call" | custom-call | tf_op jit(solution)/shard_map/place/pallas_call | solution.py:496
  152.3 1.4 select_bitcast_fusion.1
  153.7 0.0 copy-start.9
  153.7 0.8 copy-done.9
  154.5 0.1 pad_maximum_fusion
  154.6 1.0 copy-done.8
  155.6 0.3 fusion.3
  156.0 0.1 broadcast_in_dim.41
  156.0 1.8 select_reduce_fusion
  157.8 0.1 mul.54
  157.9 0.6 sqrt_add_fusion
  158.5 2.7 %subtract_select_fusion = (f32[2048,128]{1,0:T(8,128)}, f32[2048,128]{1,0:T(8,128)}) fusion(f32[2048,128]{1,0:T(8,128)S(1)} %copy-done.5, f32[2048]{0:T(1024)S(1)} %get-tuple-element.339, pred[2048]{0:T(1024)(128)(4,1)S(1)} %fusion.3, f32[2048,128]{1,0:T(8,128)S(1)} %copy-done.6, f32[16,2,64,128]{3,2,1,0:T(8,128)} %copy-done.8), kind=kLoop, calls=%fused_computation.6 | loop fusion | flops 2097152 | bytes 5253120 | tf_op jit(solution)/shard_map/jit(_where)/select_n | solution.py:589
  161.2 12.3 %all-to-all-done.4.left_ref.right_ref = bf16[128,64,128]{2,1,0:T(8,128)(2,1)} async-done(((bf16[128,64,128]{2,1,0:T(8,128)(2,1)}), bf16[128,64,128]{2,1,0:T(8,128)(2,1)}, u32[]{:S(2)}, u32[]{:S(2)}) %all-to-all-start.4) | async-done | bytes 2097184 | tf_op jit(solution)/shard_map/all_to_all | solution.py:471
  173.6 6.7 %score.1 = f32[1,128]{1,0:T(1,128)} custom-call(f32[128,128]{1,0:T(8,128)} %get-tuple-element.290.keys_ref, bf16[128,64,128]{2,1,0:T(8,128)(2,1)} %all-to-all-done.4.left_ref.right_ref, bf16[128,64,128]{2,1,0:T(8,128)(2,1)} %all-to-all-done.4.left_ref.right_ref, f32[512,128]{1,0:T(8,128)S(1)} %get-tuple-element.292.start_ref, bf16[512,1024]{1,0:T(8,128)(2,1)} %first_ref.1, ...), custom_call_target="tpu_custom_call" | custom-call | tf_op jit(solution)/shard_map/score/pallas_call | solution.py:455
  (27 shorter events, 0.1 us)
Async XLA Ops:
  20.3 53.2 %all-to-all-start.3 = ((bf16[128,96,128]{2,1,0:T(8,128)(2,1)}), bf16[128,96,128]{2,1,0:T(8,128)(2,1)S(1)}, u32[]{:S(2)}, u32[]{:S(2)}) async-start(bf16[128,96,128]{2,1,0:T(8,128)(2,1)} %pack.5), calls=%async_computation.3 | async-start | bytes 6291456 | tf_op jit(solution)/shard_map/all_to_all | solution.py:471
  82.5 37.6 %copy-start.7 = (bf16[1024,128]{1,0:T(8,128)(2,1)S(1)}, bf16[1024,128]{1,0:T(8,128)(2,1)}, u32[]{:S(2)}) copy-start(bf16[1024,128]{1,0:T(8,128)(2,1)} %get-tuple-element.556.own_ref.new_ref) | copy-start | bytes 786436
  83.4 5.1 %collective-permute-start = (f32[1,4,4,16,128]{4,3,2,1,0:T(8,128)S(1)}, f32[1,4,4,16,128]{4,3,2,1,0:T(8,128)S(1)}, u32[]{:S(2)}, u32[]{:S(2)}) collective-permute-start(f32[1,4,4,16,128]{4,3,2,1,0:T(8,128)S(1)} %constant_dynamic-slice_fusion.8), channel_id=1, source_target_pairs={{0,32},{2,34},{4,36},{6,38},{8,40},{10,42},{12,44},{14,46},{16,48}... | collective-permute-start | bytes 393224 | tf_op jit(solution)/shard_map/ppermute | solution.py:516
  90.2 5.3 %collective-permute-start.1 = (f32[1,4,4,16,128]{4,3,2,1,0:T(8,128)S(1)}, f32[1,4,4,16,128]{4,3,2,1,0:T(8,128)S(1)}, u32[]{:S(2)}, u32[]{:S(2)}) collective-permute-start(f32[1,4,4,16,128]{4,3,2,1,0:T(8,128)S(1)} %get-tuple-element.352), channel_id=1, source_target_pairs={{0,64},{2,66},{4,68},{6,70},{8,72},{10,74},{12,76},{14,78},{16,80}... | collective-permute-start | bytes 393224 | tf_op jit(solution)/shard_map/ppermute | solution.py:516
  90.2 6.0 %collective-permute-start.2 = (f32[1,4,4,16,128]{4,3,2,1,0:T(8,128)S(1)}, f32[1,4,4,16,128]{4,3,2,1,0:T(8,128)S(1)}, u32[]{:S(2)}, u32[]{:S(2)}) collective-permute-start(f32[1,4,4,16,128]{4,3,2,1,0:T(8,128)S(1)} %get-tuple-element.351), channel_id=1, source_target_pairs={{0,96},{2,98},{4,100},{6,102},{8,104},{10,106},{12,108},{14,110},{... | collective-permute-start | bytes 393224 | tf_op jit(solution)/shard_map/ppermute | solution.py:516
  97.8 5.1 %collective-permute-start.3 = (f32[4,1,4,16,128]{4,3,2,1,0:T(8,128)S(1)}, f32[4,1,4,16,128]{4,3,2,1,0:T(8,128)S(1)}, u32[]{:S(2)}, u32[]{:S(2)}) collective-permute-start(f32[4,1,4,16,128]{4,3,2,1,0:T(8,128)S(1)} %constant_dynamic-slice_fusion.5), channel_id=1, source_target_pairs={{0,8},{2,10},{4,12},{6,14},{8,16},{10,18},{12,20},{14,22},{16,24},... | collective-permute-start | bytes 393224 | tf_op jit(solution)/shard_map/ppermute | solution.py:516
  104.5 32.6 %copy-start.4 = (s32[1024,128]{1,0:T(8,128)S(1)}, s32[1024,128]{1,0:T(8,128)}, u32[]{:S(2)}) copy-start(s32[1024,128]{1,0:T(8,128)} %get-tuple-element.581) | copy-start | bytes 1572868
  104.5 5.3 %collective-permute-start.4 = (f32[4,1,4,16,128]{4,3,2,1,0:T(8,128)S(1)}, f32[4,1,4,16,128]{4,3,2,1,0:T(8,128)S(1)}, u32[]{:S(2)}, u32[]{:S(2)}) collective-permute-start(f32[4,1,4,16,128]{4,3,2,1,0:T(8,128)S(1)} %get-tuple-element.349), channel_id=1, source_target_pairs={{0,16},{2,18},{4,20},{6,22},{8,24},{10,26},{12,28},{14,30},{16,0},... | collective-permute-start | bytes 393224 | tf_op jit(solution)/shard_map/ppermute | solution.py:516
  104.6 5.9 %collective-permute-start.5 = (f32[4,1,4,16,128]{4,3,2,1,0:T(8,128)S(1)}, f32[4,1,4,16,128]{4,3,2,1,0:T(8,128)S(1)}, u32[]{:S(2)}, u32[]{:S(2)}) collective-permute-start(f32[4,1,4,16,128]{4,3,2,1,0:T(8,128)S(1)} %get-tuple-element.348), channel_id=1, source_target_pairs={{0,24},{2,26},{4,28},{6,30},{8,0},{10,2},{12,4},{14,6},{16,8},{18,... | collective-permute-start | bytes 393224 | tf_op jit(solution)/shard_map/ppermute | solution.py:516
  112.1 5.1 %collective-permute-start.6 = (f32[4,4,1,16,128]{4,3,2,1,0:T(8,128)S(1)}, f32[4,4,1,16,128]{4,3,2,1,0:T(8,128)S(1)}, u32[]{:S(2)}, u32[]{:S(2)}) collective-permute-start(f32[4,4,1,16,128]{4,3,2,1,0:T(8,128)S(1)} %constant_dynamic-slice_fusion.2), channel_id=1, source_target_pairs={{0,2},{2,4},{4,6},{6,0},{8,10},{10,12},{12,14},{14,8},{16,18},{18,... | collective-permute-start | bytes 393224 | tf_op jit(solution)/shard_map/ppermute | solution.py:516
  118.8 6.9 %collective-permute-start.7 = (f32[4,4,1,16,128]{4,3,2,1,0:T(8,128)S(1)}, f32[4,4,1,16,128]{4,3,2,1,0:T(8,128)S(1)}, u32[]{:S(2)}, u32[]{:S(2)}) collective-permute-start(f32[4,4,1,16,128]{4,3,2,1,0:T(8,128)S(1)} %get-tuple-element.346), channel_id=1, source_target_pairs={{0,4},{2,6},{4,0},{6,2},{8,12},{10,14},{12,8},{14,10},{16,20},{18,... | collective-permute-start | bytes 393224 | tf_op jit(solution)/shard_map/ppermute | solution.py:516
  118.8 7.5 %collective-permute-start.8 = (f32[4,4,1,16,128]{4,3,2,1,0:T(8,128)S(1)}, f32[4,4,1,16,128]{4,3,2,1,0:T(8,128)S(1)}, u32[]{:S(2)}, u32[]{:S(2)}) collective-permute-start(f32[4,4,1,16,128]{4,3,2,1,0:T(8,128)S(1)} %get-tuple-element.345), channel_id=1, source_target_pairs={{0,6},{2,0},{4,2},{6,4},{8,14},{10,8},{12,10},{14,12},{16,22},{18,... | collective-permute-start | bytes 393224 | tf_op jit(solution)/shard_map/ppermute | solution.py:516
  129.1 23.2 %collective-permute-start.9 = (f32[16,64,128]{2,1,0:T(8,128)}, f32[16,64,128]{2,1,0:T(8,128)}, u32[]{:S(2)}, u32[]{:S(2)}) collective-permute-start(f32[16,64,128]{2,1,0:T(8,128)} %bitcast.17), channel_id=1, source_target_pairs={{0,1},{1,0},{2,3},{3,2},{4,5},{5,4},{6,7},{7,6},{8,9},{9,8},{10,11... | collective-permute-start | bytes 1572872 | tf_op jit(solution)/shard_map/ppermute | solution.py:581
  138.0 7.1 %copy-start.13 = (s32[8,128]{1,0:T(8,128)S(1)}, s32[8,128]{1,0:T(8,128)}, u32[]{:S(2)}) copy-start(s32[8,128]{1,0:T(8,128)} %get-tuple-element.289.own_at_ref) | copy-start | bytes 12292
  138.0 7.2 %copy-start.14 = (bf16[1024]{0:T(1024)(128)(2,1)S(1)}, bf16[1024]{0:T(1024)(128)(2,1)}, u32[]{:S(2)}) copy-start(bf16[1024]{0:T(1024)(128)(2,1)} %param.27) | copy-start | bytes 6148
  138.0 35.6 %all-to-all-start.4 = ((bf16[128,64,128]{2,1,0:T(8,128)(2,1)}), bf16[128,64,128]{2,1,0:T(8,128)(2,1)}, u32[]{:S(2)}, u32[]{:S(2)}) async-start(bf16[128,64,128]{2,1,0:T(8,128)(2,1)} %reply.5), calls=%async_computation.4 | async-start | bytes 4194304 | tf_op jit(solution)/shard_map/all_to_all | solution.py:471
  143.8 2.4 %collective-permute-start.10 = (bf16[1024,128]{1,0:T(8,128)(2,1)S(1)}, bf16[1024,128]{1,0:T(8,128)(2,1)S(1)}, u32[]{:S(2)}, u32[]{:S(2)}) collective-permute-start(bf16[1024,128]{1,0:T(8,128)(2,1)S(1)} %get-tuple-element.584), channel_id=1, source_target_pairs={{0,1},{1,0},{2,3},{3,2},{4,5},{5,4},{6,7},{7,6},{8,9},{9,8},{10,11... | collective-permute-start | bytes 786440 | tf_op jit(solution)/shard_map/ppermute | solution.py:576
  145.0 1.2 collective-permute-start.11
  146.2 0.6 copy-start.12
  146.8 0.7 copy-start.10
  152.3 5.7 %copy-start.11 = (f32[2048]{0:T(1024)S(1)}, f32[2048]{0:T(1024)}, u32[]{:S(2)}) copy-start(f32[2048]{0:T(1024)} %param.23) | copy-start | bytes 24580
  152.3 6.3 %copy-start.5 = (f32[2048,128]{1,0:T(8,128)S(1)}, f32[2048,128]{1,0:T(8,128)}, u32[]{:S(2)}) copy-start(f32[2048,128]{1,0:T(8,128)} %get-tuple-element.582) | copy-start | bytes 3145732
  152.3 6.3 %copy-start.6 = (f32[2048,128]{1,0:T(8,128)S(1)}, f32[2048,128]{1,0:T(8,128)}, u32[]{:S(2)}) copy-start(f32[2048,128]{1,0:T(8,128)} %get-tuple-element.583) | copy-start | bytes 3145732
  153.7 0.8 copy-start.9
  154.6 1.0 copy-start.8

commit v6 on v4

--- a/solution.py
+++ b/solution.py
@@ -37,8 +37,10 @@
     return jnp.where(place == index, jnp.bfloat16(1), jnp.bfloat16(0))
 
 
-def route_kernel(round_ref, ids_ref, map_ref, extra_ref, slots_ref, keys_ref, row_ref):
-    bag, samples = ids_ref.shape[0] - 4, ids_ref.shape[1]
+def route_kernel(
+    round_ref, ids_ref, lengths_ref, map_ref, var_ref, serve_ref, slots_ref, keys_ref, row_ref
+):
+    bag, samples = ids_ref.shape
     step = 4
     wide = step * samples
     first = round_ref[0] * ROUND
@@ -50,7 +52,7 @@
     ends = []
     total = jnp.zeros((1, samples), I32)
     for f in range(3):
-        total = total + ids_ref[bag + f : bag + f + 1, :]
+        total = total + lengths_ref[f : f + 1, :]
         ends.append(total)
     sample = iota((1, samples), 1)
     seen = jnp.zeros((DEVS, 1), F32)
@@ -95,35 +97,61 @@
     keys_ref[...] = layout[:, :LANES] * 32.0 + layout[:, LANES:] - 1.0
     most = jnp.max(seen, axis=0, keepdims=True).astype(I32)
     rounds = ((most + ROUND - 1) // ROUND).astype(F32)
-    extra = extra_ref[...]
-    coarse = extra.astype(BF16).astype(F32)
+    var = var_ref[...]
+    spot = (serve_ref[...] & (var.shape[0] * LANES - 1)).astype(F32)
+    blank = jnp.zeros((ROUND, LANES), F32)
+    sides = [var, pltpu.roll(var, ROUND, 1), spot, pltpu.roll(spot, ROUND, 1)]
+    extra = jnp.concatenate([blank] + sides, axis=0).T
+    coarse = extra.astype(BF16)
+    fine = (extra - coarse.astype(F32)).astype(BF16)
+    twice = one_hot((iota((DEVS, DEVS), 0) >> 1) == iota((DEVS, DEVS), 1))
+    coarse = jnp.dot(twice, coarse, preferred_element_type=F32)
+    fine = jnp.dot(twice, fine, preferred_element_type=F32)
     index = iota((DEVS, LANES), 1) < ROUND
     high = jnp.where(index, layout[:, :LANES], coarse)
-    low = jnp.where(index, layout[:, LANES:], extra - coarse)
+    low = jnp.where(index, layout[:, LANES:], fine)
     row_ref[:, 0:1, :] = high.reshape(DEVS, 1, LANES)
     row_ref[:, 1:2, :] = low.reshape(DEVS, 1, LANES)
     row_ref[:, 2:8, :] = jnp.broadcast_to(rounds.reshape(1, 1, 1), (DEVS, 6, LANES))
 
 
-def route(round_index, ids, train_map, extra):
-    bag = ids.shape[0] - 4
+def route(round_index, ids, lengths, train_map, var, serve):
     return pl.pallas_call(
         route_kernel,
         in_specs=[pl.BlockSpec(memory_space=pltpu.SMEM)]
-        + [pl.BlockSpec(memory_space=pltpu.VMEM)] * 3,
+        + [pl.BlockSpec(memory_space=pltpu.VMEM)] * 5,
         out_specs=[pl.BlockSpec(memory_space=pltpu.VMEM)] * 3,
         out_shape=(
-            jax.ShapeDtypeStruct((bag, ids.shape[1]), I32),
+            jax.ShapeDtypeStruct(ids.shape, I32),
             jax.ShapeDtypeStruct((DEVS, LANES), F32),
             jax.ShapeDtypeStruct((DEVS, 8, LANES), F32),
         ),
         name="route",
-    )(round_index, ids, train_map, extra)
+    )(round_index, ids, lengths, train_map, var, serve)
 
 
 def pack_kernel(
-    slots_ref, place_ref, grads_ref, table_ref, moment_ref, head_ref, out_ref, from_ref, to_ref
+    slots_ref,
+    place_ref,
+    grads_ref,
+    table_from_ref,
+    moment_from_ref,
+    head_ref,
+    out_ref,
+    from_ref,
+    to_ref,
+    table_ref,
+    moment_ref,
+    sems,
 ):
+    half, odd = place_ref[0], place_ref[1]
+    mine = pl.ds(pl.multiple_of(half * table_ref.shape[0], 8), table_ref.shape[0])
+    copies = [
+        pltpu.make_async_copy(table_from_ref.at[mine], table_ref, sems.at[0]),
+        pltpu.make_async_copy(moment_from_ref.at[mine], moment_ref, sems.at[1]),
+    ]
+    for copy in copies:
+        copy.start()
     count = slots_ref.shape[0]
     bag = 32
     samples = count // bag
@@ -143,11 +171,8 @@
             to_ref[pl.ds(slot, 1), :] = from_ref[pl.ds(first + u * bag, 1), :]
         return carry
 
-    half, odd = place_ref[0], place_ref[1]
-
     def rows_of(ref, i):
-        base = half * (ref.shape[0] // 2) + i * 4
-        starts = [base + ((u + odd) & 1) * (LANES // 2) + u // 2 for u in range(8)]
+        starts = [i * 4 + ((u + odd) & 1) * (LANES // 2) + u // 2 for u in range(8)]
         rows = [ref[pl.ds(start, 8, stride=LANES), :] for start in starts]
         return jnp.concatenate([r.reshape(1, 8, LANES) for r in rows], axis=0)
 
@@ -165,6 +190,8 @@
 
     lax.fori_loop(0, bag * samples // block, widen, 0)
     lax.fori_loop(0, count // bag, move, 0)
+    for copy in copies:
+        copy.wait()
     lax.fori_loop(0, DEVS // 8, narrow, 0)
 
 
@@ -172,12 +199,17 @@
     return pl.pallas_call(
         pack_kernel,
         in_specs=[pl.BlockSpec(memory_space=pltpu.SMEM)] * 2
-        + [pl.BlockSpec(memory_space=pltpu.VMEM)] * 4,
+        + [pl.BlockSpec(memory_space=pltpu.VMEM)]
+        + [pl.BlockSpec(memory_space=pl.ANY)] * 2
+        + [pl.BlockSpec(memory_space=pltpu.VMEM)],
         out_specs=pl.BlockSpec(memory_space=pltpu.VMEM),
         out_shape=jax.ShapeDtypeStruct((DEVS, SENT, LANES), BF16),
         scratch_shapes=[
             pltpu.VMEM(grads.shape, F32),
             pltpu.VMEM((DEVS * ROUND + 8, LANES), F32),
+            pltpu.VMEM((table.shape[0] // 2, LANES), F32),
+            pltpu.VMEM((table.shape[0] // 2, LANES), F32),
+            pltpu.SemaphoreType.DMA((2,)),
         ],
         name="pack",
     )(slots.reshape(-1), place, grads, table, moment, head)
@@ -249,7 +281,7 @@
         within = iota(shape, 1)
         lane = iota(shape, 2)
         parity = (core + i * 8 + (source >> 1)) & 1
-        own = (source & 1) * 16 + within * 2 + parity
+        own = parity * 16 + (source & 1) * 8 + within
         high = jnp.broadcast_to(state[:, 24:25, :], shape)
         extra = high + jnp.broadcast_to(state[:, 25:26, :], shape)
         var = jnp.sum(jnp.where(lane == ROUND + own, extra, 0.0), axis=2, keepdims=True)
@@ -525,17 +557,17 @@
     odd = owner % 2 == 1
     rows_here = tab_rows // 2
 
-    ids = jnp.concatenate([touched_ids, bag_lengths], axis=1).T
-    map_rows = train_map.reshape(-1, LANES)
+    front = (
+        touched_ids.T,
+        bag_lengths.T,
+        train_map.reshape(-1, LANES),
+        row_var.reshape(-1, LANES),
+        serve_map.reshape(-1, LANES),
+    )
     grads = slot_grads.reshape(samples * bag, row_width)
 
-    spots = (serve_map % tab_rows).astype(F32).reshape(tab_rows // owners, owners).T
-    spread = jnp.concatenate([row_var.reshape(tab_rows // owners, owners).T, spots], axis=1)
-    spread = jnp.broadcast_to(spread[:, None, :], (owners, 2, 2 * tab_rows // owners))
-    extra = jnp.concatenate([jnp.zeros((DEVS, ROUND), F32), spread.reshape(DEVS, -1)], axis=1)
-
     place = jnp.stack([rep, owner % 2]).astype(I32)
-    slots, keys, head = route(jnp.zeros((1,), I32), ids, map_rows, extra)
+    slots, keys, head = route(jnp.zeros((1,), I32), *front)
     received = exchange(pack(slots, place, grads, table, moment, head))
     core = rep.reshape(1).astype(I32)
     new_rows, sums, places, acc, line, rounds = update(core, received, rows_here)
@@ -544,7 +576,7 @@
 
     def more_sums(carry):
         k, acc = carry[0], carry[1]
-        slots, _, head = route(k.reshape(1), ids, map_rows, extra)
+        slots, _, head = route(k.reshape(1), *front)
         got = exchange(pack(slots, place, grads, table, moment, head))
         line = got[:, ROUND + 24].astype(F32) * 32.0 + got[:, ROUND + 25].astype(F32) - 1.0
         acc = more_rows(line, got, acc, True, True)
@@ -578,7 +610,7 @@
 
     def more_pooled(carry):
         k, acc = carry
-        _, keys, head = route(k.reshape(1), ids, map_rows, extra)
+        _, keys, head = route(k.reshape(1), *front)
         got = exchange(head)
         line = got[:, 0] * 32.0 + got[:, 1] - 1.0
         return (k + 1, more_rows(keys, exchange(reply(line, new_rows)), acc, False, False))

time: 146 us -> 143 us (0.979)
  no operation moved by 1% of the time
where the time goes in v6:
time: 143 us
  waiting for transfers between devices  65.8 us (46%)
  Pallas kernels  41.9 us (29%)
  starting transfers between devices  23.6 us (17%)
  other arithmetic  5.06 us (4%)
  local copies, waits for them, and re-layouts  3.64 us (3%)
  loops' own time  1.68 us (1%)
    all_to_all x3, waiting for transfers between devices, exchange(): return lax.all_to_all(value, ALL, 0, 0, tiled=True)  65 us
    all_to_all x3, starting transfers between devices, exchange(): return lax.all_to_all(value, ALL, 0, 0, tiled=True)  21.7 us
    pallas_call x1, Pallas kernels, pack(): pl.pallas_call(pack_kernel, in_specs=[pl.BlockSpec(memory_space=pltpu.SME...  8.28 us
    pallas_call x1, Pallas kernels, update(): pl.pallas_call(update_kernel, grid=(STEPS,), in_specs=[pl.BlockSpec(memor...  8.21 us
    pallas_call x1, Pallas kernels, route(): pl.pallas_call(route_kernel, in_specs=[pl.BlockSpec(memory_space=pltpu.SM...  8.15 us
    pallas_call x1, Pallas kernels, score(): pl.pallas_call(score_kernel, grid=(STEPS,), in_specs=[whole(keys.shape),...  6.73 us
    pallas_call x1, Pallas kernels, reply(): pl.pallas_call(reply_kernel, in_specs=[pl.BlockSpec(memory_space=pltpu.VM...  5.81 us
    pallas_call x1, Pallas kernels, place_rows(): pl.pallas_call(place_kernel, in_specs=[pl.BlockSpec(memory_space=pltpu.VM...  4.76 us
  transfers between devices with their start and end apart: 6, of which 4 were waited for; matrix products, arithmetic and copies ran while one was open for 4% of the time, Pallas kernels for 7%

profile of v6, /device:TPU:1, one launch (start us, length us, event | category | flops | bytes accessed | tf_op | source)
XLA Modules:
  0.0 142.6 jit_solution(3829737081189302787)
XLA Ops:
  0.6 0.1 pad_add_fusion.place_ref
  0.7 8.1 %route.9 = (s32[32,128]{1,0:T(8,128)}, f32[128,128]{1,0:T(8,128)}, f32[128,8,128]{2,1,0:T(8,128)}) custom-call(s32[1]{0:T(128)} %constant.69.clone.1.round_ref, s32[32,128]{1,0:T(8,128)} %bitcast.47, s32[4,128]{1,0:T(4,128)} %bitcast.55, s32[1024,128]{1,0:T(8,128)} %bitcast.37, f32[16,128]{1,0:T(8,128)} %bitcast.49, s32[16,128]{1,0:T(8,128)} %bitcast.52), custom_call_target="tpu_custom_call" | custom-call | tf_op jit(solution)/shard_map/route/pallas_call | solution.py:119
  8.9 8.3 %pack.5 = bf16[128,96,128]{2,1,0:T(8,128)(2,1)} custom-call(s32[4096]{0:T(1024)} %bitcast.57, s32[2]{0:T(128)S(1)} %pad_add_fusion.place_ref, bf16[4096,128]{1,0:T(8,128)(2,1)} %bitcast.39, f32[2048,128]{1,0:T(8,128)} %table_from_ref.1, f32[2048,128]{1,0:T(8,128)} %moment_from_ref.1, f32[128,8,128]{2,1,0:T(8,128)} %get-tuple-element.325.head_ref), custom_call_target="tpu_custom_call" | custom-call | tf_op jit(solution)/shard_map/pack/pallas_call | solution.py:199
  17.2 11.5 %all-to-all-start.3 = ((bf16[128,96,128]{2,1,0:T(8,128)(2,1)}), bf16[128,96,128]{2,1,0:T(8,128)(2,1)S(1)}, u32[]{:S(2)}, u32[]{:S(2)}) async-start(bf16[128,96,128]{2,1,0:T(8,128)(2,1)} %pack.5), calls=%async_computation.3 | async-start | bytes 6291456 | tf_op jit(solution)/shard_map/all_to_all | solution.py:503
  28.7 0.0 copy-start.12
  28.7 0.0 copy-start.13
  28.7 0.0 copy-start.14
  28.7 0.0 copy-start.16
  28.7 41.6 %all-to-all-done.3.state_ref.left_ref.right_ref = bf16[128,96,128]{2,1,0:T(8,128)(2,1)S(1)} async-done(((bf16[128,96,128]{2,1,0:T(8,128)(2,1)}), bf16[128,96,128]{2,1,0:T(8,128)(2,1)S(1)}, u32[]{:S(2)}, u32[]{:S(2)}) %all-to-all-start.3) | async-done | bytes 3145760 | tf_op jit(solution)/shard_map/all_to_all | solution.py:503
  70.3 8.2 %update.1 = (bf16[1024,128]{1,0:T(8,128)(2,1)}, f32[128,8,128]{2,1,0:T(8,128)}, s32[8,128]{1,0:T(8,128)}, f32[1024,256]{1,0:T(8,128)}, f32[128,128]{1,0:T(8,128)}, /*index=5*/s32[1]{0:T(128)}) custom-call(s32[1]{0:T(128)} %bitcast.5.core_ref, bf16[128,96,128]{2,1,0:T(8,128)(2,1)S(1)} %all-to-all-done.3.state_ref.left_ref.right_ref, ...), custom_call_target="tpu_custom_call" | custom-call | tf_op jit(solution)/shard_map/update/pallas_call | solution.py:345
  78.5 0.0 copy-done.12
  78.5 0.0 copy-done.13
  78.6 0.0 copy-done.14
  78.6 0.0 copy-done.16
  78.6 0.8 while.30
  79.4 0.0 copy-start.4
  79.4 0.0 copy-start.7
  79.4 4.6 %all-to-all-start.4 = ((f32[128,8,128]{2,1,0:T(8,128)}), f32[128,8,128]{2,1,0:T(8,128)S(1)}, u32[]{:S(2)}, u32[]{:S(2)}) async-start(f32[128,8,128]{2,1,0:T(8,128)} %get-tuple-element.331), calls=%async_computation.4 | async-start | bytes 1048576 | tf_op jit(solution)/shard_map/all_to_all | solution.py:503
  84.0 5.8 %reply.5 = bf16[128,64,128]{2,1,0:T(8,128)(2,1)} custom-call(f32[128,128]{1,0:T(8,128)} %get-tuple-element.335.line_ref, bf16[1024,128]{1,0:T(8,128)(2,1)} %get-tuple-element.629.own_ref.new_ref), custom_call_target="tpu_custom_call" | custom-call | tf_op jit(solution)/shard_map/reply/pallas_call | solution.py:436
  89.8 7.9 %all-to-all-done.4 = f32[128,8,128]{2,1,0:T(8,128)S(1)} async-done(((f32[128,8,128]{2,1,0:T(8,128)}), f32[128,8,128]{2,1,0:T(8,128)S(1)}, u32[]{:S(2)}, u32[]{:S(2)}) %all-to-all-start.4) | async-done | bytes 524320 | tf_op jit(solution)/shard_map/all_to_all | solution.py:503
  97.7 1.0 copy.25
  98.7 0.7 broadcast_in_dim.30
  99.4 0.0 copy-done.4
  99.4 0.0 copy-done.7
  99.4 0.9 while.31
  100.3 0.0 copy-start.11
  100.3 0.0 copy-start.17
  100.3 0.0 copy-start.19
  100.3 5.7 %all-to-all-start.5 = ((bf16[128,64,128]{2,1,0:T(8,128)(2,1)}), bf16[128,64,128]{2,1,0:T(8,128)(2,1)}, u32[]{:S(2)}, u32[]{:S(2)}) async-start(bf16[128,64,128]{2,1,0:T(8,128)(2,1)} %reply.5), calls=%async_computation.5 | async-start | bytes 4194304 | tf_op jit(solution)/shard_map/all_to_all | solution.py:503
  106.0 0.0 copy-done.11
  106.0 0.0 copy-start.10
  106.0 0.0 copy-start.5
  106.0 0.0 copy-start.6
  106.1 1.4 collective-permute-start
  107.4 0.1 collective-permute-start.1
  107.5 0.0 copy-done.17
  107.5 0.4 collective-permute-start.2
  107.9 0.0 copy-done.19
  107.9 0.6 reshape.71.score_ref
  108.5 0.8 collective-permute-done.2.other_at_ref
  109.3 0.0 copy-start.18
  109.3 0.0 collective-permute-done.1.other_ref
  109.3 0.6 copy-done.18
  109.9 0.0 copy-start.15
  109.9 0.7 copy-done.15
  110.6 4.8 %place.1 = bf16[2048,128]{1,0:T(8,128)(2,1)} custom-call(bf16[2048,128]{1,0:T(8,128)(2,1)} %old_ref.1, bf16[1024,128]{1,0:T(8,128)(2,1)S(1)} %get-tuple-element.661, bf16[1024,128]{1,0:T(8,128)(2,1)} %copy-done.15, s32[8,128]{1,0:T(8,128)S(1)} %copy-done.17, s32[8,128]{1,0:T(8,128)} %copy-done.18), custom_call_target="tpu_custom_call" | custom-call | tf_op jit(solution)/shard_map/place/pallas_call | solution.py:528
  115.4 0.0 copy-done.10
  115.4 0.0 collective-permute-done
  115.4 1.7 %maximum_select_fusion = f32[2048,128]{1,0:T(8,128)S(1)} fusion(f32[1024,128]{1,0:T(8,128)} %collective-permute-done, f32[1024,128]{1,0:T(8,128)} %bitcast.45, pred[]{:T(512)S(6)} %eq.9), kind=kLoop, calls=%fused_computation.8 | loop fusion | flops 786432 | bytes 2097153 | tf_op jit(solution)/shard_map/jit(_where)/select_n | solution.py:600
  117.1 0.3 fusion.3
  117.5 0.0 copy-start.9
  117.5 0.6 select_reduce_fusion
  118.1 0.6 sqrt_add_fusion
  118.7 0.0 copy-done.5
  118.7 0.0 copy-done.6
  118.7 1.7 %subtract_select_fusion = (f32[2048,128]{1,0:T(8,128)}, f32[2048,128]{1,0:T(8,128)}) fusion(f32[2048,128]{1,0:T(8,128)S(1)} %copy-done.5, f32[2048]{0:T(1024)S(1)} %get-tuple-element.391, pred[2048]{0:T(1024)(128)(4,1)S(1)} %fusion.3, f32[2048,128]{1,0:T(8,128)S(1)} %copy-done.6, f32[2048,128]{1,0:T(8,128)S(1)} %maximum_select_fusion), kind=kLoop, calls=%fused_computation.6 | loop fusion | flops 2097152 | bytes 5253120 | tf_op jit(solution)/shard_map/jit(_where)/select_n | solution.py:607
  120.4 15.5 %all-to-all-done.5.left_ref.right_ref = bf16[128,64,128]{2,1,0:T(8,128)(2,1)} async-done(((bf16[128,64,128]{2,1,0:T(8,128)(2,1)}), bf16[128,64,128]{2,1,0:T(8,128)(2,1)}, u32[]{:S(2)}, u32[]{:S(2)}) %all-to-all-start.5) | async-done | bytes 2097184 | tf_op jit(solution)/shard_map/all_to_all | solution.py:503
  135.8 0.0 copy-done.9
  135.9 6.7 %score.1 = f32[1,128]{1,0:T(1,128)} custom-call(f32[128,128]{1,0:T(8,128)} %get-tuple-element.334.keys_ref, bf16[128,64,128]{2,1,0:T(8,128)(2,1)} %all-to-all-done.5.left_ref.right_ref, bf16[128,64,128]{2,1,0:T(8,128)(2,1)} %all-to-all-done.5.left_ref.right_ref, f32[512,128]{1,0:T(8,128)S(1)} %copy-done.9, bf16[512,1024]{1,0:T(8,128)(2,1)} %first_ref.1, ...), custom_call_target="tpu_custom_call" | custom-call | tf_op jit(solution)/shard_map/score/pallas_call | solution.py:487
  (1 shorter events, 0.0 us)
Async XLA Ops:
  17.2 53.2 %all-to-all-start.3 = ((bf16[128,96,128]{2,1,0:T(8,128)(2,1)}), bf16[128,96,128]{2,1,0:T(8,128)(2,1)S(1)}, u32[]{:S(2)}, u32[]{:S(2)}) async-start(bf16[128,96,128]{2,1,0:T(8,128)(2,1)} %pack.5), calls=%async_computation.3 | async-start | bytes 6291456 | tf_op jit(solution)/shard_map/all_to_all | solution.py:503
  28.7 49.9 %copy-start.12 = (s32[128,32]{0,1:T(8,128)S(1)}, s32[128,32]{0,1:T(8,128)}, u32[]{:S(2)}) copy-start(s32[128,32]{0,1:T(8,128)} %param.16) | copy-start | bytes 49156
  28.7 49.9 %copy-start.13 = (f32[2048]{0:T(1024)S(1)}, f32[2048]{0:T(1024)}, u32[]{:S(2)}) copy-start(f32[2048]{0:T(1024)} %param.23) | copy-start | bytes 24580
  28.7 49.9 %copy-start.14 = (s32[2048]{0:T(1024)S(1)}, s32[2048]{0:T(1024)}, u32[]{:S(2)}) copy-start(s32[2048]{0:T(1024)} %param.19) | copy-start | bytes 24580
  28.7 49.9 %copy-start.16 = (s32[128,4]{0,1:T(4,128)S(1)}, s32[128,4]{0,1:T(4,128)}, u32[]{:S(2)}) copy-start(s32[128,4]{0,1:T(4,128)} %param.17) | copy-start | bytes 6148
  79.4 20.0 %copy-start.4 = (s32[1024,128]{1,0:T(8,128)S(1)}, s32[1024,128]{1,0:T(8,128)}, u32[]{:S(2)}) copy-start(s32[1024,128]{1,0:T(8,128)} %get-tuple-element.658) | copy-start | bytes 1572868
  79.4 20.0 %copy-start.7 = (bf16[1024,128]{1,0:T(8,128)(2,1)S(1)}, bf16[1024,128]{1,0:T(8,128)(2,1)}, u32[]{:S(2)}) copy-start(bf16[1024,128]{1,0:T(8,128)(2,1)} %get-tuple-element.629.own_ref.new_ref) | copy-start | bytes 786436
  79.4 18.3 %all-to-all-start.4 = ((f32[128,8,128]{2,1,0:T(8,128)}), f32[128,8,128]{2,1,0:T(8,128)S(1)}, u32[]{:S(2)}, u32[]{:S(2)}) async-start(f32[128,8,128]{2,1,0:T(8,128)} %get-tuple-element.331), calls=%async_computation.4 | async-start | bytes 1048576 | tf_op jit(solution)/shard_map/all_to_all | solution.py:503
  100.3 5.7 %copy-start.11 = (f32[64,2,8,128]{3,0,1,2:T(8,128)S(1)}, f32[64,2,8,128]{3,0,1,2:T(8,128)}, u32[]{:S(2)}) copy-start(f32[64,2,8,128]{3,0,1,2:T(8,128)} %copy.25) | copy-start | bytes 1572868
  100.3 7.2 %copy-start.17 = (s32[8,128]{1,0:T(8,128)S(1)}, s32[8,128]{1,0:T(8,128)}, u32[]{:S(2)}) copy-start(s32[8,128]{1,0:T(8,128)} %get-tuple-element.333.own_at_ref) | copy-start | bytes 12292
  100.3 7.7 %copy-start.19 = (bf16[1024]{0:T(1024)(128)(2,1)S(1)}, bf16[1024]{0:T(1024)(128)(2,1)}, u32[]{:S(2)}) copy-start(bf16[1024]{0:T(1024)(128)(2,1)} %param.27) | copy-start | bytes 6148
  100.3 35.6 %all-to-all-start.5 = ((bf16[128,64,128]{2,1,0:T(8,128)(2,1)}), bf16[128,64,128]{2,1,0:T(8,128)(2,1)}, u32[]{:S(2)}, u32[]{:S(2)}) async-start(bf16[128,64,128]{2,1,0:T(8,128)(2,1)} %reply.5), calls=%async_computation.5 | async-start | bytes 4194304 | tf_op jit(solution)/shard_map/all_to_all | solution.py:503
  106.0 9.4 %copy-start.10 = (f32[64,2,8,128]{3,0,1,2:T(8,128)}, f32[64,2,8,128]{3,0,1,2:T(8,128)S(1)}, u32[]{:S(2)}) copy-start(f32[64,2,8,128]{3,0,1,2:T(8,128)S(1)} %reverse_select_fusion) | copy-start | bytes 1572868
  106.0 12.7 %copy-start.5 = (f32[2048,128]{1,0:T(8,128)S(1)}, f32[2048,128]{1,0:T(8,128)}, u32[]{:S(2)}) copy-start(f32[2048,128]{1,0:T(8,128)} %get-tuple-element.659) | copy-start | bytes 3145732
  106.0 12.7 %copy-start.6 = (f32[2048,128]{1,0:T(8,128)S(1)}, f32[2048,128]{1,0:T(8,128)}, u32[]{:S(2)}) copy-start(f32[2048,128]{1,0:T(8,128)} %get-tuple-element.660) | copy-start | bytes 3145732
  106.1 9.3 %collective-permute-start = (f32[1024,128]{1,0:T(8,128)S(1)}, f32[1024,128]{1,0:T(8,128)}, u32[]{:S(2)}, u32[]{:S(2)}) collective-permute-start(f32[1024,128]{1,0:T(8,128)S(1)} %bitcast.44), channel_id=1, source_target_pairs={{0,1},{1,0},{2,3},{3,2},{4,5},{5,4},{6,7},{7,6},{8,9},{9,8},{10,11... | collective-permute-start | bytes 1572872 | tf_op jit(solution)/shard_map/ppermute | solution.py:599
  107.4 1.9 %collective-permute-start.1 = (bf16[1024,128]{1,0:T(8,128)(2,1)S(1)}, bf16[1024,128]{1,0:T(8,128)(2,1)S(1)}, u32[]{:S(2)}, u32[]{:S(2)}) collective-permute-start(bf16[1024,128]{1,0:T(8,128)(2,1)S(1)} %get-tuple-element.661), channel_id=1, source_target_pairs={{0,1},{1,0},{2,3},{3,2},{4,5},{5,4},{6,7},{7,6},{8,9},{9,8},{10,11... | collective-permute-start | bytes 786440 | tf_op jit(solution)/shard_map/ppermute | solution.py:592
  107.5 1.8 %collective-permute-start.2 = (s32[8,128]{1,0:T(8,128)S(1)}, s32[8,128]{1,0:T(8,128)S(1)}, u32[]{:S(2)}, u32[]{:S(2)}) collective-permute-start(s32[8,128]{1,0:T(8,128)S(1)} %copy-done.17), channel_id=1, source_target_pairs={{0,1},{1,0},{2,3},{3,2},{4,5},{5,4},{6,7},{7,6},{8,9},{9,8},{10,11... | collective-permute-start | bytes 12296 | tf_op jit(solution)/shard_map/ppermute | solution.py:593
  109.3 0.6 copy-start.18
  109.9 0.7 copy-start.15
  117.5 18.4 %copy-start.9 = (f32[512,128]{1,0:T(8,128)S(1)}, f32[512,128]{1,0:T(8,128)}, u32[]{:S(2)}) copy-start(f32[512,128]{1,0:T(8,128)} %get-tuple-element.336.start_ref) | copy-start | bytes 786436

commit v7 on v6

--- a/solution.py
+++ b/solution.py
@@ -405,7 +405,7 @@
     )(line, rows, rows, start)
 
 
-def reply_kernel(line_ref, new_ref, out_ref, turned_ref, table_ref):
+def reply_kernel(line_ref, new_ref, sums_ref, out_ref, turned_ref, table_ref):
     turned_ref[...] = line_ref[...].T
     part = new_ref.shape[0] // 4
     table_ref[...] = jnp.concatenate(
@@ -426,24 +426,25 @@
             high = jnp.where(
                 row < 3 * part, piece[:, 2 * LANES : 3 * LANES], piece[:, 3 * LANES :]
             )
-            out_ref[i * 32 + u] = jnp.where(row < 2 * part, low, high).astype(BF16)
+            out_ref[i * 32 + u, 0:ROUND, :] = jnp.where(row < 2 * part, low, high).astype(BF16)
         return carry
 
+    out_ref[:, ROUND : ROUND + 8, :] = sums_ref[...].astype(BF16)
     lax.fori_loop(0, DEVS // 32, look, 0)
 
 
-def reply(line, new_rows):
+def reply(line, new_rows, sums):
     return pl.pallas_call(
         reply_kernel,
-        in_specs=[pl.BlockSpec(memory_space=pltpu.VMEM)] * 2,
+        in_specs=[pl.BlockSpec(memory_space=pltpu.VMEM)] * 3,
         out_specs=pl.BlockSpec(memory_space=pltpu.VMEM),
-        out_shape=jax.ShapeDtypeStruct((DEVS, ROUND, LANES), BF16),
+        out_shape=jax.ShapeDtypeStruct((DEVS, ROUND + 8, LANES), BF16),
         scratch_shapes=[
             pltpu.VMEM((DEVS, LANES), F32),
             pltpu.VMEM((new_rows.shape[0] // 4, 4 * LANES), BF16),
         ],
         name="reply",
-    )(line, new_rows)
+    )(line, new_rows, sums)
 
 
 def score_kernel(
@@ -497,6 +498,70 @@
         ],
         name="score",
     )(keys, rows, rows, start, w_first, w_second, w_score)
+
+
+def finish_kernel(
+    place_ref,
+    own_ref,
+    other_ref,
+    table_ref,
+    moment_ref,
+    var_ref,
+    new_table_ref,
+    new_moment_ref,
+    new_var_ref,
+    sums_ref,
+):
+    half, odd = place_ref[0], place_ref[1]
+    step = pl.program_id(0)
+
+    @pl.when(step == 0)
+    def _():
+        sums_ref[half] = own_ref[...].astype(F32).reshape(sums_ref.shape[1:])
+        sums_ref[1 - half] = other_ref[...].astype(F32).reshape(sums_ref.shape[1:])
+
+    eye = iota((LANES, LANES), 0) == iota((LANES, LANES), 1)
+    for u in range(4):
+        block = step * 4 + u
+        at = pl.ds(u * LANES, LANES)
+        sides = []
+        for parity in range(2):
+            first = ((parity + odd) & 1) * 8 + (block & 7)
+            sides.append(sums_ref[block >> 3, pl.ds(first, LANES // 2, stride=16), :])
+        grad = jnp.concatenate(sides, axis=0)
+        touched = grad < 0.5 * UNTOUCHED
+        var = jnp.broadcast_to(var_ref[pl.ds(block, 1), :], (LANES, LANES))
+        var = jnp.sum(jnp.where(eye, var, 0.0), axis=1, keepdims=True)
+        known = jnp.where(touched, grad, 0.0)
+        mean = jnp.sum(known * known, axis=1, keepdims=True) * (1.0 / LANES)
+        new_var = jnp.where(touched, beta_two * var + (1.0 - beta_two) * mean, var)
+        table, moment = table_ref[at, :], moment_ref[at, :]
+        new_moment = jnp.where(touched, beta_one * moment + (1.0 - beta_one) * grad, moment)
+        new_table = table - learn_rate * new_moment / (jnp.sqrt(new_var) + epsilon)
+        new_moment_ref[at, :] = new_moment
+        new_table_ref[at, :] = jnp.where(touched, new_table, table)
+        line = jnp.sum(jnp.where(eye, new_var, 0.0), axis=0, keepdims=True)
+        new_var_ref[pl.ds(block, 1), :] = line
+
+
+def finish(place, answer, other, table, moment, var):
+    rows = pl.BlockSpec((4 * LANES, LANES), lambda i: (i, 0))
+    return pl.pallas_call(
+        finish_kernel,
+        grid=(table.shape[0] // (4 * LANES),),
+        in_specs=[
+            pl.BlockSpec(memory_space=pltpu.SMEM),
+            whole((DEVS, 8, LANES), (0, ROUND // 8, 0)),
+            whole(other.shape),
+            rows,
+            rows,
+            whole(var.shape),
+        ],
+        out_specs=[rows, rows, whole(var.shape)],
+        out_shape=tuple(jax.ShapeDtypeStruct(a.shape, F32) for a in (table, moment, var)),
+        scratch_shapes=[pltpu.VMEM((2, table.shape[0] // 2, LANES), F32)],
+        name="finish",
+    )(place, answer, other, table, moment, var)
 
 
 def exchange(value):
@@ -554,7 +619,6 @@
     tab_rows, row_width = table.shape
     samples, bag = touched_ids.shape
     swap = [(0, 1), (1, 0)]
-    odd = owner % 2 == 1
     rows_here = tab_rows // 2
 
     front = (
@@ -586,34 +650,18 @@
         lambda c: c[0] < rounds, more_sums, (one, acc, new_rows, sums, places)
     )
 
-    back = exchange(sums)
-    answer = exchange(reply(line, new_rows))
+    answer = exchange(reply(line, new_rows, sums))
 
     other_rows = lax.ppermute(new_rows, "rep", swap)
     other_places = lax.ppermute(places, "rep", swap)
     serving_table = place_rows(serving_old, new_rows, other_rows, places, other_places)
-
-    back = back.reshape(owners, 2, 8, row_width)
-    back = jnp.where(odd, back[:, ::-1], back)
-    half = back.transpose(2, 1, 0, 3).reshape(rows_here, row_width)
-    other = lax.ppermute(half, "rep", swap)
-    grad_sum = jnp.where(
-        rep == 0, jnp.concatenate([half, other]), jnp.concatenate([other, half])
-    )
-    touched = grad_sum[:, :1] < 0.5 * UNTOUCHED
-    new_moment = jnp.where(touched, beta_one * moment + (1.0 - beta_one) * grad_sum, moment)
-    mean = jnp.mean(jnp.where(touched, grad_sum * grad_sum, 0.0), axis=1)
-    new_var = jnp.where(touched[:, 0], beta_two * row_var + (1.0 - beta_two) * mean, row_var)
-    new_table = jnp.where(
-        touched, table - learn_rate * new_moment / (jnp.sqrt(new_var)[:, None] + epsilon), table
-    )
 
     def more_pooled(carry):
         k, acc = carry
         _, keys, head = route(k.reshape(1), *front)
         got = exchange(head)
         line = got[:, 0] * 32.0 + got[:, 1] - 1.0
-        return (k + 1, more_rows(keys, exchange(reply(line, new_rows)), acc, False, False))
+        return (k + 1, more_rows(keys, exchange(reply(line, new_rows, sums)), acc, False, False))
 
     rounds, _ = lax.optimization_barrier((rounds, answer[0, 0, 0]))
     _, pooled = lax.while_loop(
@@ -621,8 +669,12 @@
         more_pooled,
         (one, jnp.zeros((4 * samples, row_width), F32)),
     )
+    other = lax.ppermute(answer[:, ROUND:], "rep", swap)
     scores = score(keys, answer, pooled, w_first, w_second, w_score.reshape(1, -1))
-    return (new_table, new_moment, new_var, serving_table, scores.reshape(samples))
+    new_table, new_moment, new_var = finish(
+        place, answer, other, table, moment, row_var.reshape(-1, LANES)
+    )
+    return (new_table, new_moment, new_var.reshape(-1), serving_table, scores.reshape(samples))
 
 
 def solution(mesh):

time: 143 us -> 138 us (0.965)
  other arithmetic: 5.06 us -> 0.08 us
  starting transfers between devices: 23.6 us -> 18.8 us
  Pallas kernels: 41.9 us -> 46.1 us
  waiting for transfers between devices: 65.8 us -> 67.3 us
    all_to_all x3 -> x2, starting transfers between devices: 21.7 us -> 16.1 us  [exchange(): return lax.all_to_all(value, ALL, 0, 0, tiled=True)]
    pallas_call x0 -> x1, Pallas kernels: none -> 3.7 us  [finish(): pl.pallas_call(finish_kernel, grid=(table.shape[0] // (4 * LANES),), in_s...]
    select_n x3 -> x0, other arithmetic: 3.4 us -> none  [the longest x1 1.7 us: per_device(): jnp.where(rep == 0, jnp.concatenate([half, other]), jnp.concatenate([othe...]
    all_to_all x3 -> x2, waiting for transfers between devices: 65 us -> 66.5 us  [exchange(): return lax.all_to_all(value, ALL, 0, 0, tiled=True)]
  transfers between devices with their start and end apart: 6 -> 5, of which waited for: 4 -> 3; matrix products, arithmetic and copies ran while one was open for 4% -> 1% of each run, Pallas kernels for 7% -> 9%
where the time goes in v7:
time: 138 us
  waiting for transfers between devices  67.3 us (49%)
  Pallas kernels  46.1 us (33%)
  starting transfers between devices  18.8 us (14%)
  local copies, waits for them, and re-layouts  2.74 us (2%)
  loops' own time  1.68 us (1%)
    all_to_all x2, waiting for transfers between devices, exchange(): return lax.all_to_all(value, ALL, 0, 0, tiled=True)  66.5 us
    all_to_all x2, starting transfers between devices, exchange(): return lax.all_to_all(value, ALL, 0, 0, tiled=True)  16.1 us
    pallas_call x1, Pallas kernels, pack(): pl.pallas_call(pack_kernel, in_specs=[pl.BlockSpec(memory_space=pltpu.SME...  8.27 us
    pallas_call x1, Pallas kernels, update(): pl.pallas_call(update_kernel, grid=(STEPS,), in_specs=[pl.BlockSpec(memor...  8.21 us
    pallas_call x1, Pallas kernels, route(): pl.pallas_call(route_kernel, in_specs=[pl.BlockSpec(memory_space=pltpu.SM...  8.15 us
    pallas_call x1, Pallas kernels, score(): pl.pallas_call(score_kernel, grid=(STEPS,), in_specs=[whole(keys.shape),...  6.92 us
    pallas_call x1, Pallas kernels, reply(): pl.pallas_call(reply_kernel, in_specs=[pl.BlockSpec(memory_space=pltpu.VM...  6.07 us
    pallas_call x1, Pallas kernels, place_rows(): pl.pallas_call(place_kernel, in_specs=[pl.BlockSpec(memory_space=pltpu.VM...  4.83 us
  transfers between devices with their start and end apart: 5, of which 3 were waited for; matrix products, arithmetic and copies ran while one was open for 1% of the time, Pallas kernels for 9%

profile of v7, /device:TPU:1, one launch (start us, length us, event | category | flops | bytes accessed | tf_op | source)
XLA Modules:
  0.0 137.5 jit_solution(11136745104760714594)
XLA Ops:
  0.6 0.1 pad_add_fusion.place_ref
  0.7 8.1 %route.9 = (s32[32,128]{1,0:T(8,128)}, f32[128,128]{1,0:T(8,128)}, f32[128,8,128]{2,1,0:T(8,128)}) custom-call(s32[1]{0:T(128)} %constant.56.clone.1.round_ref, s32[32,128]{1,0:T(8,128)} %bitcast.41, s32[4,128]{1,0:T(4,128)} %bitcast.48, s32[1024,128]{1,0:T(8,128)} %bitcast.34, f32[16,128]{1,0:T(8,128)} %bitcast.43, s32[16,128]{1,0:T(8,128)} %bitcast.45), custom_call_target="tpu_custom_call" | custom-call | tf_op jit(solution)/shard_map/route/pallas_call | solution.py:119
  8.9 8.3 %pack.5 = bf16[128,96,128]{2,1,0:T(8,128)(2,1)} custom-call(s32[4096]{0:T(1024)} %bitcast.50, s32[2]{0:T(128)S(1)} %pad_add_fusion.place_ref, bf16[4096,128]{1,0:T(8,128)(2,1)} %bitcast.36, f32[2048,128]{1,0:T(8,128)} %table_ref.1, f32[2048,128]{1,0:T(8,128)} %moment_ref.1, f32[128,8,128]{2,1,0:T(8,128)} %get-tuple-element.339.head_ref), custom_call_target="tpu_custom_call" | custom-call | tf_op jit(solution)/shard_map/pack/pallas_call | solution.py:199
  17.1 11.5 %all-to-all-start.3 = ((bf16[128,96,128]{2,1,0:T(8,128)(2,1)}), bf16[128,96,128]{2,1,0:T(8,128)(2,1)S(1)}, u32[]{:S(2)}, u32[]{:S(2)}) async-start(bf16[128,96,128]{2,1,0:T(8,128)(2,1)} %pack.5), calls=%async_computation.3 | async-start | bytes 6291456 | tf_op jit(solution)/shard_map/all_to_all | solution.py:568
  28.6 0.0 copy-start.9
  28.7 0.0 copy-start.10
  28.7 0.0 copy-start.11
  28.7 0.0 copy-start.12
  28.7 41.6 %all-to-all-done.3.state_ref.left_ref.right_ref = bf16[128,96,128]{2,1,0:T(8,128)(2,1)S(1)} async-done(((bf16[128,96,128]{2,1,0:T(8,128)(2,1)}), bf16[128,96,128]{2,1,0:T(8,128)(2,1)S(1)}, u32[]{:S(2)}, u32[]{:S(2)}) %all-to-all-start.3) | async-done | bytes 3145760 | tf_op jit(solution)/shard_map/all_to_all | solution.py:568
  70.3 8.2 %update.1 = (bf16[1024,128]{1,0:T(8,128)(2,1)}, f32[128,8,128]{2,1,0:T(8,128)}, s32[8,128]{1,0:T(8,128)}, f32[1024,256]{1,0:T(8,128)}, f32[128,128]{1,0:T(8,128)}, /*index=5*/s32[1]{0:T(128)}) custom-call(s32[1]{0:T(128)} %bitcast.5.core_ref, bf16[128,96,128]{2,1,0:T(8,128)(2,1)S(1)} %all-to-all-done.3.state_ref.left_ref.right_ref, ...), custom_call_target="tpu_custom_call" | custom-call | tf_op jit(solution)/shard_map/update/pallas_call | solution.py:345
  78.5 0.0 copy-done.9
  78.5 0.0 copy-done.10
  78.5 0.0 copy-done.11
  78.6 0.0 copy-done.12
  78.6 0.8 while.30
  79.4 6.1 %reply.5 = bf16[128,72,128]{2,1,0:T(8,128)(2,1)} custom-call(f32[128,128]{1,0:T(8,128)} %get-tuple-element.340.line_ref, bf16[1024,128]{1,0:T(8,128)(2,1)} %get-tuple-element.650.new_ref.own_ref, f32[128,8,128]{2,1,0:T(8,128)} %get-tuple-element.651.sums_ref), custom_call_target="tpu_custom_call" | custom-call | tf_op jit(solution)/shard_map/reply/pallas_call | solution.py:437
  85.5 0.0 copy-start.13
  85.5 0.0 copy-start.15
  85.5 0.0 copy-start.4
  85.5 0.0 copy-start.8
  85.5 4.6 %all-to-all-start.4 = ((bf16[128,72,128]{2,1,0:T(8,128)(2,1)}), bf16[128,72,128]{2,1,0:T(8,128)(2,1)S(1)}, u32[]{:S(2)}, u32[]{:S(2)}) async-start(bf16[128,72,128]{2,1,0:T(8,128)(2,1)} %reply.5), calls=%async_computation.4 | async-start | bytes 4718592 | tf_op jit(solution)/shard_map/all_to_all | solution.py:568
  90.1 1.3 collective-permute-start.1
  91.4 0.0 copy-done.13
  91.4 0.1 collective-permute-start.2
  91.5 0.0 copy-done.15
  91.5 0.6 reshape.63.score_ref
  92.1 0.8 collective-permute-done.2.other_at_ref
  92.9 0.0 copy-start.14
  92.9 0.0 collective-permute-done.1.other_ref
  92.9 0.6 copy-done.14
  93.5 4.8 %place.1 = bf16[2048,128]{1,0:T(8,128)(2,1)} custom-call(bf16[2048,128]{1,0:T(8,128)(2,1)} %old_ref.1, bf16[1024,128]{1,0:T(8,128)(2,1)} %get-tuple-element.650.new_ref.own_ref, bf16[1024,128]{1,0:T(8,128)(2,1)} %collective-permute-done.1.other_ref, s32[8,128]{1,0:T(8,128)S(1)} %copy-done.13, s32[8,128]{1,0:T(8,128)} %copy-done.14), custom_call_target="tpu_custom_call" | custom-call | tf_op jit(solution)/shard_map/place/pallas_call | solution.py:593
  98.3 24.8 %all-to-all-done.4.own_ref.left_ref.right_ref = bf16[128,72,128]{2,1,0:T(8,128)(2,1)S(1)} async-done(((bf16[128,72,128]{2,1,0:T(8,128)(2,1)}), bf16[128,72,128]{2,1,0:T(8,128)(2,1)S(1)}, u32[]{:S(2)}, u32[]{:S(2)}) %all-to-all-start.4) | async-done | bytes 2359328 | tf_op jit(solution)/shard_map/all_to_all | solution.py:568
  123.2 0.0 copy-start.7
  123.2 0.8 slice.33
  124.0 1.3 collective-permute-start
  125.3 0.7 broadcast_in_dim.3
  126.0 0.0 copy-done.4
  126.0 0.0 copy-done.8
  126.0 0.0 copy-done.7
  126.0 0.9 while.31
  126.8 0.0 copy-start.5
  126.9 0.0 copy-start.6
  126.9 6.9 %score.1 = f32[1,128]{1,0:T(1,128)} custom-call(f32[128,128]{1,0:T(8,128)} %get-tuple-element.352.keys_ref, bf16[128,72,128]{2,1,0:T(8,128)(2,1)} %copy-done.7, bf16[128,72,128]{2,1,0:T(8,128)(2,1)} %copy-done.7, f32[512,128]{1,0:T(8,128)} %get-tuple-element.353.start_ref, bf16[512,1024]{1,0:T(8,128)(2,1)} %first_ref.1, bf16[1024,1024]{1,0:T(8,128)(2,1)} %second_ref.1, ...), custom_call_target="tpu_custom_call" | custom-call | tf_op jit(solution)/shard_map/score/pallas_call | solution.py:488
  133.8 0.0 collective-permute-done.other_ref
  133.8 0.0 copy-done.5
  133.8 0.0 copy-done.6
  133.8 3.7 %finish.1 = (f32[2048,128]{1,0:T(8,128)}, f32[2048,128]{1,0:T(8,128)}, f32[16,128]{1,0:T(8,128)}) custom-call(s32[2]{0:T(128)S(1)} %get-tuple-element.696, bf16[128,72,128]{2,1,0:T(8,128)(2,1)} %copy-done.7, bf16[128,8,128]{2,1,0:T(8,128)(2,1)} %collective-permute-done.other_ref, f32[2048,128]{1,0:T(8,128)S(1)} %copy-done.5, f32[2048,128]{1,0:T(8,128)S(1)} %copy-done.6, ...), custom_call_target="tpu_custom_call" | custom-call | tf_op jit(solution)/shard_map/finish/pallas_call | solution.py:549
Async XLA Ops:
  17.1 53.2 %all-to-all-start.3 = ((bf16[128,96,128]{2,1,0:T(8,128)(2,1)}), bf16[128,96,128]{2,1,0:T(8,128)(2,1)S(1)}, u32[]{:S(2)}, u32[]{:S(2)}) async-start(bf16[128,96,128]{2,1,0:T(8,128)(2,1)} %pack.5), calls=%async_computation.3 | async-start | bytes 6291456 | tf_op jit(solution)/shard_map/all_to_all | solution.py:568
  28.6 49.9 %copy-start.9 = (s32[128,32]{0,1:T(8,128)S(1)}, s32[128,32]{0,1:T(8,128)}, u32[]{:S(2)}) copy-start(s32[128,32]{0,1:T(8,128)} %param.16) | copy-start | bytes 49156
  28.7 49.9 %copy-start.10 = (f32[2048]{0:T(1024)S(1)}, f32[2048]{0:T(1024)}, u32[]{:S(2)}) copy-start(f32[2048]{0:T(1024)} %param.23) | copy-start | bytes 24580
  28.7 49.9 %copy-start.11 = (s32[2048]{0:T(1024)S(1)}, s32[2048]{0:T(1024)}, u32[]{:S(2)}) copy-start(s32[2048]{0:T(1024)} %param.19) | copy-start | bytes 24580
  28.7 49.9 %copy-start.12 = (s32[128,4]{0,1:T(4,128)S(1)}, s32[128,4]{0,1:T(4,128)}, u32[]{:S(2)}) copy-start(s32[128,4]{0,1:T(4,128)} %param.17) | copy-start | bytes 6148
  85.5 5.9 %copy-start.13 = (s32[8,128]{1,0:T(8,128)S(1)}, s32[8,128]{1,0:T(8,128)}, u32[]{:S(2)}) copy-start(s32[8,128]{1,0:T(8,128)} %get-tuple-element.351.own_at_ref) | copy-start | bytes 12292
  85.5 6.0 %copy-start.15 = (bf16[1024]{0:T(1024)(128)(2,1)S(1)}, bf16[1024]{0:T(1024)(128)(2,1)}, u32[]{:S(2)}) copy-start(bf16[1024]{0:T(1024)(128)(2,1)} %param.27) | copy-start | bytes 6148
  85.5 40.5 %copy-start.4 = (s32[1024,128]{1,0:T(8,128)S(1)}, s32[1024,128]{1,0:T(8,128)}, u32[]{:S(2)}) copy-start(s32[1024,128]{1,0:T(8,128)} %get-tuple-element.682) | copy-start | bytes 1572868
  85.5 40.5 %copy-start.8 = (f32[128,8,128]{2,1,0:T(8,128)S(1)}, f32[128,8,128]{2,1,0:T(8,128)}, u32[]{:S(2)}) copy-start(f32[128,8,128]{2,1,0:T(8,128)} %get-tuple-element.651.sums_ref) | copy-start | bytes 1572868
  85.5 37.7 %all-to-all-start.4 = ((bf16[128,72,128]{2,1,0:T(8,128)(2,1)}), bf16[128,72,128]{2,1,0:T(8,128)(2,1)S(1)}, u32[]{:S(2)}, u32[]{:S(2)}) async-start(bf16[128,72,128]{2,1,0:T(8,128)(2,1)} %reply.5), calls=%async_computation.4 | async-start | bytes 4718592 | tf_op jit(solution)/shard_map/all_to_all | solution.py:568
  90.1 2.8 %collective-permute-start.1 = (bf16[1024,128]{1,0:T(8,128)(2,1)}, bf16[1024,128]{1,0:T(8,128)(2,1)}, u32[]{:S(2)}, u32[]{:S(2)}) collective-permute-start(bf16[1024,128]{1,0:T(8,128)(2,1)} %get-tuple-element.650.new_ref.own_ref), channel_id=1, source_target_pairs={{0,1},{1,0},{2,3},{3,2},{4,5},{5,4},{6,7},{7,6},{8,9},{9,8},{10,11... | collective-permute-start | bytes 786440 | tf_op jit(solution)/shard_map/ppermute | solution.py:655
  91.4 1.5 %collective-permute-start.2 = (s32[8,128]{1,0:T(8,128)S(1)}, s32[8,128]{1,0:T(8,128)S(1)}, u32[]{:S(2)}, u32[]{:S(2)}) collective-permute-start(s32[8,128]{1,0:T(8,128)S(1)} %copy-done.13), channel_id=1, source_target_pairs={{0,1},{1,0},{2,3},{3,2},{4,5},{5,4},{6,7},{7,6},{8,9},{9,8},{10,11... | collective-permute-start | bytes 12296 | tf_op jit(solution)/shard_map/ppermute | solution.py:656
  92.9 0.6 copy-start.14
  123.2 2.8 %copy-start.7 = (bf16[128,72,128]{2,1,0:T(8,128)(2,1)}, bf16[128,72,128]{2,1,0:T(8,128)(2,1)S(1)}, u32[]{:S(2)}) copy-start(bf16[128,72,128]{2,1,0:T(8,128)(2,1)S(1)} %all-to-all-done.4.own_ref.left_ref.right_ref) | copy-start | bytes 7077892
  124.0 9.8 %collective-permute-start = (bf16[128,8,128]{2,1,0:T(8,128)(2,1)}, bf16[128,8,128]{2,1,0:T(8,128)(2,1)}, u32[]{:S(2)}, u32[]{:S(2)}) collective-permute-start(bf16[128,8,128]{2,1,0:T(8,128)(2,1)} %slice.33), channel_id=1, source_target_pairs={{0,1},{1,0},{2,3},{3,2},{4,5},{5,4},{6,7},{7,6},{8,9},{9,8},{10,11... | collective-permute-start | bytes 786440 | tf_op jit(solution)/shard_map/ppermute | solution.py:672
  126.8 7.0 %copy-start.5 = (f32[2048,128]{1,0:T(8,128)S(1)}, f32[2048,128]{1,0:T(8,128)}, u32[]{:S(2)}) copy-start(f32[2048,128]{1,0:T(8,128)} %get-tuple-element.683) | copy-start | bytes 3145732
  126.9 6.9 %copy-start.6 = (f32[2048,128]{1,0:T(8,128)S(1)}, f32[2048,128]{1,0:T(8,128)}, u32[]{:S(2)}) copy-start(f32[2048,128]{1,0:T(8,128)} %get-tuple-element.684) | copy-start | bytes 3145732

commit v8 on v7

--- a/solution.py
+++ b/solution.py
@@ -243,8 +243,8 @@
     lax.fori_loop(0, turns, add, 0)
 
 
-PAIRS = 16
-STEPS = 4
+PAIRS = 32
+STEPS = 2
 
 
 def half_spec(second):

time: 138 us -> 137 us (level)
  transfers between devices with their start and end apart: 5 -> 5, of which waited for: 3 -> 3; matrix products, arithmetic and copies ran while one was open for 1% -> 1% of each run, Pallas kernels for 9% -> 8%
where the time goes in v8:
time: 137 us; the launch traced here: 136 us
  waiting for transfers between devices  67.3 us (49%)
  Pallas kernels  45.1 us (33%)
  starting transfers between devices  18.8 us (14%)
  local copies, waits for them, and re-layouts  2.74 us (2%)
  loops' own time  1.68 us (1%)
    all_to_all x2, waiting for transfers between devices, exchange(): return lax.all_to_all(value, ALL, 0, 0, tiled=True)  66.5 us
    all_to_all x2, starting transfers between devices, exchange(): return lax.all_to_all(value, ALL, 0, 0, tiled=True)  16.1 us
    pallas_call x1, Pallas kernels, pack(): pl.pallas_call(pack_kernel, in_specs=[pl.BlockSpec(memory_space=pltpu.SME...  8.27 us
    pallas_call x1, Pallas kernels, route(): pl.pallas_call(route_kernel, in_specs=[pl.BlockSpec(memory_space=pltpu.SM...  8.15 us
    pallas_call x1, Pallas kernels, update(): pl.pallas_call(update_kernel, grid=(STEPS,), in_specs=[pl.BlockSpec(memor...  7.77 us
    pallas_call x1, Pallas kernels, score(): pl.pallas_call(score_kernel, grid=(STEPS,), in_specs=[whole(keys.shape),...  6.35 us
    pallas_call x1, Pallas kernels, reply(): pl.pallas_call(reply_kernel, in_specs=[pl.BlockSpec(memory_space=pltpu.VM...  6.07 us
    pallas_call x1, Pallas kernels, place_rows(): pl.pallas_call(place_kernel, in_specs=[pl.BlockSpec(memory_space=pltpu.VM...  4.83 us
  transfers between devices with their start and end apart: 5, of which 3 were waited for; matrix products, arithmetic and copies ran while one was open for 1% of the time, Pallas kernels for 8%

profile of v8, /device:TPU:1, one launch (start us, length us, event | category | flops | bytes accessed | tf_op | source)
XLA Modules:
  0.0 136.5 jit_solution(5426603859053183683)
XLA Ops:
  0.6 0.1 pad_add_fusion.place_ref
  0.7 8.1 %route.9 = (s32[32,128]{1,0:T(8,128)}, f32[128,128]{1,0:T(8,128)}, f32[128,8,128]{2,1,0:T(8,128)}) custom-call(s32[1]{0:T(128)} %constant.56.clone.1.round_ref, s32[32,128]{1,0:T(8,128)} %bitcast.41, s32[4,128]{1,0:T(4,128)} %bitcast.48, s32[1024,128]{1,0:T(8,128)} %bitcast.34, f32[16,128]{1,0:T(8,128)} %bitcast.43, s32[16,128]{1,0:T(8,128)} %bitcast.45), custom_call_target="tpu_custom_call" | custom-call | tf_op jit(solution)/shard_map/route/pallas_call | solution.py:119
  8.9 8.3 %pack.5 = bf16[128,96,128]{2,1,0:T(8,128)(2,1)} custom-call(s32[4096]{0:T(1024)} %bitcast.50, s32[2]{0:T(128)S(1)} %pad_add_fusion.place_ref, bf16[4096,128]{1,0:T(8,128)(2,1)} %bitcast.36, f32[2048,128]{1,0:T(8,128)} %table_ref.1, f32[2048,128]{1,0:T(8,128)} %moment_ref.1, f32[128,8,128]{2,1,0:T(8,128)} %get-tuple-element.339.head_ref), custom_call_target="tpu_custom_call" | custom-call | tf_op jit(solution)/shard_map/pack/pallas_call | solution.py:199
  17.1 11.5 %all-to-all-start.3 = ((bf16[128,96,128]{2,1,0:T(8,128)(2,1)}), bf16[128,96,128]{2,1,0:T(8,128)(2,1)S(1)}, u32[]{:S(2)}, u32[]{:S(2)}) async-start(bf16[128,96,128]{2,1,0:T(8,128)(2,1)} %pack.5), calls=%async_computation.3 | async-start | bytes 6291456 | tf_op jit(solution)/shard_map/all_to_all | solution.py:568
  28.6 0.0 copy-start.9
  28.7 0.0 copy-start.10
  28.7 0.0 copy-start.11
  28.7 0.0 copy-start.12
  28.7 41.6 %all-to-all-done.3.state_ref.left_ref.right_ref = bf16[128,96,128]{2,1,0:T(8,128)(2,1)S(1)} async-done(((bf16[128,96,128]{2,1,0:T(8,128)(2,1)}), bf16[128,96,128]{2,1,0:T(8,128)(2,1)S(1)}, u32[]{:S(2)}, u32[]{:S(2)}) %all-to-all-start.3) | async-done | bytes 3145760 | tf_op jit(solution)/shard_map/all_to_all | solution.py:568
  70.3 7.8 %update.1 = (bf16[1024,128]{1,0:T(8,128)(2,1)}, f32[128,8,128]{2,1,0:T(8,128)}, s32[8,128]{1,0:T(8,128)}, f32[1024,256]{1,0:T(8,128)}, f32[128,128]{1,0:T(8,128)}, /*index=5*/s32[1]{0:T(128)}) custom-call(s32[1]{0:T(128)} %bitcast.5.core_ref, bf16[128,96,128]{2,1,0:T(8,128)(2,1)S(1)} %all-to-all-done.3.state_ref.left_ref.right_ref, ...), custom_call_target="tpu_custom_call" | custom-call | tf_op jit(solution)/shard_map/update/pallas_call | solution.py:345
  78.1 0.0 copy-done.9
  78.1 0.0 copy-done.10
  78.1 0.0 copy-done.11
  78.1 0.0 copy-done.12
  78.1 0.8 while.30
  79.0 6.1 %reply.5 = bf16[128,72,128]{2,1,0:T(8,128)(2,1)} custom-call(f32[128,128]{1,0:T(8,128)} %get-tuple-element.340.line_ref, bf16[1024,128]{1,0:T(8,128)(2,1)} %get-tuple-element.650.new_ref.own_ref, f32[128,8,128]{2,1,0:T(8,128)} %get-tuple-element.651.sums_ref), custom_call_target="tpu_custom_call" | custom-call | tf_op jit(solution)/shard_map/reply/pallas_call | solution.py:437
  85.0 0.0 copy-start.13
  85.0 0.0 copy-start.15
  85.0 0.0 copy-start.4
  85.0 0.0 copy-start.8
  85.0 4.6 %all-to-all-start.4 = ((bf16[128,72,128]{2,1,0:T(8,128)(2,1)}), bf16[128,72,128]{2,1,0:T(8,128)(2,1)S(1)}, u32[]{:S(2)}, u32[]{:S(2)}) async-start(bf16[128,72,128]{2,1,0:T(8,128)(2,1)} %reply.5), calls=%async_computation.4 | async-start | bytes 4718592 | tf_op jit(solution)/shard_map/all_to_all | solution.py:568
  89.7 1.3 collective-permute-start.1
  90.9 0.0 copy-done.13
  91.0 0.1 collective-permute-start.2
  91.1 0.0 copy-done.15
  91.1 0.6 reshape.63.score_ref
  91.6 0.8 collective-permute-done.2.other_at_ref
  92.5 0.0 copy-start.14
  92.5 0.0 collective-permute-done.1.other_ref
  92.5 0.6 copy-done.14
  93.0 4.8 %place.1 = bf16[2048,128]{1,0:T(8,128)(2,1)} custom-call(bf16[2048,128]{1,0:T(8,128)(2,1)} %old_ref.1, bf16[1024,128]{1,0:T(8,128)(2,1)} %get-tuple-element.650.new_ref.own_ref, bf16[1024,128]{1,0:T(8,128)(2,1)} %collective-permute-done.1.other_ref, s32[8,128]{1,0:T(8,128)S(1)} %copy-done.13, s32[8,128]{1,0:T(8,128)} %copy-done.14), custom_call_target="tpu_custom_call" | custom-call | tf_op jit(solution)/shard_map/place/pallas_call | solution.py:593
  97.9 24.8 %all-to-all-done.4.own_ref.left_ref.right_ref = bf16[128,72,128]{2,1,0:T(8,128)(2,1)S(1)} async-done(((bf16[128,72,128]{2,1,0:T(8,128)(2,1)}), bf16[128,72,128]{2,1,0:T(8,128)(2,1)S(1)}, u32[]{:S(2)}, u32[]{:S(2)}) %all-to-all-start.4) | async-done | bytes 2359328 | tf_op jit(solution)/shard_map/all_to_all | solution.py:568
  122.7 0.0 copy-start.7
  122.7 0.8 slice.33
  123.5 1.3 collective-permute-start
  124.8 0.7 broadcast_in_dim.3
  125.5 0.0 copy-done.4
  125.5 0.0 copy-done.8
  125.5 0.0 copy-done.7
  125.5 0.9 while.31
  126.4 0.0 copy-start.5
  126.4 0.0 copy-start.6
  126.4 6.3 %score.1 = f32[1,128]{1,0:T(1,128)} custom-call(f32[128,128]{1,0:T(8,128)} %get-tuple-element.352.keys_ref, bf16[128,72,128]{2,1,0:T(8,128)(2,1)} %copy-done.7, bf16[128,72,128]{2,1,0:T(8,128)(2,1)} %copy-done.7, f32[512,128]{1,0:T(8,128)} %get-tuple-element.353.start_ref, bf16[512,1024]{1,0:T(8,128)(2,1)} %first_ref.1, bf16[1024,1024]{1,0:T(8,128)(2,1)} %second_ref.1, ...), custom_call_target="tpu_custom_call" | custom-call | tf_op jit(solution)/shard_map/score/pallas_call | solution.py:488
  132.8 0.0 collective-permute-done.other_ref
  132.8 0.0 copy-done.5
  132.8 0.0 copy-done.6
  132.8 3.7 %finish.1 = (f32[2048,128]{1,0:T(8,128)}, f32[2048,128]{1,0:T(8,128)}, f32[16,128]{1,0:T(8,128)}) custom-call(s32[2]{0:T(128)S(1)} %get-tuple-element.696, bf16[128,72,128]{2,1,0:T(8,128)(2,1)} %copy-done.7, bf16[128,8,128]{2,1,0:T(8,128)(2,1)} %collective-permute-done.other_ref, f32[2048,128]{1,0:T(8,128)S(1)} %copy-done.5, f32[2048,128]{1,0:T(8,128)S(1)} %copy-done.6, ...), custom_call_target="tpu_custom_call" | custom-call | tf_op jit(solution)/shard_map/finish/pallas_call | solution.py:549
Async XLA Ops:
  17.1 53.2 %all-to-all-start.3 = ((bf16[128,96,128]{2,1,0:T(8,128)(2,1)}), bf16[128,96,128]{2,1,0:T(8,128)(2,1)S(1)}, u32[]{:S(2)}, u32[]{:S(2)}) async-start(bf16[128,96,128]{2,1,0:T(8,128)(2,1)} %pack.5), calls=%async_computation.3 | async-start | bytes 6291456 | tf_op jit(solution)/shard_map/all_to_all | solution.py:568
  28.6 49.4 %copy-start.9 = (s32[128,32]{0,1:T(8,128)S(1)}, s32[128,32]{0,1:T(8,128)}, u32[]{:S(2)}) copy-start(s32[128,32]{0,1:T(8,128)} %param.16) | copy-start | bytes 49156
  28.7 49.4 %copy-start.10 = (f32[2048]{0:T(1024)S(1)}, f32[2048]{0:T(1024)}, u32[]{:S(2)}) copy-start(f32[2048]{0:T(1024)} %param.23) | copy-start | bytes 24580
  28.7 49.4 %copy-start.11 = (s32[2048]{0:T(1024)S(1)}, s32[2048]{0:T(1024)}, u32[]{:S(2)}) copy-start(s32[2048]{0:T(1024)} %param.19) | copy-start | bytes 24580
  28.7 49.4 %copy-start.12 = (s32[128,4]{0,1:T(4,128)S(1)}, s32[128,4]{0,1:T(4,128)}, u32[]{:S(2)}) copy-start(s32[128,4]{0,1:T(4,128)} %param.17) | copy-start | bytes 6148
  85.0 5.9 %copy-start.13 = (s32[8,128]{1,0:T(8,128)S(1)}, s32[8,128]{1,0:T(8,128)}, u32[]{:S(2)}) copy-start(s32[8,128]{1,0:T(8,128)} %get-tuple-element.351.own_at_ref) | copy-start | bytes 12292
  85.0 6.0 %copy-start.15 = (bf16[1024]{0:T(1024)(128)(2,1)S(1)}, bf16[1024]{0:T(1024)(128)(2,1)}, u32[]{:S(2)}) copy-start(bf16[1024]{0:T(1024)(128)(2,1)} %param.27) | copy-start | bytes 6148
  85.0 40.5 %copy-start.4 = (s32[1024,128]{1,0:T(8,128)S(1)}, s32[1024,128]{1,0:T(8,128)}, u32[]{:S(2)}) copy-start(s32[1024,128]{1,0:T(8,128)} %get-tuple-element.682) | copy-start | bytes 1572868
  85.0 40.5 %copy-start.8 = (f32[128,8,128]{2,1,0:T(8,128)S(1)}, f32[128,8,128]{2,1,0:T(8,128)}, u32[]{:S(2)}) copy-start(f32[128,8,128]{2,1,0:T(8,128)} %get-tuple-element.651.sums_ref) | copy-start | bytes 1572868
  85.0 37.7 %all-to-all-start.4 = ((bf16[128,72,128]{2,1,0:T(8,128)(2,1)}), bf16[128,72,128]{2,1,0:T(8,128)(2,1)S(1)}, u32[]{:S(2)}, u32[]{:S(2)}) async-start(bf16[128,72,128]{2,1,0:T(8,128)(2,1)} %reply.5), calls=%async_computation.4 | async-start | bytes 4718592 | tf_op jit(solution)/shard_map/all_to_all | solution.py:568
  89.7 2.8 %collective-permute-start.1 = (bf16[1024,128]{1,0:T(8,128)(2,1)}, bf16[1024,128]{1,0:T(8,128)(2,1)}, u32[]{:S(2)}, u32[]{:S(2)}) collective-permute-start(bf16[1024,128]{1,0:T(8,128)(2,1)} %get-tuple-element.650.new_ref.own_ref), channel_id=1, source_target_pairs={{0,1},{1,0},{2,3},{3,2},{4,5},{5,4},{6,7},{7,6},{8,9},{9,8},{10,11... | collective-permute-start | bytes 786440 | tf_op jit(solution)/shard_map/ppermute | solution.py:655
  91.0 1.5 %collective-permute-start.2 = (s32[8,128]{1,0:T(8,128)S(1)}, s32[8,128]{1,0:T(8,128)S(1)}, u32[]{:S(2)}, u32[]{:S(2)}) collective-permute-start(s32[8,128]{1,0:T(8,128)S(1)} %copy-done.13), channel_id=1, source_target_pairs={{0,1},{1,0},{2,3},{3,2},{4,5},{5,4},{6,7},{7,6},{8,9},{9,8},{10,11... | collective-permute-start | bytes 12296 | tf_op jit(solution)/shard_map/ppermute | solution.py:656
  92.5 0.6 copy-start.14
  122.7 2.8 %copy-start.7 = (bf16[128,72,128]{2,1,0:T(8,128)(2,1)}, bf16[128,72,128]{2,1,0:T(8,128)(2,1)S(1)}, u32[]{:S(2)}) copy-start(bf16[128,72,128]{2,1,0:T(8,128)(2,1)S(1)} %all-to-all-done.4.own_ref.left_ref.right_ref) | copy-start | bytes 7077892
  123.5 9.3 %collective-permute-start = (bf16[128,8,128]{2,1,0:T(8,128)(2,1)}, bf16[128,8,128]{2,1,0:T(8,128)(2,1)}, u32[]{:S(2)}, u32[]{:S(2)}) collective-permute-start(bf16[128,8,128]{2,1,0:T(8,128)(2,1)} %slice.33), channel_id=1, source_target_pairs={{0,1},{1,0},{2,3},{3,2},{4,5},{5,4},{6,7},{7,6},{8,9},{9,8},{10,11... | collective-permute-start | bytes 786440 | tf_op jit(solution)/shard_map/ppermute | solution.py:672
  126.4 6.4 %copy-start.5 = (f32[2048,128]{1,0:T(8,128)S(1)}, f32[2048,128]{1,0:T(8,128)}, u32[]{:S(2)}) copy-start(f32[2048,128]{1,0:T(8,128)} %get-tuple-element.683) | copy-start | bytes 3145732
  126.4 6.4 %copy-start.6 = (f32[2048,128]{1,0:T(8,128)S(1)}, f32[2048,128]{1,0:T(8,128)}, u32[]{:S(2)}) copy-start(f32[2048,128]{1,0:T(8,128)} %get-tuple-element.684) | copy-start | bytes 3145732
